TPU v7x, 256 devices: a whole 4x4x8 slice. The times are simulated.
256 devices in a mesh: seq: 32 (over x_lo, z, core), head: 8 (over y, x_hi).
Axes of the slice: x: 4 (x_hi: 2, x_lo: 2; x = x_hi * 2 + x_lo), y: 4, z: 8, core: 2. Of those that a mesh axis runs over, the one named last changes fastest.
Arguments:
- query: bfloat16 [36864, 3072], P(('seq', 'head')), may hold values from -6 to 6
- keys: bfloat16 [36864, 3072], P(('seq', 'head')), may hold values from -6 to 6
- values: bfloat16 [36864, 3072], P(('seq', 'head')), may hold values from -6 to 6
- windows: int32 [96, 5], P('seq'), may hold values from -1 to 95, as said below
Outputs:
- attended: bfloat16 [36864, 3072], P(('seq', 'head'))
Inputs may be any that keep to these rules, and one draw needn't show every extreme that they name: `windows`: row t starts with t, then lists distinct tiles, then -1 in every remaining slot. Each listed tile other than t has a tile row within 1 of t's and lies either in t's tile-frame in t's tile column or the one beside it (tile column index within 1), or in t's tile column of the tile-frame before or after; so with s = t // 3 it lies in tile column s, s - 1, s + 1, s - 8 or s + 8.
All inputs are finite; a program needn't handle non-finite values.
Results may differ from a plain program's by a relative error of at most 0.0048.
Values may be sent and summed in bfloat16 or wider, within the bound.
No kernel may reach another device: no remote copies, remote signals or barrier semaphores. Data moves between devices by JAX's collectives and lax.ppermute only.
A program may use at most 128 MiB of HBM per device.

v0:
```python
import jax
import jax.numpy as jnp
from jax import lax
from jax.sharding import PartitionSpec as P

HD = 128
TFR = 4


def from_behind(value, axis, by):
    peers = lax.axis_size(axis)
    pairs = [(i, i + by) for i in range(peers) if 0 <= i + by < peers]
    return lax.ppermute(value, axis, pairs)


def body(query, keys, values, windows):
    q_here, k_here, v_here = (
        lax.all_to_all(query, "head", split_axis=1, concat_axis=0, tiled=True),
        lax.all_to_all(keys, "head", split_axis=1, concat_axis=0, tiled=True),
        lax.all_to_all(values, "head", split_axis=1, concat_axis=0, tiled=True),
    )
    paired = jnp.concatenate([k_here, v_here], axis=1)
    columns = lax.axis_size("seq") // TFR
    neighbours = []
    for reach in (columns, 1, -1, -columns):
        neighbours.append(from_behind(paired, "seq", reach))
    slab = q_here.shape[0]
    local = q_here.shape[1]
    heads = local // HD
    per_slab = windows.shape[0]
    tile = slab // per_slab
    widened = jnp.concatenate(
        [neighbours[0], neighbours[1], paired, neighbours[2], neighbours[3]], axis=0
    )
    widened = widened.reshape(-1, tile, 2, heads, HD)
    own_column = lax.axis_index("seq")
    live = windows >= 0
    delta = windows // per_slab - own_column
    code = jnp.where(
        delta == -columns,
        0,
        jnp.where(delta == -1, 1, jnp.where(delta == 0, 2, jnp.where(delta == 1, 3, 4))),
    )
    slots = jnp.where(live, code * per_slab + windows % per_slab, 0)
    queries = q_here.reshape(per_slab, tile, heads, HD)
    scale = 1.0 / HD**0.5

    def one_tile(item):
        q_tile, row, row_live = item
        picked = jnp.take(widened, row, axis=0).reshape(-1, 2, heads, HD)
        scores = (
            jnp.einsum("qhd,khd->hqk", q_tile, picked[:, 0], preferred_element_type=jnp.float32)
            * scale
        )
        key_live = jnp.repeat(row_live, tile)
        scores = jnp.where(key_live[None, None, :], scores, -jnp.inf)
        top = jnp.max(scores, axis=-1, keepdims=True)
        expo = jnp.exp(scores - top)
        total = jnp.sum(expo, axis=-1)
        weights = expo.astype(jnp.bfloat16)
        mixed = jnp.einsum(
            "hqk,khd->qhd", weights, picked[:, 1], preferred_element_type=jnp.float32
        )
        return (mixed / jnp.transpose(total)[:, :, None]).astype(jnp.bfloat16)

    result = lax.map(one_tile, (queries, slots, live))
    result = result.reshape(slab, local)
    return lax.all_to_all(result, "head", split_axis=0, concat_axis=1, tiled=True)


def solution(mesh):
    return jax.shard_map(
        body,
        mesh=mesh,
        in_specs=(
            P(("seq", "head"), None),
            P(("seq", "head"), None),
            P(("seq", "head"), None),
            P("seq", None),
        ),
        out_specs=P(("seq", "head"), None),
        check_vma=False,
    )
```

profile of v0, /device:TPU:32, one launch (start us, length us, event | category | flops | bytes accessed | tf_op | source)
XLA Modules:
  0.0 338.2 jit_solution(18034697757634407766)
XLA Ops:
  2.2 6.9 %all-to-all-start = ((bf16[144,8,384]{2,0,1:T(8,128)(2,1)}), bf16[144,8,384]{2,0,1:T(8,128)(2,1)S(1)}, u32[]{:S(2)}, u32[]{:S(2)}) async-start(bf16[144,8,384]{2,0,1:T(8,128)(2,1)} %bitcast.69), calls=%async_computation | async-start | bytes 1769472 | tf_op jit(solution)/shard_map/all_to_all | solution.py:19
  9.3 15.3 %all-to-all-done = bf16[144,8,384]{2,0,1:T(8,128)(2,1)S(1)} async-done(((bf16[144,8,384]{2,0,1:T(8,128)(2,1)}), bf16[144,8,384]{2,0,1:T(8,128)(2,1)S(1)}, u32[]{:S(2)}, u32[]{:S(2)}) %all-to-all-start) | async-done | bytes 884768 | tf_op jit(solution)/shard_map/all_to_all | solution.py:19
  24.6 18.1 %all_to_all.73 = bf16[144,8,384]{2,0,1:T(8,128)(2,1)S(1)} all-to-all(bf16[144,8,384]{2,0,1:T(8,128)(2,1)S(1)} %bitcast.96), channel_id=1, replica_groups=mesh['seq'=32,'head'=8] {'head'}, dimensions={1} | all-to-all | bytes 1769472 | tf_op jit(solution)/shard_map/all_to_all | solution.py:20
  44.1 9.5 %collective-permute-start = (bf16[1152,768]{1,0:T(8,128)(2,1)}, bf16[1152,768]{1,0:T(8,128)(2,1)}, u32[]{:S(2)}, u32[]{:S(2)}) collective-permute-start(bf16[1152,768]{1,0:T(8,128)(2,1)} %pad_maximum_fusion), channel_id=1, source_target_pairs={{0,64},{8,72},{16,80},{24,88},{32,96},{40,104},{48,112},{56,120},{... | collective-permute-start | bytes 5308424 | tf_op jit(solution)/shard_map/ppermute | solution.py:13
  55.6 3.6 %collective-permute-start.2 = (bf16[1152,768]{1,0:T(8,128)(2,1)}, bf16[1152,768]{1,0:T(8,128)(2,1)}, u32[]{:S(2)}, u32[]{:S(2)}) collective-permute-start(bf16[1152,768]{1,0:T(8,128)(2,1)} %pad_maximum_fusion), channel_id=1, source_target_pairs={{8,0},{16,8},{24,16},{32,24},{40,32},{48,40},{56,48},{64,56},{72,6... | collective-permute-start | bytes 5308424 | tf_op jit(solution)/shard_map/ppermute | solution.py:13
  60.3 3.5 %all-to-all-start.2 = ((bf16[144,8,384]{2,0,1:T(8,128)(2,1)}), bf16[144,8,384]{2,0,1:T(8,128)(2,1)S(1)}, u32[]{:S(2)}, u32[]{:S(2)}) async-start(bf16[144,8,384]{2,0,1:T(8,128)(2,1)} %bitcast.67), calls=%async_computation.2 | async-start | bytes 1769472 | tf_op jit(solution)/shard_map/all_to_all | solution.py:18
  65.2 24.9 %all-to-all-done.2 = bf16[144,8,384]{2,0,1:T(8,128)(2,1)S(1)} async-done(((bf16[144,8,384]{2,0,1:T(8,128)(2,1)}), bf16[144,8,384]{2,0,1:T(8,128)(2,1)S(1)}, u32[]{:S(2)}, u32[]{:S(2)}) %all-to-all-start.2) | async-done | bytes 884768 | tf_op jit(solution)/shard_map/all_to_all | solution.py:18
  94.7 32.7 %collective-permute-done = bf16[1152,768]{1,0:T(8,128)(2,1)} collective-permute-done((bf16[1152,768]{1,0:T(8,128)(2,1)}, bf16[1152,768]{1,0:T(8,128)(2,1)}, u32[]{:S(2)}, u32[]{:S(2)}) %collective-permute-start) | collective-permute-done | bytes 1769504 | tf_op jit(solution)/shard_map/ppermute | solution.py:13
  127.4 2.9 constant_dynamic-update-slice_fusion.4
  130.3 24.1 %collective-permute-done.1 = bf16[1152,768]{1,0:T(8,128)(2,1)} collective-permute-done((bf16[1152,768]{1,0:T(8,128)(2,1)}, bf16[1152,768]{1,0:T(8,128)(2,1)}, u32[]{:S(2)}, u32[]{:S(2)}) %collective-permute-start.1) | collective-permute-done | bytes 1769504 | tf_op jit(solution)/shard_map/ppermute | solution.py:13
  158.5 2.8 constant_dynamic-update-slice_fusion.1
  161.4 62.0 %collective-permute-done.3 = bf16[1152,768]{1,0:T(8,128)(2,1)} collective-permute-done((bf16[1152,768]{1,0:T(8,128)(2,1)}, bf16[1152,768]{1,0:T(8,128)(2,1)}, u32[]{:S(2)}, u32[]{:S(2)}) %collective-permute-start.3) | collective-permute-done | bytes 1769504 | tf_op jit(solution)/shard_map/ppermute | solution.py:13
  226.1 20.0 %reshape.72 = bf16[15,384,2,3,128]{4,3,2,1,0:T(4,128)(2,1)} reshape(bf16[5760,768]{1,0:T(8,128)(2,1)} %constant_dynamic-update-slice_fusion) | data formatting | bytes 17694720 | tf_op jit(solution)/shard_map/reshape | solution.py:35
  246.1 72.7 %while.10 = (s32[]{:T(128)}, bf16[3,384,3,128]{1,3,2,0:T(8,128)(2,1)}, s32[3,5]{1,0:T(4,128)S(1)}, bf16[15,384,2,3,128]{4,3,2,1,0:T(4,128)(2,1)}, pred[3,5]{1,0:...) while((s32[]{:T(128)}, bf16[3,384,3,128]{1,3,2,0:T(8,128)(2,1)}, s32[3,5]{1,0:T(4,128)S(1)}, ...), condition=%wide.region_3.4_spmd, body=%wide.region_0.3_spmd.sunk | while | flops 1158560512 | bytes 59623024 | solution.py:66
  246.2 11.0 %gather_fusion = bf16[5,384,2,3,128]{4,3,2,1,0:T(4,128)(2,1)} fusion(bf16[15,384,2,3,128]{4,3,2,1,0:T(4,128)(2,1)} %get-tuple-element.134, s32[1024]{0:T(1024)S(1)} %pad_clamp_fusion.2), kind=kCustom, calls=%fused_computation.clone.1 | custom fusion | bytes 5898260 | tf_op jit(solution)/shard_map/while/body/eval_jaxpr/jit(_take)/gather | solution.py:50
  262.4 3.0 fusion.39
  267.2 3.2 fusion.41
  270.4 11.0 %gather_fusion = bf16[5,384,2,3,128]{4,3,2,1,0:T(4,128)(2,1)} fusion(bf16[15,384,2,3,128]{4,3,2,1,0:T(4,128)(2,1)} %get-tuple-element.134, s32[1024]{0:T(1024)S(1)} %pad_clamp_fusion.2), kind=kCustom, calls=%fused_computation.clone.1 | custom fusion | bytes 5898260 | tf_op jit(solution)/shard_map/while/body/eval_jaxpr/jit(_take)/gather | solution.py:50
  286.6 3.0 fusion.39
  291.5 3.2 fusion.41
  294.7 10.9 %gather_fusion = bf16[5,384,2,3,128]{4,3,2,1,0:T(4,128)(2,1)} fusion(bf16[15,384,2,3,128]{4,3,2,1,0:T(4,128)(2,1)} %get-tuple-element.134, s32[1024]{0:T(1024)S(1)} %pad_clamp_fusion.2), kind=kCustom, calls=%fused_computation.clone.1 | custom fusion | bytes 5898260 | tf_op jit(solution)/shard_map/while/body/eval_jaxpr/jit(_take)/gather | solution.py:50
  310.8 3.0 fusion.39
  315.7 3.2 fusion.41
  322.1 15.1 %all_to_all.74 = bf16[8,144,384]{2,1,0:T(8,128)(2,1)S(1)} all-to-all(bf16[8,144,384]{2,1,0:T(8,128)(2,1)S(1)} %all_to_all.65), channel_id=1, replica_groups=mesh['seq'=32,'head'=8] {'head'}, dimensions={0} | all-to-all | bytes 1769472 | tf_op jit(solution)/shard_map/all_to_all | solution.py:68
  (65 shorter events, 45.1 us)
Async XLA Ops:
  0.0 9.2 %copy-start.2 = (bf16[144,3072]{1,0:T(8,128)(2,1)S(1)}, bf16[144,3072]{1,0:T(8,128)(2,1)}, u32[]{:S(2)}) copy-start(bf16[144,3072]{1,0:T(8,128)(2,1)} %param.8) | copy-start | bytes 2654212
  2.2 22.4 %all-to-all-start = ((bf16[144,8,384]{2,0,1:T(8,128)(2,1)}), bf16[144,8,384]{2,0,1:T(8,128)(2,1)S(1)}, u32[]{:S(2)}, u32[]{:S(2)}) async-start(bf16[144,8,384]{2,0,1:T(8,128)(2,1)} %bitcast.69), calls=%async_computation | async-start | bytes 1769472 | tf_op jit(solution)/shard_map/all_to_all | solution.py:19
  9.2 50.0 %copy-start.3 = (bf16[144,3072]{1,0:T(8,128)(2,1)S(1)}, bf16[144,3072]{1,0:T(8,128)(2,1)}, u32[]{:S(2)}) copy-start(bf16[144,3072]{1,0:T(8,128)(2,1)} %param.6) | copy-start | bytes 2654212
  42.8 22.4 %copy-start.4 = (s32[3,5]{1,0:T(4,128)S(1)}, s32[3,5]{1,0:T(4,128)}, u32[]{:S(2)}) copy-start(s32[3,5]{1,0:T(4,128)} %param.9) | copy-start | bytes 184
  44.1 83.2 %collective-permute-start = (bf16[1152,768]{1,0:T(8,128)(2,1)}, bf16[1152,768]{1,0:T(8,128)(2,1)}, u32[]{:S(2)}, u32[]{:S(2)}) collective-permute-start(bf16[1152,768]{1,0:T(8,128)(2,1)} %pad_maximum_fusion), channel_id=1, source_target_pairs={{0,64},{8,72},{16,80},{24,88},{32,96},{40,104},{48,112},{56,120},{... | collective-permute-start | bytes 5308424 | tf_op jit(solution)/shard_map/ppermute | solution.py:13
  53.6 100.7 %collective-permute-start.1 = (bf16[1152,768]{1,0:T(8,128)(2,1)}, bf16[1152,768]{1,0:T(8,128)(2,1)}, u32[]{:S(2)}, u32[]{:S(2)}) collective-permute-start(bf16[1152,768]{1,0:T(8,128)(2,1)} %pad_maximum_fusion), channel_id=1, source_target_pairs={{0,8},{8,16},{16,24},{24,32},{32,40},{40,48},{48,56},{56,64},{64,7... | collective-permute-start | bytes 5308424 | tf_op jit(solution)/shard_map/ppermute | solution.py:13
  55.6 103.0 %collective-permute-start.2 = (bf16[1152,768]{1,0:T(8,128)(2,1)}, bf16[1152,768]{1,0:T(8,128)(2,1)}, u32[]{:S(2)}, u32[]{:S(2)}) collective-permute-start(bf16[1152,768]{1,0:T(8,128)(2,1)} %pad_maximum_fusion), channel_id=1, source_target_pairs={{8,0},{16,8},{24,16},{32,24},{40,32},{48,40},{56,48},{64,56},{72,6... | collective-permute-start | bytes 5308424 | tf_op jit(solution)/shard_map/ppermute | solution.py:13
  60.3 29.8 %all-to-all-start.2 = ((bf16[144,8,384]{2,0,1:T(8,128)(2,1)}), bf16[144,8,384]{2,0,1:T(8,128)(2,1)S(1)}, u32[]{:S(2)}, u32[]{:S(2)}) async-start(bf16[144,8,384]{2,0,1:T(8,128)(2,1)} %bitcast.67), calls=%async_computation.2 | async-start | bytes 1769472 | tf_op jit(solution)/shard_map/all_to_all | solution.py:18
  63.8 159.5 %collective-permute-start.3 = (bf16[1152,768]{1,0:T(8,128)(2,1)}, bf16[1152,768]{1,0:T(8,128)(2,1)}, u32[]{:S(2)}, u32[]{:S(2)}) collective-permute-start(bf16[1152,768]{1,0:T(8,128)(2,1)} %pad_maximum_fusion), channel_id=1, source_target_pairs={{64,0},{72,8},{80,16},{88,24},{96,32},{104,40},{112,48},{120,56},{... | collective-permute-start | bytes 5308424 | tf_op jit(solution)/shard_map/ppermute | solution.py:13
  90.1 1.0 copy-start.1
  265.4 1.9 copy-start
  289.6 1.9 copy-start
  313.8 1.9 copy-start
where the time goes:
time: 340 us; the launch traced here: 338 us
  waiting for transfers between devices  159 us (47%)
  local copies, waits for them, and re-layouts  85.6 us (25%)
  blocking collectives  33.2 us (10%)
  starting transfers between devices  26.8 us (8%)
  matrix products  18.5 us (5%)
  other arithmetic  14.9 us (4%)
    ppermute x4, waiting for transfers between devices, from_behind(): return lax.ppermute(value, axis, pairs)  119 us
    gather x6, local copies, waits for them, and re-layouts, one_tile(): picked = jnp.take(widened, row, axis=0).reshape(-1, 2, heads, HD)  41.3 us
    all_to_all x1, waiting for transfers between devices, body(): lax.all_to_all(query, 'head', split_axis=1, concat_axis=0, tiled=True)  24.9 us
    reshape x1, local copies, waits for them, and re-layouts, body(): widened = widened.reshape(-1, tile, 2, heads, HD)  20 us
    all_to_all x1, blocking collectives, body(): lax.all_to_all(values, 'head', split_axis=1, concat_axis=0, tiled=True)  18.1 us
    ppermute x4, starting transfers between devices, from_behind(): return lax.ppermute(value, axis, pairs)  16.3 us
    all_to_all x1, waiting for transfers between devices, body(): lax.all_to_all(keys, 'head', split_axis=1, concat_axis=0, tiled=True)  15.3 us
    all_to_all x1, blocking collectives, body(): lax.all_to_all(result, 'head', split_axis=0, concat_axis=1, tiled=True)  15.1 us
  transfers between devices with their start and end apart: 6, of which 5 were waited for; matrix products, arithmetic and copies ran while one was open for 4% of the time, Pallas kernels for 0%

commit v1 on v0

v1 whole, which is shorter than its diff:
```python
import functools

import jax
import jax.numpy as jnp
from jax import lax
from jax.experimental import pallas as pl
from jax.experimental.pallas import tpu as pltpu
from jax.sharding import PartitionSpec as P

HD = 128
TFR = 4
SCALE2 = 1.4426950408889634 / HD**0.5


def attend_kernel(tile, per_slab, idx_ref, live_ref, q_ref, *rest):
    sources, (o_ref, kv, sems) = rest[:5], rest[5:]
    blocks, rows = sources[0].shape[0], sources[0].shape[2]
    copies = []
    for at, source in enumerate(sources):
        for part in range(2):
            copy = pltpu.make_async_copy(
                source.at[:, part], kv.at[part, pl.ds(at * blocks, blocks)], sems.at[at, part]
            )
            copy.start()
            copies.append(copy)
    for copy in copies:
        copy.wait()
    flat = kv.reshape(2, len(sources) * blocks * rows, HD)
    slots = idx_ref.shape[1]

    def one_tile(t, carry):
        start = pl.multiple_of(t * tile, 128)
        q = q_ref[pl.ds(start, tile), :]
        scores, tops, begins, alive = [], [], [], []
        for j in range(slots):
            begin = pl.multiple_of(idx_ref[t, j] * tile, 128)
            k = flat[0, pl.ds(begin, tile), :]
            s = lax.dot_general(q, k, (((1,), (1,)), ((), ())), preferred_element_type=jnp.float32)
            top = jnp.max(s, axis=1, keepdims=True)
            on = live_ref[t, j] > 0
            tops.append(jnp.where(on, top, -jnp.inf))
            scores.append(s)
            begins.append(begin)
            alive.append(on)
        top = functools.reduce(jnp.maximum, tops) * SCALE2
        total = jnp.zeros((tile, 1), jnp.float32)
        mixed = jnp.zeros((tile, HD), jnp.float32)
        for j in range(slots):
            shift = jnp.where(alive[j], top, jnp.inf)
            expo = jnp.exp2(scores[j] * SCALE2 - shift)
            total = total + jnp.sum(expo, axis=1, keepdims=True)
            v = flat[1, pl.ds(begins[j], tile), :]
            mixed = mixed + jnp.dot(expo.astype(jnp.bfloat16), v, preferred_element_type=jnp.float32)
        o_ref[pl.ds(start, tile), :] = (mixed / total).astype(o_ref.dtype)
        return carry

    lax.fori_loop(0, per_slab, one_tile, 0)


def attend(idx, live, q, sources):
    per_slab = idx.shape[0]
    slab = q.shape[0]
    tile = slab // per_slab
    blocks, _, rows, _ = sources[0].shape
    count = len(sources)
    keys = idx.shape[1] * tile
    return pl.pallas_call(
        functools.partial(attend_kernel, tile, per_slab),
        out_shape=jax.ShapeDtypeStruct((slab, HD), q.dtype),
        grid_spec=pltpu.PrefetchScalarGridSpec(
            num_scalar_prefetch=2,
            grid=(1,),
            in_specs=[pl.BlockSpec((slab, HD), lambda i, *_: (0, 0))]
            + [pl.BlockSpec(memory_space=pl.ANY)] * count,
            out_specs=pl.BlockSpec((slab, HD), lambda i, *_: (0, 0)),
            scratch_shapes=[
                pltpu.VMEM((2, count * blocks, rows, HD), q.dtype),
                pltpu.SemaphoreType.DMA((count, 2)),
            ],
        ),
        cost_estimate=pl.CostEstimate(
            flops=4 * slab * keys * HD, bytes_accessed=4 * slab * HD * (count + 1), transcendentals=slab * keys
        ),
        name="attend",
    )(idx, live, q, *sources)


def body(query, keys, values, windows):
    groups = lax.axis_size("head")
    peers = lax.axis_size("seq")
    columns = peers // TFR
    rows = query.shape[0]
    local = query.shape[1] // (groups * HD)
    per_slab = windows.shape[0]

    across = [(s, s ^ columns) for s in range(peers)]
    right = [(s, s + 1) for s in range(peers) if (s + 1) % columns]
    left = [(s, s - 1) for s in range(peers) if s % columns]
    middle = [(s, s + 2 * columns) for s in range(columns)] + [
        (s, s - 2 * columns) for s in range(3 * columns, peers)
    ]

    here = lax.axis_index("seq")
    live = windows >= 0
    delta = windows // per_slab - here
    partner = jnp.where(here // columns % 2 == 0, columns, -columns)
    code = jnp.where(
        delta == 0,
        0,
        jnp.where(delta == -1, 1, jnp.where(delta == 1, 2, jnp.where(delta == partner, 3, 4))),
    )
    idx = jnp.where(live, code * per_slab + windows % per_slab, 0)
    live = live.astype(jnp.int32)

    def by_group(x):
        return jnp.transpose(x.reshape(rows, groups, local, HD), (2, 1, 0, 3))

    q_parts, k_parts, v_parts = by_group(query), by_group(keys), by_group(values)

    def exchange(x):
        return lax.all_to_all(x, "head", split_axis=0, concat_axis=0, tiled=True)

    outs = []
    for i in range(local):
        own = exchange(jnp.stack([k_parts[i], v_parts[i]], axis=1))
        far = lax.ppermute(own, "seq", across)
        before = lax.ppermute(own, "seq", right)
        after = lax.ppermute(own, "seq", left)
        second = lax.ppermute(far, "seq", middle)
        q = exchange(q_parts[i]).reshape(groups * rows, HD)
        o = attend(idx, live, q, [own, before, after, far, second])
        outs.append(exchange(o.reshape(groups, rows, HD)))
    out = jnp.stack(outs, axis=1)
    return jnp.transpose(out, (2, 0, 1, 3)).reshape(rows, groups * local * HD)


def solution(mesh):
    return jax.shard_map(
        body,
        mesh=mesh,
        in_specs=(
            P(("seq", "head"), None),
            P(("seq", "head"), None),
            P(("seq", "head"), None),
            P("seq", None),
        ),
        out_specs=P(("seq", "head"), None),
        check_vma=False,
    )
```

time: 340 us -> 197 us (0.58)
  waiting for transfers between devices: 159 us -> 47.9 us
  local copies, waits for them, and re-layouts: 85.6 us -> 16.9 us
  starting transfers between devices: 26.8 us -> 85.8 us
  Pallas kernels: 0 us -> 25.7 us
  matrix products: 18.5 us -> 0 us
  blocking collectives: 33.2 us -> 16.4 us
  other arithmetic: 14.9 us -> 2.24 us
    ppermute x4 -> x12, waiting for transfers between devices: 119 us -> 18.3 us  [the longest x3 11.7 us: body(): after = lax.ppermute(own, 'seq', left)]
    gather x6 -> x0, local copies, waits for them, and re-layouts: 41.3 us -> none  [one_tile(): picked = jnp.take(widened, row, axis=0).reshape(-1, 2, heads, HD)]
    all_to_all x2 -> x8, starting transfers between devices: 10.5 us -> 44 us  [exchange(): return lax.all_to_all(x, 'head', split_axis=0, concat_axis=0, tiled=True)]
    pallas_call x0 -> x3, Pallas kernels: none -> 25.7 us  [attend(): pl.pallas_call(functools.partial(attend_kernel, tile, per_slab), out_shap...]
    ppermute x4 -> x12, starting transfers between devices: 16.3 us -> 41.8 us  [the longest x3 16.1 us: body(): far = lax.ppermute(own, 'seq', across)]
    dot_general x6 -> x0, matrix products: 18.5 us -> none  [the longest x3 9.48 us: one_tile(): jnp.einsum('hqk,khd->qhd', weights, picked[:, 1], preferred_element_type=...]
    all_to_all x2 -> x1, blocking collectives: 33.2 us -> 16.4 us  [exchange(): return lax.all_to_all(x, 'head', split_axis=0, concat_axis=0, tiled=True)]
    reshape x2 -> x6, local copies, waits for them, and re-layouts: 22.6 us -> 8.17 us  [the longest x5 6.22 us: by_group(): return jnp.transpose(x.reshape(rows, groups, local, HD), (2, 1, 0, 3))]
  transfers between devices with their start and end apart: 6 -> 20, of which waited for: 5 -> 7; matrix products, arithmetic and copies ran while one was open for 4% -> 4% of each run, Pallas kernels for 0% -> 13%
where the time goes in v1:
time: 197 us; the launch traced here: 195 us
  starting transfers between devices  85.8 us (44%)
  waiting for transfers between devices  47.9 us (24%)
  Pallas kernels  25.7 us (13%)
  local copies, waits for them, and re-layouts  16.9 us (9%)
  blocking collectives  16.4 us (8%)
  other arithmetic  2.24 us (1%)
    all_to_all x8, starting transfers between devices, exchange(): return lax.all_to_all(x, 'head', split_axis=0, concat_axis=0, tiled=True)  44 us
    all_to_all x8, waiting for transfers between devices, exchange(): return lax.all_to_all(x, 'head', split_axis=0, concat_axis=0, tiled=True)  29.6 us
    pallas_call x3, Pallas kernels, attend(): pl.pallas_call(functools.partial(attend_kernel, tile, per_slab), out_shap...  25.7 us
    all_to_all x1, blocking collectives, exchange(): return lax.all_to_all(x, 'head', split_axis=0, concat_axis=0, tiled=True)  16.4 us
    ppermute x3, starting transfers between devices, body(): far = lax.ppermute(own, 'seq', across)  16.1 us
    ppermute x3, waiting for transfers between devices, body(): after = lax.ppermute(own, 'seq', left)  11.7 us
    ppermute x3, starting transfers between devices, body(): after = lax.ppermute(own, 'seq', left)  11.1 us
    ppermute x3, starting transfers between devices, body(): second = lax.ppermute(far, 'seq', middle)  7.54 us
  transfers between devices with their start and end apart: 20, of which 7 were waited for; matrix products, arithmetic and copies ran while one was open for 4% of the time, Pallas kernels for 13%

profile of v1, /device:TPU:32, one launch (start us, length us, event | category | flops | bytes accessed | tf_op | source)
XLA Modules:
  0.0 195.2 jit_solution(14279702757873972193)
XLA Ops:
  6.8 6.9 %all-to-all-start.4 = ((bf16[8,2,144,128]{3,2,1,0:T(8,128)(2,1)}), bf16[8,2,144,128]{3,2,1,0:T(8,128)(2,1)}, u32[]{:S(2)}, u32[]{:S(2)}) async-start(bf16[8,2,144,128]{3,2,1,0:T(8,128)(2,1)} %copy.59), calls=%async_computation.4 | async-start | bytes 1179648 | tf_op jit(solution)/shard_map/all_to_all | solution.py:121
  14.6 11.5 %all-to-all-done.4.rest_0_ = bf16[8,2,144,128]{3,2,1,0:T(8,128)(2,1)} async-done(((bf16[8,2,144,128]{3,2,1,0:T(8,128)(2,1)}), bf16[8,2,144,128]{3,2,1,0:T(8,128)(2,1)}, u32[]{:S(2)}, u32[]{:S(2)}) %all-to-all-start.4) | async-done | bytes 589856 | tf_op jit(solution)/shard_map/all_to_all | solution.py:121
  26.1 3.5 %all-to-all-start.7 = ((bf16[8,2,144,128]{3,2,1,0:T(8,128)(2,1)}), bf16[8,2,144,128]{3,2,1,0:T(8,128)(2,1)S(1)}, u32[]{:S(2)}, u32[]{:S(2)}) async-start(bf16[8,2,144,128]{3,2,1,0:T(8,128)(2,1)} %pad_maximum_fusion.2), calls=%async_computation.7 | async-start | bytes 1179648 | tf_op jit(solution)/shard_map/all_to_all | solution.py:121
  29.6 6.4 %collective-permute-start.6 = (bf16[8,2,144,128]{3,2,1,0:T(8,128)(2,1)}, bf16[8,2,144,128]{3,2,1,0:T(8,128)(2,1)}, u32[]{:S(2)}, u32[]{:S(2)}) collective-permute-start(bf16[8,2,144,128]{3,2,1,0:T(8,128)(2,1)} %all-to-all-done.4.rest_0_), channel_id=1, source_target_pairs={{0,64},{8,72},{16,80},{24,88},{32,96},{40,104},{48,112},{56,120},{... | collective-permute-start | bytes 1769480 | tf_op jit(solution)/shard_map/ppermute | solution.py:126
  41.0 5.0 %all-to-all-start.1 = ((bf16[8,2,144,128]{3,2,1,0:T(8,128)(2,1)}), bf16[8,2,144,128]{3,2,1,0:T(8,128)(2,1)S(1)}, u32[]{:S(2)}, u32[]{:S(2)}) async-start(bf16[8,2,144,128]{3,2,1,0:T(8,128)(2,1)} %copy.57), calls=%async_computation.1 | async-start | bytes 1179648 | tf_op jit(solution)/shard_map/all_to_all | solution.py:121
  49.4 4.8 %collective-permute-start.10 = (bf16[8,2,144,128]{3,2,1,0:T(8,128)(2,1)S(1)}, bf16[8,2,144,128]{3,2,1,0:T(8,128)(2,1)}, u32[]{:S(2)}, u32[]{:S(2)}) collective-permute-start(bf16[8,2,144,128]{3,2,1,0:T(8,128)(2,1)S(1)} %all-to-all-done.7.rest_0_), channel_id=1, source_target_pairs={{0,64},{8,72},{16,80},{24,88},{32,96},{40,104},{48,112},{56,120},{... | collective-permute-start | bytes 1769480 | tf_op jit(solution)/shard_map/ppermute | solution.py:126
  54.1 3.4 %collective-permute-start.9 = (bf16[8,2,144,128]{3,2,1,0:T(8,128)(2,1)S(1)}, bf16[8,2,144,128]{3,2,1,0:T(8,128)(2,1)}, u32[]{:S(2)}, u32[]{:S(2)}) collective-permute-start(bf16[8,2,144,128]{3,2,1,0:T(8,128)(2,1)S(1)} %all-to-all-done.7.rest_0_), channel_id=1, source_target_pairs={{8,0},{16,8},{24,16},{32,24},{40,32},{48,40},{56,48},{72,64},{80,7... | collective-permute-start | bytes 1769480 | tf_op jit(solution)/shard_map/ppermute | solution.py:128
  58.9 6.6 %collective-permute-done.6.rest_3_ = bf16[8,2,144,128]{3,2,1,0:T(8,128)(2,1)} collective-permute-done((bf16[8,2,144,128]{3,2,1,0:T(8,128)(2,1)}, bf16[8,2,144,128]{3,2,1,0:T(8,128)(2,1)}, u32[]{:S(2)}, u32[]{:S(2)}) %collective-permute-start.6) | collective-permute-done | bytes 589856 | tf_op jit(solution)/shard_map/ppermute | solution.py:126
  65.5 4.9 %collective-permute-start.2 = (bf16[8,2,144,128]{3,2,1,0:T(8,128)(2,1)S(1)}, bf16[8,2,144,128]{3,2,1,0:T(8,128)(2,1)}, u32[]{:S(2)}, u32[]{:S(2)}) collective-permute-start(bf16[8,2,144,128]{3,2,1,0:T(8,128)(2,1)S(1)} %all-to-all-done.1.rest_0_), channel_id=1, source_target_pairs={{0,64},{8,72},{16,80},{24,88},{32,96},{40,104},{48,112},{56,120},{... | collective-permute-start | bytes 1769480 | tf_op jit(solution)/shard_map/ppermute | solution.py:126
  70.4 11.7 %collective-permute-done.5.rest_2_ = bf16[8,2,144,128]{3,2,1,0:T(8,128)(2,1)} collective-permute-done((bf16[8,2,144,128]{3,2,1,0:T(8,128)(2,1)}, bf16[8,2,144,128]{3,2,1,0:T(8,128)(2,1)}, u32[]{:S(2)}, u32[]{:S(2)}) %collective-permute-start.5) | collective-permute-done | bytes 589856 | tf_op jit(solution)/shard_map/ppermute | solution.py:128
  82.1 3.3 %collective-permute-start.7 = (bf16[8,2,144,128]{3,2,1,0:T(8,128)(2,1)}, bf16[8,2,144,128]{3,2,1,0:T(8,128)(2,1)}, u32[]{:S(2)}, u32[]{:S(2)}) collective-permute-start(bf16[8,2,144,128]{3,2,1,0:T(8,128)(2,1)} %collective-permute-done.6.rest_3_), channel_id=1, source_target_pairs={{0,128},{8,136},{16,144},{24,152},{32,160},{40,168},{48,176},{56,1... | collective-permute-start | bytes 1769480 | tf_op jit(solution)/shard_map/ppermute | solution.py:129
  87.4 7.6 %all-to-all-start = ((bf16[8,144,128]{2,1,0:T(8,128)(2,1)}), bf16[8,144,128]{2,1,0:T(8,128)(2,1)S(1)}, u32[]{:S(2)}, u32[]{:S(2)}) async-start(bf16[8,144,128]{2,1,0:T(8,128)(2,1)} %bitcast.40), calls=%async_computation | async-start | bytes 589824 | tf_op jit(solution)/shard_map/all_to_all | solution.py:121
  95.9 10.9 %all-to-all-done = bf16[8,144,128]{2,1,0:T(8,128)(2,1)S(1)} async-done(((bf16[8,144,128]{2,1,0:T(8,128)(2,1)}), bf16[8,144,128]{2,1,0:T(8,128)(2,1)S(1)}, u32[]{:S(2)}, u32[]{:S(2)}) %all-to-all-start) | async-done | bytes 294944 | tf_op jit(solution)/shard_map/all_to_all | solution.py:121
  106.7 3.4 %all-to-all-start.3 = ((bf16[8,144,128]{2,1,0:T(8,128)(2,1)}), bf16[8,144,128]{2,1,0:T(8,128)(2,1)S(1)}, u32[]{:S(2)}, u32[]{:S(2)}) async-start(bf16[8,144,128]{2,1,0:T(8,128)(2,1)} %bitcast.39), calls=%async_computation.3 | async-start | bytes 589824 | tf_op jit(solution)/shard_map/all_to_all | solution.py:121
  110.2 3.0 %collective-permute-start.8 = (bf16[8,2,144,128]{3,2,1,0:T(8,128)(2,1)S(1)}, bf16[8,2,144,128]{3,2,1,0:T(8,128)(2,1)S(1)}, u32[]{:S(2)}, u32[]{:S(2)}) collective-permute-start(bf16[8,2,144,128]{3,2,1,0:T(8,128)(2,1)S(1)} %all-to-all-done.7.rest_0_), channel_id=1, source_target_pairs={{0,8},{8,16},{16,24},{24,32},{32,40},{40,48},{48,56},{64,72},{72,8... | collective-permute-start | bytes 1769480 | tf_op jit(solution)/shard_map/ppermute | solution.py:127
  116.8 3.7 %all-to-all-done.3 = bf16[8,144,128]{2,1,0:T(8,128)(2,1)S(1)} async-done(((bf16[8,144,128]{2,1,0:T(8,128)(2,1)}), bf16[8,144,128]{2,1,0:T(8,128)(2,1)S(1)}, u32[]{:S(2)}, u32[]{:S(2)}) %all-to-all-start.3) | async-done | bytes 294944 | tf_op jit(solution)/shard_map/all_to_all | solution.py:121
  120.5 3.4 %all-to-all-start.6 = ((bf16[8,144,128]{2,1,0:T(8,128)(2,1)}), bf16[8,144,128]{2,1,0:T(8,128)(2,1)S(1)}, u32[]{:S(2)}, u32[]{:S(2)}) async-start(bf16[8,144,128]{2,1,0:T(8,128)(2,1)} %bitcast.38), calls=%async_computation.6 | async-start | bytes 589824 | tf_op jit(solution)/shard_map/all_to_all | solution.py:121
  123.9 5.9 %collective-permute-start.1 = (bf16[8,2,144,128]{3,2,1,0:T(8,128)(2,1)S(1)}, bf16[8,2,144,128]{3,2,1,0:T(8,128)(2,1)S(1)}, u32[]{:S(2)}, u32[]{:S(2)}) collective-permute-start(bf16[8,2,144,128]{3,2,1,0:T(8,128)(2,1)S(1)} %all-to-all-done.1.rest_0_), channel_id=1, source_target_pairs={{8,0},{16,8},{24,16},{32,24},{40,32},{48,40},{56,48},{72,64},{80,7... | collective-permute-start | bytes 1769480 | tf_op jit(solution)/shard_map/ppermute | solution.py:128
  134.5 8.6 %attend.4 = bf16[1152,128]{1,0:T(8,128)(2,1)} custom-call(s32[3,5]{1,0:T(4,128)} %fusion.1.idx_ref, s32[3,5]{1,0:T(4,128)} %fusion.4.live_ref, bf16[1152,128]{1,0:T(8,128)(2,1)} %bitcast.48, bf16[8,2,144,128]{3,2,1,0:T(8,128)(2,1)} %all-to-all-done.4.rest_0_, bf16[8,2,144,128]{3,2,1,0:T(8,128)(2,1)} %collective-permute-done.4.rest_1_, ...), custom_call_target="tpu_custom_call" | custom-call | flops 1132462080 | bytes 3538944 | tf_op jit(solution)/shard_map/attend/pallas_call | solution.py:67
  143.1 6.9 %all-to-all-start.5 = ((bf16[8,144,128]{2,1,0:T(8,128)(2,1)}), bf16[8,144,128]{2,1,0:T(8,128)(2,1)S(1)}, u32[]{:S(2)}, u32[]{:S(2)}) async-start(bf16[8,144,128]{2,1,0:T(8,128)(2,1)} %bitcast.51), calls=%async_computation.5 | async-start | bytes 589824 | tf_op jit(solution)/shard_map/all_to_all | solution.py:121
  150.8 8.6 %attend.5 = bf16[1152,128]{1,0:T(8,128)(2,1)} custom-call(s32[3,5]{1,0:T(4,128)} %fusion.1.idx_ref, s32[3,5]{1,0:T(4,128)} %fusion.4.live_ref, bf16[1152,128]{1,0:T(8,128)(2,1)} %bitcast.49, bf16[8,2,144,128]{3,2,1,0:T(8,128)(2,1)} %copy-done.3, bf16[8,2,144,128]{3,2,1,0:T(8,128)(2,1)} %copy-done.8, bf16[8,2,144,128]{3,2,1,0:T(8,128)(2,1)} %collective-permute-done.9.rest_2_, ...), custom_call_target="tpu_custom_call" | custom-call | flops 1132462080 | bytes 3538944 | tf_op jit(solution)/shard_map/attend/pallas_call | solution.py:67
  159.4 7.2 %all-to-all-start.8 = ((bf16[8,144,128]{2,1,0:T(8,128)(2,1)}), bf16[8,144,128]{2,1,0:T(8,128)(2,1)S(1)}, u32[]{:S(2)}, u32[]{:S(2)}) async-start(bf16[8,144,128]{2,1,0:T(8,128)(2,1)} %bitcast.50), calls=%async_computation.8 | async-start | bytes 589824 | tf_op jit(solution)/shard_map/all_to_all | solution.py:121
  167.4 8.5 %attend.3 = bf16[1152,128]{1,0:T(8,128)(2,1)} custom-call(s32[3,5]{1,0:T(4,128)} %fusion.1.idx_ref, s32[3,5]{1,0:T(4,128)} %fusion.4.live_ref, bf16[1152,128]{1,0:T(8,128)(2,1)} %bitcast.47, bf16[8,2,144,128]{3,2,1,0:T(8,128)(2,1)} %copy-done.2, bf16[8,2,144,128]{3,2,1,0:T(8,128)(2,1)} %collective-permute-done.rest_1_, bf16[8,2,144,128]{3,2,1,0:T(8,128)(2,1)} %copy-done.9, ...), custom_call_target="tpu_custom_call" | custom-call | flops 1132462080 | bytes 3538944 | tf_op jit(solution)/shard_map/attend/pallas_call | solution.py:67
  176.0 16.4 %all_to_all.45 = bf16[8,144,128]{2,1,0:T(8,128)(2,1)S(1)} all-to-all(bf16[8,144,128]{2,1,0:T(8,128)(2,1)} %bitcast.52), channel_id=1, replica_groups=mesh['seq'=32,'head'=8] {'head'}, dimensions={0} | all-to-all | bytes 589824 | tf_op jit(solution)/shard_map/all_to_all | solution.py:121
  (60 shorter events, 32.8 us)
Async XLA Ops:
  6.8 19.3 %all-to-all-start.4 = ((bf16[8,2,144,128]{3,2,1,0:T(8,128)(2,1)}), bf16[8,2,144,128]{3,2,1,0:T(8,128)(2,1)}, u32[]{:S(2)}, u32[]{:S(2)}) async-start(bf16[8,2,144,128]{3,2,1,0:T(8,128)(2,1)} %copy.59), calls=%async_computation.4 | async-start | bytes 1179648 | tf_op jit(solution)/shard_map/all_to_all | solution.py:121
  26.1 14.9 %all-to-all-start.7 = ((bf16[8,2,144,128]{3,2,1,0:T(8,128)(2,1)}), bf16[8,2,144,128]{3,2,1,0:T(8,128)(2,1)S(1)}, u32[]{:S(2)}, u32[]{:S(2)}) async-start(bf16[8,2,144,128]{3,2,1,0:T(8,128)(2,1)} %pad_maximum_fusion.2), calls=%async_computation.7 | async-start | bytes 1179648 | tf_op jit(solution)/shard_map/all_to_all | solution.py:121
  29.6 35.8 %collective-permute-start.6 = (bf16[8,2,144,128]{3,2,1,0:T(8,128)(2,1)}, bf16[8,2,144,128]{3,2,1,0:T(8,128)(2,1)}, u32[]{:S(2)}, u32[]{:S(2)}) collective-permute-start(bf16[8,2,144,128]{3,2,1,0:T(8,128)(2,1)} %all-to-all-done.4.rest_0_), channel_id=1, source_target_pairs={{0,64},{8,72},{16,80},{24,88},{32,96},{40,104},{48,112},{56,120},{... | collective-permute-start | bytes 1769480 | tf_op jit(solution)/shard_map/ppermute | solution.py:126
  36.0 46.1 %collective-permute-start.5 = (bf16[8,2,144,128]{3,2,1,0:T(8,128)(2,1)}, bf16[8,2,144,128]{3,2,1,0:T(8,128)(2,1)}, u32[]{:S(2)}, u32[]{:S(2)}) collective-permute-start(bf16[8,2,144,128]{3,2,1,0:T(8,128)(2,1)} %all-to-all-done.4.rest_0_), channel_id=1, source_target_pairs={{8,0},{16,8},{24,16},{32,24},{40,32},{48,40},{56,48},{72,64},{80,7... | collective-permute-start | bytes 1769480 | tf_op jit(solution)/shard_map/ppermute | solution.py:128
  41.0 69.2 %copy-start.3 = (bf16[8,2,144,128]{3,2,1,0:T(8,128)(2,1)}, bf16[8,2,144,128]{3,2,1,0:T(8,128)(2,1)S(1)}, u32[]{:S(2)}) copy-start(bf16[8,2,144,128]{3,2,1,0:T(8,128)(2,1)S(1)} %all-to-all-done.7.rest_0_) | copy-start | bytes 1769476
  41.0 17.9 %all-to-all-start.1 = ((bf16[8,2,144,128]{3,2,1,0:T(8,128)(2,1)}), bf16[8,2,144,128]{3,2,1,0:T(8,128)(2,1)S(1)}, u32[]{:S(2)}, u32[]{:S(2)}) async-start(bf16[8,2,144,128]{3,2,1,0:T(8,128)(2,1)} %copy.57), calls=%async_computation.1 | async-start | bytes 1179648 | tf_op jit(solution)/shard_map/all_to_all | solution.py:121
  47.2 62.9 %collective-permute-start.4 = (bf16[8,2,144,128]{3,2,1,0:T(8,128)(2,1)}, bf16[8,2,144,128]{3,2,1,0:T(8,128)(2,1)}, u32[]{:S(2)}, u32[]{:S(2)}) collective-permute-start(bf16[8,2,144,128]{3,2,1,0:T(8,128)(2,1)} %all-to-all-done.4.rest_0_), channel_id=1, source_target_pairs={{0,8},{8,16},{16,24},{24,32},{32,40},{40,48},{48,56},{64,72},{72,8... | collective-permute-start | bytes 1769480 | tf_op jit(solution)/shard_map/ppermute | solution.py:127
  49.4 63.9 %collective-permute-start.10 = (bf16[8,2,144,128]{3,2,1,0:T(8,128)(2,1)S(1)}, bf16[8,2,144,128]{3,2,1,0:T(8,128)(2,1)}, u32[]{:S(2)}, u32[]{:S(2)}) collective-permute-start(bf16[8,2,144,128]{3,2,1,0:T(8,128)(2,1)S(1)} %all-to-all-done.7.rest_0_), channel_id=1, source_target_pairs={{0,64},{8,72},{16,80},{24,88},{32,96},{40,104},{48,112},{56,120},{... | collective-permute-start | bytes 1769480 | tf_op jit(solution)/shard_map/ppermute | solution.py:126
  54.1 69.8 %collective-permute-start.9 = (bf16[8,2,144,128]{3,2,1,0:T(8,128)(2,1)S(1)}, bf16[8,2,144,128]{3,2,1,0:T(8,128)(2,1)}, u32[]{:S(2)}, u32[]{:S(2)}) collective-permute-start(bf16[8,2,144,128]{3,2,1,0:T(8,128)(2,1)S(1)} %all-to-all-done.7.rest_0_), channel_id=1, source_target_pairs={{8,0},{16,8},{24,16},{32,24},{40,32},{48,40},{56,48},{72,64},{80,7... | collective-permute-start | bytes 1769480 | tf_op jit(solution)/shard_map/ppermute | solution.py:128
  58.9 70.9 %copy-start.2 = (bf16[8,2,144,128]{3,2,1,0:T(8,128)(2,1)}, bf16[8,2,144,128]{3,2,1,0:T(8,128)(2,1)S(1)}, u32[]{:S(2)}) copy-start(bf16[8,2,144,128]{3,2,1,0:T(8,128)(2,1)S(1)} %all-to-all-done.1.rest_0_) | copy-start | bytes 1769476
  65.5 64.3 %collective-permute-start.2 = (bf16[8,2,144,128]{3,2,1,0:T(8,128)(2,1)S(1)}, bf16[8,2,144,128]{3,2,1,0:T(8,128)(2,1)}, u32[]{:S(2)}, u32[]{:S(2)}) collective-permute-start(bf16[8,2,144,128]{3,2,1,0:T(8,128)(2,1)S(1)} %all-to-all-done.1.rest_0_), channel_id=1, source_target_pairs={{0,64},{8,72},{16,80},{24,88},{32,96},{40,104},{48,112},{56,120},{... | collective-permute-start | bytes 1769480 | tf_op jit(solution)/shard_map/ppermute | solution.py:126
  82.1 49.7 %collective-permute-start.7 = (bf16[8,2,144,128]{3,2,1,0:T(8,128)(2,1)}, bf16[8,2,144,128]{3,2,1,0:T(8,128)(2,1)}, u32[]{:S(2)}, u32[]{:S(2)}) collective-permute-start(bf16[8,2,144,128]{3,2,1,0:T(8,128)(2,1)} %collective-permute-done.6.rest_3_), channel_id=1, source_target_pairs={{0,128},{8,136},{16,144},{24,152},{32,160},{40,168},{48,176},{56,1... | collective-permute-start | bytes 1769480 | tf_op jit(solution)/shard_map/ppermute | solution.py:129
  87.4 27.9 %copy-start.7 = (s32[3,5]{1,0:T(4,128)S(1)}, s32[3,5]{1,0:T(4,128)}, u32[]{:S(2)}) copy-start(s32[3,5]{1,0:T(4,128)} %param.7) | copy-start | bytes 184
  87.4 19.3 %all-to-all-start = ((bf16[8,144,128]{2,1,0:T(8,128)(2,1)}), bf16[8,144,128]{2,1,0:T(8,128)(2,1)S(1)}, u32[]{:S(2)}, u32[]{:S(2)}) async-start(bf16[8,144,128]{2,1,0:T(8,128)(2,1)} %bitcast.40), calls=%async_computation | async-start | bytes 589824 | tf_op jit(solution)/shard_map/all_to_all | solution.py:121
  106.7 36.3 %copy-start.4 = (bf16[8,144,128]{2,1,0:T(8,128)(2,1)}, bf16[8,144,128]{2,1,0:T(8,128)(2,1)S(1)}, u32[]{:S(2)}) copy-start(bf16[8,144,128]{2,1,0:T(8,128)(2,1)S(1)} %all-to-all-done) | copy-start | bytes 884740
  106.7 13.8 %all-to-all-start.3 = ((bf16[8,144,128]{2,1,0:T(8,128)(2,1)}), bf16[8,144,128]{2,1,0:T(8,128)(2,1)S(1)}, u32[]{:S(2)}, u32[]{:S(2)}) async-start(bf16[8,144,128]{2,1,0:T(8,128)(2,1)} %bitcast.39), calls=%async_computation.3 | async-start | bytes 589824 | tf_op jit(solution)/shard_map/all_to_all | solution.py:121
  110.2 39.8 %collective-permute-start.8 = (bf16[8,2,144,128]{3,2,1,0:T(8,128)(2,1)S(1)}, bf16[8,2,144,128]{3,2,1,0:T(8,128)(2,1)S(1)}, u32[]{:S(2)}, u32[]{:S(2)}) collective-permute-start(bf16[8,2,144,128]{3,2,1,0:T(8,128)(2,1)S(1)} %all-to-all-done.7.rest_0_), channel_id=1, source_target_pairs={{0,8},{8,16},{16,24},{24,32},{32,40},{40,48},{48,56},{64,72},{72,8... | collective-permute-start | bytes 1769480 | tf_op jit(solution)/shard_map/ppermute | solution.py:127
  113.2 36.8 %collective-permute-start.11 = (bf16[8,2,144,128]{3,2,1,0:T(8,128)(2,1)}, bf16[8,2,144,128]{3,2,1,0:T(8,128)(2,1)}, u32[]{:S(2)}, u32[]{:S(2)}) collective-permute-start(bf16[8,2,144,128]{3,2,1,0:T(8,128)(2,1)} %collective-permute-done.10.rest_3_), channel_id=1, source_target_pairs={{0,128},{8,136},{16,144},{24,152},{32,160},{40,168},{48,176},{56,1... | collective-permute-start | bytes 1769480 | tf_op jit(solution)/shard_map/ppermute | solution.py:129
  120.5 22.5 %all-to-all-start.6 = ((bf16[8,144,128]{2,1,0:T(8,128)(2,1)}), bf16[8,144,128]{2,1,0:T(8,128)(2,1)S(1)}, u32[]{:S(2)}, u32[]{:S(2)}) async-start(bf16[8,144,128]{2,1,0:T(8,128)(2,1)} %bitcast.38), calls=%async_computation.6 | async-start | bytes 589824 | tf_op jit(solution)/shard_map/all_to_all | solution.py:121
  123.9 42.7 %collective-permute-start.1 = (bf16[8,2,144,128]{3,2,1,0:T(8,128)(2,1)S(1)}, bf16[8,2,144,128]{3,2,1,0:T(8,128)(2,1)S(1)}, u32[]{:S(2)}, u32[]{:S(2)}) collective-permute-start(bf16[8,2,144,128]{3,2,1,0:T(8,128)(2,1)S(1)} %all-to-all-done.1.rest_0_), channel_id=1, source_target_pairs={{8,0},{16,8},{24,16},{32,24},{40,32},{48,40},{56,48},{72,64},{80,7... | collective-permute-start | bytes 1769480 | tf_op jit(solution)/shard_map/ppermute | solution.py:128
  129.8 36.8 %collective-permute-start = (bf16[8,2,144,128]{3,2,1,0:T(8,128)(2,1)S(1)}, bf16[8,2,144,128]{3,2,1,0:T(8,128)(2,1)}, u32[]{:S(2)}, u32[]{:S(2)}) collective-permute-start(bf16[8,2,144,128]{3,2,1,0:T(8,128)(2,1)S(1)} %all-to-all-done.1.rest_0_), channel_id=1, source_target_pairs={{0,8},{8,16},{16,24},{24,32},{32,40},{40,48},{48,56},{64,72},{72,8... | collective-permute-start | bytes 1769480 | tf_op jit(solution)/shard_map/ppermute | solution.py:127
  131.8 34.9 %collective-permute-start.3 = (bf16[8,2,144,128]{3,2,1,0:T(8,128)(2,1)}, bf16[8,2,144,128]{3,2,1,0:T(8,128)(2,1)}, u32[]{:S(2)}, u32[]{:S(2)}) collective-permute-start(bf16[8,2,144,128]{3,2,1,0:T(8,128)(2,1)} %collective-permute-done.2.rest_3_), channel_id=1, source_target_pairs={{0,128},{8,136},{16,144},{24,152},{32,160},{40,168},{48,176},{56,1... | collective-permute-start | bytes 1769480 | tf_op jit(solution)/shard_map/ppermute | solution.py:129
  143.1 16.3 %all-to-all-start.5 = ((bf16[8,144,128]{2,1,0:T(8,128)(2,1)}), bf16[8,144,128]{2,1,0:T(8,128)(2,1)S(1)}, u32[]{:S(2)}, u32[]{:S(2)}) async-start(bf16[8,144,128]{2,1,0:T(8,128)(2,1)} %bitcast.51), calls=%async_computation.5 | async-start | bytes 589824 | tf_op jit(solution)/shard_map/all_to_all | solution.py:121
  159.4 16.6 %all-to-all-start.8 = ((bf16[8,144,128]{2,1,0:T(8,128)(2,1)}), bf16[8,144,128]{2,1,0:T(8,128)(2,1)S(1)}, u32[]{:S(2)}, u32[]{:S(2)}) async-start(bf16[8,144,128]{2,1,0:T(8,128)(2,1)} %bitcast.50), calls=%async_computation.8 | async-start | bytes 589824 | tf_op jit(solution)/shard_map/all_to_all | solution.py:121
  (6 other events, 31.7 us)

commit v2 on v1

v2 whole, which is shorter than its diff:
```python
import functools

import jax
import jax.numpy as jnp
from jax import lax
from jax.experimental import pallas as pl
from jax.experimental.pallas import tpu as pltpu
from jax.sharding import PartitionSpec as P


HD = 128
TFR = 4
SCALE2 = 1.4426950408889634 / HD**0.5


ANY = pl.BlockSpec(memory_space=pl.ANY)


def after(value, *first):
    return lax.optimization_barrier((value,) + first)[0]


def pack_kernel(picks, local, count, *refs):
    arrays, o_ref, sems = refs[:count], refs[count], refs[count + 1]
    copies = []
    for at, (array, head) in enumerate(picks):
        for g in range(o_ref.shape[0]):
            copy = pltpu.make_async_copy(
                arrays[array].at[:, pl.ds((g * local + head) * HD, HD)], o_ref.at[g, at], sems.at[at, g]
            )
            copy.start()
            copies.append(copy)
    for copy in copies:
        copy.wait()


def pack(arrays, picks, groups):
    rows, width = arrays[0].shape
    shape = (groups, len(picks), rows, HD)
    return pl.pallas_call(
        functools.partial(pack_kernel, picks, width // (groups * HD), len(arrays)),
        out_shape=jax.ShapeDtypeStruct(shape, arrays[0].dtype),
        grid=(1,),
        in_specs=[ANY] * len(arrays),
        out_specs=pl.BlockSpec(shape, lambda i: (0, 0, 0, 0)),
        scratch_shapes=[pltpu.SemaphoreType.DMA((len(picks), groups))],
        cost_estimate=pl.CostEstimate(
            flops=0, bytes_accessed=4 * groups * len(picks) * rows * HD, transcendentals=0
        ),
        name="pack",
    )(*arrays)


def unpack_kernel(local, *refs):
    parts, o_ref, sems = refs[:local], refs[local], refs[local + 1]
    copies = []
    for head, part in enumerate(parts):
        for g in range(part.shape[0]):
            copy = pltpu.make_async_copy(
                part.at[g], o_ref.at[:, pl.ds((g * local + head) * HD, HD)], sems.at[head, g]
            )
            copy.start()
            copies.append(copy)
    for copy in copies:
        copy.wait()


def unpack(parts):
    local = len(parts)
    groups, rows, _ = parts[0].shape
    return pl.pallas_call(
        functools.partial(unpack_kernel, local),
        out_shape=jax.ShapeDtypeStruct((rows, groups * local * HD), parts[0].dtype),
        grid=(1,),
        in_specs=[pl.BlockSpec((groups, rows, HD), lambda i: (0, 0, 0))] * local,
        out_specs=ANY,
        scratch_shapes=[pltpu.SemaphoreType.DMA((local, groups))],
        cost_estimate=pl.CostEstimate(
            flops=0, bytes_accessed=4 * groups * local * rows * HD, transcendentals=0
        ),
        name="unpack",
    )(*parts)


def attend_kernel(tile, per_slab, places, idx_ref, live_ref, *refs):
    count = len(places)
    sources, o_ref, held, q_held, sems = refs[:count], refs[count], refs[count + 1], refs[count + 2], refs[count + 3]
    blocks, rows = sources[0].shape[0], sources[0].shape[2]
    copies = []
    for at, (source, parts) in enumerate(zip(sources, places)):
        for n, part in enumerate(parts):
            into = q_held if at == 0 else held.at[n, pl.ds((at - 1) * blocks, blocks)]
            copy = pltpu.make_async_copy(source.at[:, part], into, sems.at[at, n])
            copy.start()
            copies.append(copy)
    for copy in copies:
        copy.wait()
    flat = held.reshape(2, (count - 1) * blocks * rows, HD)
    q_flat = q_held.reshape(blocks * rows, HD)
    o_flat = o_ref.reshape(blocks * rows, HD)
    slots = idx_ref.shape[1]

    def one_tile(t, carry):
        start = pl.multiple_of(t * tile, 128)
        q = q_flat[pl.ds(start, tile), :]
        scores, tops, begins, alive = [], [], [], []
        for j in range(slots):
            begin = pl.multiple_of(idx_ref[t, j] * tile, 128)
            k = flat[0, pl.ds(begin, tile), :]
            s = lax.dot_general(q, k, (((1,), (1,)), ((), ())), preferred_element_type=jnp.float32)
            top = jnp.max(s, axis=1, keepdims=True)
            on = live_ref[t, j] > 0
            tops.append(jnp.where(on, top, -jnp.inf))
            scores.append(s)
            begins.append(begin)
            alive.append(on)
        top = functools.reduce(jnp.maximum, tops) * SCALE2
        total = jnp.zeros((tile, 1), jnp.float32)
        mixed = jnp.zeros((tile, HD), jnp.float32)
        for j in range(slots):
            shift = jnp.where(alive[j], top, jnp.inf)
            expo = jnp.exp2(scores[j] * SCALE2 - shift)
            total = total + jnp.sum(expo, axis=1, keepdims=True)
            v = flat[1, pl.ds(begins[j], tile), :]
            mixed = mixed + jnp.dot(expo.astype(jnp.bfloat16), v, preferred_element_type=jnp.float32)
        o_flat[pl.ds(start, tile), :] = (mixed / total).astype(o_ref.dtype)
        return carry

    lax.fori_loop(0, per_slab, one_tile, 0)


def attend(idx, live, sources, places):
    per_slab = idx.shape[0]
    blocks, _, rows, _ = sources[0].shape
    slab = blocks * rows
    keys = idx.shape[1] * slab // per_slab
    count = len(sources)
    dtype = sources[0].dtype
    return pl.pallas_call(
        functools.partial(attend_kernel, slab // per_slab, per_slab, places),
        out_shape=jax.ShapeDtypeStruct((blocks, rows, HD), dtype),
        grid_spec=pltpu.PrefetchScalarGridSpec(
            num_scalar_prefetch=2,
            grid=(1,),
            in_specs=[ANY] * count,
            out_specs=pl.BlockSpec((blocks, rows, HD), lambda i, *_: (0, 0, 0)),
            scratch_shapes=[
                pltpu.VMEM((2, (count - 1) * blocks, rows, HD), dtype),
                pltpu.VMEM((blocks, rows, HD), dtype),
                pltpu.SemaphoreType.DMA((count, 2)),
            ],
        ),
        cost_estimate=pl.CostEstimate(
            flops=4 * slab * keys * HD, bytes_accessed=4 * slab * HD * (count + 1), transcendentals=slab * keys
        ),
        name="attend",
    )(idx, live, *sources)


def body(query, keys, values, windows):
    groups = lax.axis_size("head")
    peers = lax.axis_size("seq")
    columns = peers // TFR
    local = query.shape[1] // (groups * HD)
    per_slab = windows.shape[0]

    across = [(s, s ^ columns) for s in range(peers)]
    right = [(s, s + 1) for s in range(peers) if (s + 1) % columns]
    left = [(s, s - 1) for s in range(peers) if s % columns]
    middle = [(s, s + 2 * columns) for s in range(columns)] + [
        (s, s - 2 * columns) for s in range(3 * columns, peers)
    ]

    def send(x, pairs):
        return lax.ppermute(x, "seq", pairs)

    def exchange(x):
        return lax.all_to_all(x, "head", split_axis=0, concat_axis=0, tiled=True)

    here = lax.axis_index("seq")
    live = windows >= 0
    delta = windows // per_slab - here
    partner = jnp.where(here // columns % 2 == 0, columns, -columns)
    code = jnp.where(
        delta == 0,
        0,
        jnp.where(delta == -1, 1, jnp.where(delta == 1, 2, jnp.where(delta == partner, 3, 4))),
    )
    idx = jnp.where(live, code * per_slab + windows % per_slab, 0)
    live = live.astype(jnp.int32)

    first = pack([keys, values], [(0, 0), (1, 0)], groups)
    crossed = send(first, across)
    rest = pack([keys, values], [(n, i) for i in range(local) for n in range(2)], groups)
    own = exchange(rest)
    q_all = pack([query], [(0, i) for i in range(local)], groups)
    own_of = [own[:, 2 * i : 2 * i + 2] for i in range(local)]
    far, second, before, behind, outs = [[None] * local for _ in range(5)]
    far[1] = send(after(own_of[1], crossed), across)
    far[0] = exchange(crossed)
    far[2] = send(after(own_of[2], far[1]), across)
    q_all = exchange(q_all)
    for i in range(local):
        before[i] = send(own_of[i], right)
        behind[i] = send(own_of[i], left)
        second[i] = send(far[i], middle)
        o = attend(
            idx,
            live,
            [q_all, own, before[i], behind[i], far[i], second[i]],
            [(i,), (2 * i, 2 * i + 1)] + [(0, 1)] * 4,
        )
        outs[i] = exchange(o)
    return unpack(outs)


def solution(mesh):
    return jax.shard_map(
        body,
        mesh=mesh,
        in_specs=(
            P(("seq", "head"), None),
            P(("seq", "head"), None),
            P(("seq", "head"), None),
            P("seq", None),
        ),
        out_specs=P(("seq", "head"), None),
        check_vma=False,
    )
```

time: 197 us -> 180 us (0.914)
  the two profiles are of different devices: /device:TPU:32 before, /device:TPU:1 now
where the time goes in v2:
time: 180 us; the launch traced here: 179 us
  starting transfers between devices  97.1 us (54%)
  Pallas kernels  32.8 us (18%)
  waiting for transfers between devices  29.3 us (16%)
  blocking collectives  15.3 us (8%)
  local copies, waits for them, and re-layouts  3.02 us (2%)
    ppermute x12, starting transfers between devices, send(): return lax.ppermute(x, 'seq', pairs)  67.4 us
    all_to_all x5, starting transfers between devices, exchange(): return lax.all_to_all(x, 'head', split_axis=0, concat_axis=0, tiled=True)  29.7 us
    ppermute x12, waiting for transfers between devices, send(): return lax.ppermute(x, 'seq', pairs)  25.8 us
    pallas_call x3, Pallas kernels, attend(): pl.pallas_call(functools.partial(attend_kernel, slab // per_slab, per_sla...  23.2 us
    all_to_all x1, blocking collectives, exchange(): return lax.all_to_all(x, 'head', split_axis=0, concat_axis=0, tiled=True)  15.3 us
    pallas_call x3, Pallas kernels, pack(): pl.pallas_call(functools.partial(pack_kernel, picks, width // (groups * H...  7.42 us
  transfers between devices with their start and end apart: 17, of which 4 were waited for; matrix products, arithmetic and copies ran while one was open for 1% of the time, Pallas kernels for 15%

profile of v2, /device:TPU:1, one launch (start us, length us, event | category | flops | bytes accessed | tf_op | source)
XLA Modules:
  0.0 179.0 jit_solution(2895146602362782845)
XLA Ops:
  0.0 3.1 %pack.4 = bf16[8,6,144,128]{3,2,1,0:T(8,128)(2,1)} custom-call(bf16[144,3072]{1,0:T(8,128)(2,1)} %refs_0_.5, bf16[144,3072]{1,0:T(8,128)(2,1)} %refs_1_.3), custom_call_target="tpu_custom_call" | custom-call | bytes 3538944 | tf_op jit(solution)/shard_map/pack/pallas_call | solution.py:40
  3.1 7.5 %all-to-all-start.1 = ((bf16[8,6,144,128]{3,2,1,0:T(8,128)(2,1)}), bf16[8,6,144,128]{3,2,1,0:T(8,128)(2,1)S(1)}, u32[]{:S(2)}, u32[]{:S(2)}) async-start(bf16[8,6,144,128]{3,2,1,0:T(8,128)(2,1)} %pack.4), calls=%async_computation.1 | async-start | bytes 3538944 | tf_op jit(solution)/shard_map/all_to_all | solution.py:178
  12.6 7.0 %collective-permute-start.2 = (bf16[8,2,144,128]{3,2,1,0:T(8,128)(2,1)}, bf16[8,2,144,128]{3,2,1,0:T(8,128)(2,1)}, u32[]{:S(2)}, u32[]{:S(2)}) collective-permute-start(bf16[8,2,144,128]{3,2,1,0:T(8,128)(2,1)} %pack.5), channel_id=1, source_target_pairs={{0,64},{8,72},{16,80},{24,88},{32,96},{40,104},{48,112},{56,120},{... | collective-permute-start | bytes 1769480 | tf_op jit(solution)/shard_map/ppermute | solution.py:175
  19.6 15.2 %collective-permute-done.2 = bf16[8,2,144,128]{3,2,1,0:T(8,128)(2,1)} collective-permute-done((bf16[8,2,144,128]{3,2,1,0:T(8,128)(2,1)}, bf16[8,2,144,128]{3,2,1,0:T(8,128)(2,1)}, u32[]{:S(2)}, u32[]{:S(2)}) %collective-permute-start.2) | collective-permute-done | bytes 589856 | tf_op jit(solution)/shard_map/ppermute | solution.py:175
  34.8 6.4 %all-to-all-start.2 = ((bf16[8,2,144,128]{3,2,1,0:T(8,128)(2,1)}), bf16[8,2,144,128]{3,2,1,0:T(8,128)(2,1)S(1)}, u32[]{:S(2)}, u32[]{:S(2)}) async-start(bf16[8,2,144,128]{3,2,1,0:T(8,128)(2,1)} %collective-permute-done.2), calls=%async_computation.2 | async-start | bytes 1179648 | tf_op jit(solution)/shard_map/all_to_all | solution.py:178
  42.5 5.2 %collective-permute-start.6 = (bf16[8,2,144,128]{3,2,1,0:T(8,128)(2,1)}, bf16[8,2,144,128]{3,2,1,0:T(8,128)(2,1)S(1)}, u32[]{:S(2)}, u32[]{:S(2)}) collective-permute-start(bf16[8,2,144,128]{3,2,1,0:T(8,128)(2,1)} %get-tuple-element.7), channel_id=1, source_target_pairs={{0,64},{8,72},{16,80},{24,88},{32,96},{40,104},{48,112},{56,120},{... | collective-permute-start | bytes 1769480 | tf_op jit(solution)/shard_map/ppermute | solution.py:175
  47.7 3.0 %all-to-all-done.2.refs_4_ = bf16[8,2,144,128]{3,2,1,0:T(8,128)(2,1)S(1)} async-done(((bf16[8,2,144,128]{3,2,1,0:T(8,128)(2,1)}), bf16[8,2,144,128]{3,2,1,0:T(8,128)(2,1)S(1)}, u32[]{:S(2)}, u32[]{:S(2)}) %all-to-all-start.2) | async-done | bytes 589856 | tf_op jit(solution)/shard_map/all_to_all | solution.py:178
  50.6 3.1 %collective-permute-start.3 = (bf16[8,2,144,128]{3,2,1,0:T(8,128)(2,1)S(1)}, bf16[8,2,144,128]{3,2,1,0:T(8,128)(2,1)}, u32[]{:S(2)}, u32[]{:S(2)}) collective-permute-start(bf16[8,2,144,128]{3,2,1,0:T(8,128)(2,1)S(1)} %all-to-all-done.2.refs_4_), channel_id=1, source_target_pairs={{0,128},{8,136},{16,144},{24,152},{32,160},{40,168},{48,176},{56,1... | collective-permute-start | bytes 1769480 | tf_op jit(solution)/shard_map/ppermute | solution.py:175
  53.7 17.2 %collective-permute-start = (bf16[8,2,144,128]{3,2,1,0:T(8,128)(2,1)}, bf16[8,2,144,128]{3,2,1,0:T(8,128)(2,1)}, u32[]{:S(2)}, u32[]{:S(2)}) collective-permute-start(bf16[8,2,144,128]{3,2,1,0:T(8,128)(2,1)} %get-tuple-element.11), channel_id=1, source_target_pairs={{0,8},{8,16},{16,24},{24,32},{32,40},{40,48},{48,56},{64,72},{72,8... | collective-permute-start | bytes 1769480 | tf_op jit(solution)/shard_map/ppermute | solution.py:175
  72.8 3.6 %collective-permute-start.4 = (bf16[8,2,144,128]{3,2,1,0:T(8,128)(2,1)}, bf16[8,2,144,128]{3,2,1,0:T(8,128)(2,1)S(1)}, u32[]{:S(2)}, u32[]{:S(2)}) collective-permute-start(bf16[8,2,144,128]{3,2,1,0:T(8,128)(2,1)} %get-tuple-element.7), channel_id=1, source_target_pairs={{0,8},{8,16},{16,24},{24,32},{32,40},{40,48},{48,56},{64,72},{72,8... | collective-permute-start | bytes 1769480 | tf_op jit(solution)/shard_map/ppermute | solution.py:175
  76.5 3.0 %collective-permute-start.10 = (bf16[8,2,144,128]{3,2,1,0:T(8,128)(2,1)}, bf16[8,2,144,128]{3,2,1,0:T(8,128)(2,1)S(1)}, u32[]{:S(2)}, u32[]{:S(2)}) collective-permute-start(bf16[8,2,144,128]{3,2,1,0:T(8,128)(2,1)} %get-tuple-element.8), channel_id=1, source_target_pairs={{0,64},{8,72},{16,80},{24,88},{32,96},{40,104},{48,112},{56,120},{... | collective-permute-start | bytes 1769480 | tf_op jit(solution)/shard_map/ppermute | solution.py:175
  79.6 2.3 %pack.3 = bf16[8,3,144,128]{3,2,1,0:T(8,128)(2,1)} custom-call(bf16[144,3072]{1,0:T(8,128)(2,1)} %refs_0_.3), custom_call_target="tpu_custom_call" | custom-call | bytes 1769472 | tf_op jit(solution)/shard_map/pack/pallas_call | solution.py:40
  81.9 3.6 %all-to-all-start = ((bf16[8,3,144,128]{3,2,1,0:T(8,128)(2,1)}), bf16[8,3,144,128]{3,2,1,0:T(8,128)(2,1)S(1)}, u32[]{:S(2)}, u32[]{:S(2)}) async-start(bf16[8,3,144,128]{3,2,1,0:T(8,128)(2,1)} %pack.3), calls=%async_computation | async-start | bytes 1769472 | tf_op jit(solution)/shard_map/all_to_all | solution.py:178
  85.5 13.2 %collective-permute-start.5 = (bf16[8,2,144,128]{3,2,1,0:T(8,128)(2,1)}, bf16[8,2,144,128]{3,2,1,0:T(8,128)(2,1)S(1)}, u32[]{:S(2)}, u32[]{:S(2)}) collective-permute-start(bf16[8,2,144,128]{3,2,1,0:T(8,128)(2,1)} %get-tuple-element.7), channel_id=1, source_target_pairs={{8,0},{16,8},{24,16},{32,24},{40,32},{48,40},{56,48},{72,64},{80,7... | collective-permute-start | bytes 1769480 | tf_op jit(solution)/shard_map/ppermute | solution.py:175
  98.6 4.7 %collective-permute-start.7 = (bf16[8,2,144,128]{3,2,1,0:T(8,128)(2,1)S(1)}, bf16[8,2,144,128]{3,2,1,0:T(8,128)(2,1)}, u32[]{:S(2)}, u32[]{:S(2)}) collective-permute-start(bf16[8,2,144,128]{3,2,1,0:T(8,128)(2,1)S(1)} %collective-permute-done.6.refs_4_), channel_id=1, source_target_pairs={{0,128},{8,136},{16,144},{24,152},{32,160},{40,168},{48,176},{56,1... | collective-permute-start | bytes 1769480 | tf_op jit(solution)/shard_map/ppermute | solution.py:175
  105.9 3.2 %collective-permute-start.9 = (bf16[8,2,144,128]{3,2,1,0:T(8,128)(2,1)}, bf16[8,2,144,128]{3,2,1,0:T(8,128)(2,1)}, u32[]{:S(2)}, u32[]{:S(2)}) collective-permute-start(bf16[8,2,144,128]{3,2,1,0:T(8,128)(2,1)} %get-tuple-element.8), channel_id=1, source_target_pairs={{8,0},{16,8},{24,16},{32,24},{40,32},{48,40},{56,48},{72,64},{80,7... | collective-permute-start | bytes 1769480 | tf_op jit(solution)/shard_map/ppermute | solution.py:175
  109.1 10.6 %collective-permute-done.10.refs_4_ = bf16[8,2,144,128]{3,2,1,0:T(8,128)(2,1)S(1)} collective-permute-done((bf16[8,2,144,128]{3,2,1,0:T(8,128)(2,1)}, bf16[8,2,144,128]{3,2,1,0:T(8,128)(2,1)S(1)}, u32[]{:S(2)}, u32[]{:S(2)}) %collective-permute-start.10) | collective-permute-done | bytes 589856 | tf_op jit(solution)/shard_map/ppermute | solution.py:175
  119.7 3.3 %collective-permute-start.11 = (bf16[8,2,144,128]{3,2,1,0:T(8,128)(2,1)S(1)}, bf16[8,2,144,128]{3,2,1,0:T(8,128)(2,1)}, u32[]{:S(2)}, u32[]{:S(2)}) collective-permute-start(bf16[8,2,144,128]{3,2,1,0:T(8,128)(2,1)S(1)} %collective-permute-done.10.refs_4_), channel_id=1, source_target_pairs={{0,128},{8,136},{16,144},{24,152},{32,160},{40,168},{48,176},{56,1... | collective-permute-start | bytes 1769480 | tf_op jit(solution)/shard_map/ppermute | solution.py:175
  124.6 7.7 %attend.3 = bf16[8,144,128]{2,1,0:T(8,128)(2,1)} custom-call(s32[3,5]{1,0:T(4,128)} %fusion.1.idx_ref, s32[3,5]{1,0:T(4,128)} %fusion.4.live_ref, bf16[8,3,144,128]{3,2,1,0:T(8,128)(2,1)} %copy-done.1, bf16[8,6,144,128]{3,2,1,0:T(8,128)(2,1)} %copy-done, bf16[8,2,144,128]{3,2,1,0:T(8,128)(2,1)} %collective-permute-done.refs_2_, ...), custom_call_target="tpu_custom_call" | custom-call | flops 1132462080 | bytes 4128768 | tf_op jit(solution)/shard_map/attend/pallas_call | solution.py:139
  132.3 5.6 %all-to-all-start.3 = ((bf16[8,144,128]{2,1,0:T(8,128)(2,1)}), bf16[8,144,128]{2,1,0:T(8,128)(2,1)S(1)}, u32[]{:S(2)}, u32[]{:S(2)}) async-start(bf16[8,144,128]{2,1,0:T(8,128)(2,1)} %attend.3), calls=%async_computation.3 | async-start | bytes 589824 | tf_op jit(solution)/shard_map/all_to_all | solution.py:178
  138.8 7.7 %attend.4 = bf16[8,144,128]{2,1,0:T(8,128)(2,1)} custom-call(s32[3,5]{1,0:T(4,128)} %fusion.1.idx_ref, s32[3,5]{1,0:T(4,128)} %fusion.4.live_ref, bf16[8,3,144,128]{3,2,1,0:T(8,128)(2,1)} %copy-done.1, bf16[8,6,144,128]{3,2,1,0:T(8,128)(2,1)} %copy-done, bf16[8,2,144,128]{3,2,1,0:T(8,128)(2,1)} %copy-done.7, bf16[8,2,144,128]{3,2,1,0:T(8,128)(2,1)} %copy-done.8, ...), custom_call_target="tpu_custom_call" | custom-call | flops 1132462080 | bytes 4128768 | tf_op jit(solution)/shard_map/attend/pallas_call | solution.py:139
  146.5 6.6 %all-to-all-start.4 = ((bf16[8,144,128]{2,1,0:T(8,128)(2,1)}), bf16[8,144,128]{2,1,0:T(8,128)(2,1)S(1)}, u32[]{:S(2)}, u32[]{:S(2)}) async-start(bf16[8,144,128]{2,1,0:T(8,128)(2,1)} %attend.4), calls=%async_computation.4 | async-start | bytes 589824 | tf_op jit(solution)/shard_map/all_to_all | solution.py:178
  153.2 7.7 %attend.5 = bf16[8,144,128]{2,1,0:T(8,128)(2,1)} custom-call(s32[3,5]{1,0:T(4,128)} %fusion.1.idx_ref, s32[3,5]{1,0:T(4,128)} %fusion.4.live_ref, bf16[8,3,144,128]{3,2,1,0:T(8,128)(2,1)} %copy-done.1, bf16[8,6,144,128]{3,2,1,0:T(8,128)(2,1)} %copy-done, bf16[8,2,144,128]{3,2,1,0:T(8,128)(2,1)} %collective-permute-done.8.refs_2_, ...), custom_call_target="tpu_custom_call" | custom-call | flops 1132462080 | bytes 4128768 | tf_op jit(solution)/shard_map/attend/pallas_call | solution.py:139
  161.4 15.3 %all_to_all.30.refs_2_ = bf16[8,144,128]{2,1,0:T(8,128)(2,1)} all-to-all(bf16[8,144,128]{2,1,0:T(8,128)(2,1)} %attend.5), channel_id=1, replica_groups=mesh['seq'=32,'head'=8] {'head'}, dimensions={0} | all-to-all | bytes 589824 | tf_op jit(solution)/shard_map/all_to_all | solution.py:178
  (41 shorter events, 12.8 us)
Async XLA Ops:
  3.1 31.7 %all-to-all-start.1 = ((bf16[8,6,144,128]{3,2,1,0:T(8,128)(2,1)}), bf16[8,6,144,128]{3,2,1,0:T(8,128)(2,1)S(1)}, u32[]{:S(2)}, u32[]{:S(2)}) async-start(bf16[8,6,144,128]{3,2,1,0:T(8,128)(2,1)} %pack.4), calls=%async_computation.1 | async-start | bytes 3538944 | tf_op jit(solution)/shard_map/all_to_all | solution.py:178
  12.6 22.2 %collective-permute-start.2 = (bf16[8,2,144,128]{3,2,1,0:T(8,128)(2,1)}, bf16[8,2,144,128]{3,2,1,0:T(8,128)(2,1)}, u32[]{:S(2)}, u32[]{:S(2)}) collective-permute-start(bf16[8,2,144,128]{3,2,1,0:T(8,128)(2,1)} %pack.5), channel_id=1, source_target_pairs={{0,64},{8,72},{16,80},{24,88},{32,96},{40,104},{48,112},{56,120},{... | collective-permute-start | bytes 1769480 | tf_op jit(solution)/shard_map/ppermute | solution.py:175
  34.8 15.8 %all-to-all-start.2 = ((bf16[8,2,144,128]{3,2,1,0:T(8,128)(2,1)}), bf16[8,2,144,128]{3,2,1,0:T(8,128)(2,1)S(1)}, u32[]{:S(2)}, u32[]{:S(2)}) async-start(bf16[8,2,144,128]{3,2,1,0:T(8,128)(2,1)} %collective-permute-done.2), calls=%async_computation.2 | async-start | bytes 1179648 | tf_op jit(solution)/shard_map/all_to_all | solution.py:178
  42.5 34.0 %collective-permute-start.6 = (bf16[8,2,144,128]{3,2,1,0:T(8,128)(2,1)}, bf16[8,2,144,128]{3,2,1,0:T(8,128)(2,1)S(1)}, u32[]{:S(2)}, u32[]{:S(2)}) collective-permute-start(bf16[8,2,144,128]{3,2,1,0:T(8,128)(2,1)} %get-tuple-element.7), channel_id=1, source_target_pairs={{0,64},{8,72},{16,80},{24,88},{32,96},{40,104},{48,112},{56,120},{... | collective-permute-start | bytes 1769480 | tf_op jit(solution)/shard_map/ppermute | solution.py:175
  50.6 31.3 %copy-start.2 = (bf16[8,2,144,128]{3,2,1,0:T(8,128)(2,1)}, bf16[8,2,144,128]{3,2,1,0:T(8,128)(2,1)S(1)}, u32[]{:S(2)}) copy-start(bf16[8,2,144,128]{3,2,1,0:T(8,128)(2,1)S(1)} %all-to-all-done.2.refs_4_) | copy-start | bytes 1769476
  50.6 34.8 %collective-permute-start.3 = (bf16[8,2,144,128]{3,2,1,0:T(8,128)(2,1)S(1)}, bf16[8,2,144,128]{3,2,1,0:T(8,128)(2,1)}, u32[]{:S(2)}, u32[]{:S(2)}) collective-permute-start(bf16[8,2,144,128]{3,2,1,0:T(8,128)(2,1)S(1)} %all-to-all-done.2.refs_4_), channel_id=1, source_target_pairs={{0,128},{8,136},{16,144},{24,152},{32,160},{40,168},{48,176},{56,1... | collective-permute-start | bytes 1769480 | tf_op jit(solution)/shard_map/ppermute | solution.py:175
  53.7 44.9 %collective-permute-start = (bf16[8,2,144,128]{3,2,1,0:T(8,128)(2,1)}, bf16[8,2,144,128]{3,2,1,0:T(8,128)(2,1)}, u32[]{:S(2)}, u32[]{:S(2)}) collective-permute-start(bf16[8,2,144,128]{3,2,1,0:T(8,128)(2,1)} %get-tuple-element.11), channel_id=1, source_target_pairs={{0,8},{8,16},{16,24},{24,32},{32,40},{40,48},{48,56},{64,72},{72,8... | collective-permute-start | bytes 1769480 | tf_op jit(solution)/shard_map/ppermute | solution.py:175
  70.9 33.1 %collective-permute-start.1 = (bf16[8,2,144,128]{3,2,1,0:T(8,128)(2,1)}, bf16[8,2,144,128]{3,2,1,0:T(8,128)(2,1)}, u32[]{:S(2)}, u32[]{:S(2)}) collective-permute-start(bf16[8,2,144,128]{3,2,1,0:T(8,128)(2,1)} %get-tuple-element.11), channel_id=1, source_target_pairs={{8,0},{16,8},{24,16},{32,24},{40,32},{48,40},{56,48},{72,64},{80,7... | collective-permute-start | bytes 1769480 | tf_op jit(solution)/shard_map/ppermute | solution.py:175
  72.8 33.1 %collective-permute-start.4 = (bf16[8,2,144,128]{3,2,1,0:T(8,128)(2,1)}, bf16[8,2,144,128]{3,2,1,0:T(8,128)(2,1)S(1)}, u32[]{:S(2)}, u32[]{:S(2)}) collective-permute-start(bf16[8,2,144,128]{3,2,1,0:T(8,128)(2,1)} %get-tuple-element.7), channel_id=1, source_target_pairs={{0,8},{8,16},{16,24},{24,32},{32,40},{40,48},{48,56},{64,72},{72,8... | collective-permute-start | bytes 1769480 | tf_op jit(solution)/shard_map/ppermute | solution.py:175
  76.5 22.1 %copy-start.5 = (bf16[8,2,144,128]{3,2,1,0:T(8,128)(2,1)}, bf16[8,2,144,128]{3,2,1,0:T(8,128)(2,1)S(1)}, u32[]{:S(2)}) copy-start(bf16[8,2,144,128]{3,2,1,0:T(8,128)(2,1)S(1)} %collective-permute-done.6.refs_4_) | copy-start | bytes 1769476
  76.5 26.9 %copy-start.9 = (s32[3,5]{1,0:T(4,128)S(1)}, s32[3,5]{1,0:T(4,128)}, u32[]{:S(2)}) copy-start(s32[3,5]{1,0:T(4,128)} %param.7) | copy-start | bytes 184
  76.5 43.2 %collective-permute-start.10 = (bf16[8,2,144,128]{3,2,1,0:T(8,128)(2,1)}, bf16[8,2,144,128]{3,2,1,0:T(8,128)(2,1)S(1)}, u32[]{:S(2)}, u32[]{:S(2)}) collective-permute-start(bf16[8,2,144,128]{3,2,1,0:T(8,128)(2,1)} %get-tuple-element.8), channel_id=1, source_target_pairs={{0,64},{8,72},{16,80},{24,88},{32,96},{40,104},{48,112},{56,120},{... | collective-permute-start | bytes 1769480 | tf_op jit(solution)/shard_map/ppermute | solution.py:175
  81.9 41.8 %all-to-all-start = ((bf16[8,3,144,128]{3,2,1,0:T(8,128)(2,1)}), bf16[8,3,144,128]{3,2,1,0:T(8,128)(2,1)S(1)}, u32[]{:S(2)}, u32[]{:S(2)}) async-start(bf16[8,3,144,128]{3,2,1,0:T(8,128)(2,1)} %pack.3), calls=%async_computation | async-start | bytes 1769472 | tf_op jit(solution)/shard_map/all_to_all | solution.py:178
  85.5 52.5 %collective-permute-start.5 = (bf16[8,2,144,128]{3,2,1,0:T(8,128)(2,1)}, bf16[8,2,144,128]{3,2,1,0:T(8,128)(2,1)S(1)}, u32[]{:S(2)}, u32[]{:S(2)}) collective-permute-start(bf16[8,2,144,128]{3,2,1,0:T(8,128)(2,1)} %get-tuple-element.7), channel_id=1, source_target_pairs={{8,0},{16,8},{24,16},{32,24},{40,32},{48,40},{56,48},{72,64},{80,7... | collective-permute-start | bytes 1769480 | tf_op jit(solution)/shard_map/ppermute | solution.py:175
  98.6 39.3 %collective-permute-start.7 = (bf16[8,2,144,128]{3,2,1,0:T(8,128)(2,1)S(1)}, bf16[8,2,144,128]{3,2,1,0:T(8,128)(2,1)}, u32[]{:S(2)}, u32[]{:S(2)}) collective-permute-start(bf16[8,2,144,128]{3,2,1,0:T(8,128)(2,1)S(1)} %collective-permute-done.6.refs_4_), channel_id=1, source_target_pairs={{0,128},{8,136},{16,144},{24,152},{32,160},{40,168},{48,176},{56,1... | collective-permute-start | bytes 1769480 | tf_op jit(solution)/shard_map/ppermute | solution.py:175
  104.0 49.2 %collective-permute-start.8 = (bf16[8,2,144,128]{3,2,1,0:T(8,128)(2,1)}, bf16[8,2,144,128]{3,2,1,0:T(8,128)(2,1)}, u32[]{:S(2)}, u32[]{:S(2)}) collective-permute-start(bf16[8,2,144,128]{3,2,1,0:T(8,128)(2,1)} %get-tuple-element.8), channel_id=1, source_target_pairs={{0,8},{8,16},{16,24},{24,32},{32,40},{40,48},{48,56},{64,72},{72,8... | collective-permute-start | bytes 1769480 | tf_op jit(solution)/shard_map/ppermute | solution.py:175
  105.9 32.0 %copy-start.7 = (bf16[8,2,144,128]{3,2,1,0:T(8,128)(2,1)}, bf16[8,2,144,128]{3,2,1,0:T(8,128)(2,1)S(1)}, u32[]{:S(2)}) copy-start(bf16[8,2,144,128]{3,2,1,0:T(8,128)(2,1)S(1)} %collective-permute-done.4.refs_2_) | copy-start | bytes 1769476
  105.9 47.3 %collective-permute-start.9 = (bf16[8,2,144,128]{3,2,1,0:T(8,128)(2,1)}, bf16[8,2,144,128]{3,2,1,0:T(8,128)(2,1)}, u32[]{:S(2)}, u32[]{:S(2)}) collective-permute-start(bf16[8,2,144,128]{3,2,1,0:T(8,128)(2,1)} %get-tuple-element.8), channel_id=1, source_target_pairs={{8,0},{16,8},{24,16},{32,24},{40,32},{48,40},{56,48},{72,64},{80,7... | collective-permute-start | bytes 1769480 | tf_op jit(solution)/shard_map/ppermute | solution.py:175
  119.7 26.8 %copy-start.6 = (bf16[8,2,144,128]{3,2,1,0:T(8,128)(2,1)}, bf16[8,2,144,128]{3,2,1,0:T(8,128)(2,1)S(1)}, u32[]{:S(2)}) copy-start(bf16[8,2,144,128]{3,2,1,0:T(8,128)(2,1)S(1)} %collective-permute-done.10.refs_4_) | copy-start | bytes 1769476
  119.7 33.5 %collective-permute-start.11 = (bf16[8,2,144,128]{3,2,1,0:T(8,128)(2,1)S(1)}, bf16[8,2,144,128]{3,2,1,0:T(8,128)(2,1)}, u32[]{:S(2)}, u32[]{:S(2)}) collective-permute-start(bf16[8,2,144,128]{3,2,1,0:T(8,128)(2,1)S(1)} %collective-permute-done.10.refs_4_), channel_id=1, source_target_pairs={{0,128},{8,136},{16,144},{24,152},{32,160},{40,168},{48,176},{56,1... | collective-permute-start | bytes 1769480 | tf_op jit(solution)/shard_map/ppermute | solution.py:175
  132.3 14.2 %all-to-all-start.3 = ((bf16[8,144,128]{2,1,0:T(8,128)(2,1)}), bf16[8,144,128]{2,1,0:T(8,128)(2,1)S(1)}, u32[]{:S(2)}, u32[]{:S(2)}) async-start(bf16[8,144,128]{2,1,0:T(8,128)(2,1)} %attend.3), calls=%async_computation.3 | async-start | bytes 589824 | tf_op jit(solution)/shard_map/all_to_all | solution.py:178
  146.5 14.4 %copy-start.3 = (bf16[8,144,128]{2,1,0:T(8,128)(2,1)}, bf16[8,144,128]{2,1,0:T(8,128)(2,1)S(1)}, u32[]{:S(2)}) copy-start(bf16[8,144,128]{2,1,0:T(8,128)(2,1)S(1)} %all-to-all-done.3.refs_0_) | copy-start | bytes 884740
  146.5 14.9 %all-to-all-start.4 = ((bf16[8,144,128]{2,1,0:T(8,128)(2,1)}), bf16[8,144,128]{2,1,0:T(8,128)(2,1)S(1)}, u32[]{:S(2)}, u32[]{:S(2)}) async-start(bf16[8,144,128]{2,1,0:T(8,128)(2,1)} %attend.4), calls=%async_computation.4 | async-start | bytes 589824 | tf_op jit(solution)/shard_map/all_to_all | solution.py:178
  161.4 15.3 %copy-start.4 = (bf16[8,144,128]{2,1,0:T(8,128)(2,1)}, bf16[8,144,128]{2,1,0:T(8,128)(2,1)S(1)}, u32[]{:S(2)}) copy-start(bf16[8,144,128]{2,1,0:T(8,128)(2,1)S(1)} %all-to-all-done.4.refs_1_) | copy-start | bytes 884740
  (3 other events, 9.4 us)

commit v3 on v2

--- a/solution.py
+++ b/solution.py
@@ -25,9 +25,9 @@
     copies = []
     for at, (array, head) in enumerate(picks):
         for g in range(o_ref.shape[0]):
-            copy = pltpu.make_async_copy(
-                arrays[array].at[:, pl.ds((g * local + head) * HD, HD)], o_ref.at[g, at], sems.at[at, g]
-            )
+            source = arrays[array]
+            piece = source.at[:, pl.ds((g * local + head) * HD, HD)] if len(source.shape) == 2 else source.at[g, head]
+            copy = pltpu.make_async_copy(piece, o_ref.at[g, at], sems.at[at, g])
             copy.start()
             copies.append(copy)
     for copy in copies:
@@ -191,24 +191,33 @@
 
     first = pack([keys, values], [(0, 0), (1, 0)], groups)
     crossed = send(first, across)
-    rest = pack([keys, values], [(n, i) for i in range(local) for n in range(2)], groups)
-    own = exchange(rest)
-    q_all = pack([query], [(0, i) for i in range(local)], groups)
-    own_of = [own[:, 2 * i : 2 * i + 2] for i in range(local)]
+    rest = pack([keys, values], [(0, 1), (1, 1), (0, 2), (1, 2)], groups)
+    rest = exchange(rest)
+    most = pack(
+        [keys, values, query, crossed],
+        [(0, 0), (1, 0), (2, 0), (2, 1), (2, 2), (3, 0), (3, 1)],
+        groups,
+    )
+    most = exchange(most)
+    own_of = [most[:, 0:2], rest[:, 0:2], rest[:, 2:4]]
     far, second, before, behind, outs = [[None] * local for _ in range(5)]
+    far[0] = most[:, 5:7]
     far[1] = send(after(own_of[1], crossed), across)
-    far[0] = exchange(crossed)
     far[2] = send(after(own_of[2], far[1]), across)
-    q_all = exchange(q_all)
-    for i in range(local):
+    places = [
+        [(2,), (0, 1), (0, 1), (0, 1), (5, 6), (0, 1)],
+        [(3,), (0, 1), (0, 1), (0, 1), (0, 1), (0, 1)],
+        [(4,), (2, 3), (0, 1), (0, 1), (0, 1), (0, 1)],
+    ]
+    for i in (1, 0, 2):
         before[i] = send(own_of[i], right)
         behind[i] = send(own_of[i], left)
         second[i] = send(far[i], middle)
         o = attend(
             idx,
             live,
-            [q_all, own, before[i], behind[i], far[i], second[i]],
-            [(i,), (2 * i, 2 * i + 1)] + [(0, 1)] * 4,
+            [most, rest if i else most, before[i], behind[i], far[i] if i else most, second[i]],
+            places[i],
         )
         outs[i] = exchange(o)
     return unpack(outs)

time: 180 us -> 187 us (1.039)
  the two profiles are of different devices: /device:TPU:1 before, /device:TPU:32 now
where the time goes in v3:
time: 187 us; the launch traced here: 186 us
  starting transfers between devices  66.7 us (36%)
  waiting for transfers between devices  66.2 us (35%)
  Pallas kernels  33.4 us (18%)
  blocking collectives  15.3 us (8%)
  local copies, waits for them, and re-layouts  3.13 us (2%)
    ppermute x12, waiting for transfers between devices, send(): return lax.ppermute(x, 'seq', pairs)  61.7 us
    ppermute x12, starting transfers between devices, send(): return lax.ppermute(x, 'seq', pairs)  41.9 us
    all_to_all x4, starting transfers between devices, exchange(): return lax.all_to_all(x, 'head', split_axis=0, concat_axis=0, tiled=True)  24.8 us
    pallas_call x3, Pallas kernels, attend(): pl.pallas_call(functools.partial(attend_kernel, slab // per_slab, per_sla...  23.2 us
    all_to_all x1, blocking collectives, exchange(): return lax.all_to_all(x, 'head', split_axis=0, concat_axis=0, tiled=True)  15.3 us
    pallas_call x3, Pallas kernels, pack(): pl.pallas_call(functools.partial(pack_kernel, picks, width // (groups * H...  7.95 us
    all_to_all x4, waiting for transfers between devices, exchange(): return lax.all_to_all(x, 'head', split_axis=0, concat_axis=0, tiled=True)  4.46 us
  transfers between devices with their start and end apart: 16, of which 6 were waited for; matrix products, arithmetic and copies ran while one was open for 2% of the time, Pallas kernels for 15%

profile of v3, /device:TPU:32, one launch (start us, length us, event | category | flops | bytes accessed | tf_op | source)
XLA Modules:
  0.0 186.1 jit_solution(17481927975737910286)
XLA Ops:
  0.0 2.6 %pack.5 = bf16[8,4,144,128]{3,2,1,0:T(8,128)(2,1)} custom-call(bf16[144,3072]{1,0:T(8,128)(2,1)} %refs_0_.5, bf16[144,3072]{1,0:T(8,128)(2,1)} %refs_1_.5), custom_call_target="tpu_custom_call" | custom-call | bytes 2359296 | tf_op jit(solution)/shard_map/pack/pallas_call | solution.py:40
  2.6 6.9 %all-to-all-start.2 = ((bf16[8,4,144,128]{3,2,1,0:T(8,128)(2,1)}), bf16[8,4,144,128]{3,2,1,0:T(8,128)(2,1)S(1)}, u32[]{:S(2)}, u32[]{:S(2)}) async-start(bf16[8,4,144,128]{3,2,1,0:T(8,128)(2,1)} %pack.5), calls=%async_computation.2 | async-start | bytes 2359296 | tf_op jit(solution)/shard_map/all_to_all | solution.py:178
  11.5 6.4 %collective-permute-start = (bf16[8,2,144,128]{3,2,1,0:T(8,128)(2,1)}, bf16[8,2,144,128]{3,2,1,0:T(8,128)(2,1)S(1)}, u32[]{:S(2)}, u32[]{:S(2)}) collective-permute-start(bf16[8,2,144,128]{3,2,1,0:T(8,128)(2,1)} %pack.3), channel_id=1, source_target_pairs={{0,64},{8,72},{16,80},{24,88},{32,96},{40,104},{48,112},{56,120},{... | collective-permute-start | bytes 1769480 | tf_op jit(solution)/shard_map/ppermute | solution.py:175
  17.9 26.0 %collective-permute-done.refs_3_ = bf16[8,2,144,128]{3,2,1,0:T(8,128)(2,1)S(1)} collective-permute-done((bf16[8,2,144,128]{3,2,1,0:T(8,128)(2,1)}, bf16[8,2,144,128]{3,2,1,0:T(8,128)(2,1)S(1)}, u32[]{:S(2)}, u32[]{:S(2)}) %collective-permute-start) | collective-permute-done | bytes 589856 | tf_op jit(solution)/shard_map/ppermute | solution.py:175
  44.7 3.4 %pack.4 = bf16[8,7,144,128]{3,2,1,0:T(8,128)(2,1)} custom-call(bf16[144,3072]{1,0:T(8,128)(2,1)} %refs_0_.5, bf16[144,3072]{1,0:T(8,128)(2,1)} %refs_1_.5, bf16[144,3072]{1,0:T(8,128)(2,1)} %refs_2_.1, bf16[8,2,144,128]{3,2,1,0:T(8,128)(2,1)} %copy-done.6), custom_call_target="tpu_custom_call" | custom-call | bytes 4128768 | tf_op jit(solution)/shard_map/pack/pallas_call | solution.py:40
  48.1 6.9 %all-to-all-start = ((bf16[8,7,144,128]{3,2,1,0:T(8,128)(2,1)}), bf16[8,7,144,128]{3,2,1,0:T(8,128)(2,1)S(1)}, u32[]{:S(2)}, u32[]{:S(2)}) async-start(bf16[8,7,144,128]{3,2,1,0:T(8,128)(2,1)} %pack.4), calls=%async_computation | async-start | bytes 4128768 | tf_op jit(solution)/shard_map/all_to_all | solution.py:178
  56.2 5.6 %collective-permute-start.6 = (bf16[8,2,144,128]{3,2,1,0:T(8,128)(2,1)}, bf16[8,2,144,128]{3,2,1,0:T(8,128)(2,1)S(1)}, u32[]{:S(2)}, u32[]{:S(2)}) collective-permute-start(bf16[8,2,144,128]{3,2,1,0:T(8,128)(2,1)} %get-tuple-element.7), channel_id=1, source_target_pairs={{0,64},{8,72},{16,80},{24,88},{32,96},{40,104},{48,112},{56,120},{... | collective-permute-start | bytes 1769480 | tf_op jit(solution)/shard_map/ppermute | solution.py:175
  63.7 32.0 %collective-permute-done.6.refs_4_ = bf16[8,2,144,128]{3,2,1,0:T(8,128)(2,1)S(1)} collective-permute-done((bf16[8,2,144,128]{3,2,1,0:T(8,128)(2,1)}, bf16[8,2,144,128]{3,2,1,0:T(8,128)(2,1)S(1)}, u32[]{:S(2)}, u32[]{:S(2)}) %collective-permute-start.6) | collective-permute-done | bytes 589856 | tf_op jit(solution)/shard_map/ppermute | solution.py:175
  95.7 5.1 %collective-permute-start.10 = (bf16[8,2,144,128]{3,2,1,0:T(8,128)(2,1)}, bf16[8,2,144,128]{3,2,1,0:T(8,128)(2,1)S(1)}, u32[]{:S(2)}, u32[]{:S(2)}) collective-permute-start(bf16[8,2,144,128]{3,2,1,0:T(8,128)(2,1)} %get-tuple-element.8), channel_id=1, source_target_pairs={{0,64},{8,72},{16,80},{24,88},{32,96},{40,104},{48,112},{56,120},{... | collective-permute-start | bytes 1769480 | tf_op jit(solution)/shard_map/ppermute | solution.py:175
  102.7 2.4 %collective-permute-start.8 = (bf16[8,2,144,128]{3,2,1,0:T(8,128)(2,1)}, bf16[8,2,144,128]{3,2,1,0:T(8,128)(2,1)}, u32[]{:S(2)}, u32[]{:S(2)}) collective-permute-start(bf16[8,2,144,128]{3,2,1,0:T(8,128)(2,1)} %get-tuple-element.8), channel_id=1, source_target_pairs={{0,8},{8,16},{16,24},{24,32},{32,40},{40,48},{48,56},{64,72},{72,8... | collective-permute-start | bytes 1769480 | tf_op jit(solution)/shard_map/ppermute | solution.py:175
  105.1 3.3 %collective-permute-start.7 = (bf16[8,2,144,128]{3,2,1,0:T(8,128)(2,1)S(1)}, bf16[8,2,144,128]{3,2,1,0:T(8,128)(2,1)}, u32[]{:S(2)}, u32[]{:S(2)}) collective-permute-start(bf16[8,2,144,128]{3,2,1,0:T(8,128)(2,1)S(1)} %collective-permute-done.6.refs_4_), channel_id=1, source_target_pairs={{0,128},{8,136},{16,144},{24,152},{32,160},{40,168},{48,176},{56,1... | collective-permute-start | bytes 1769480 | tf_op jit(solution)/shard_map/ppermute | solution.py:175
  109.0 2.9 %collective-permute-start.9 = (bf16[8,2,144,128]{3,2,1,0:T(8,128)(2,1)}, bf16[8,2,144,128]{3,2,1,0:T(8,128)(2,1)}, u32[]{:S(2)}, u32[]{:S(2)}) collective-permute-start(bf16[8,2,144,128]{3,2,1,0:T(8,128)(2,1)} %get-tuple-element.8), channel_id=1, source_target_pairs={{8,0},{16,8},{24,16},{32,24},{40,32},{48,40},{56,48},{72,64},{80,7... | collective-permute-start | bytes 1769480 | tf_op jit(solution)/shard_map/ppermute | solution.py:175
  111.9 3.1 %collective-permute-done.10.refs_4_ = bf16[8,2,144,128]{3,2,1,0:T(8,128)(2,1)S(1)} collective-permute-done((bf16[8,2,144,128]{3,2,1,0:T(8,128)(2,1)}, bf16[8,2,144,128]{3,2,1,0:T(8,128)(2,1)S(1)}, u32[]{:S(2)}, u32[]{:S(2)}) %collective-permute-start.10) | collective-permute-done | bytes 589856 | tf_op jit(solution)/shard_map/ppermute | solution.py:175
  115.0 3.4 %collective-permute-start.11 = (bf16[8,2,144,128]{3,2,1,0:T(8,128)(2,1)S(1)}, bf16[8,2,144,128]{3,2,1,0:T(8,128)(2,1)}, u32[]{:S(2)}, u32[]{:S(2)}) collective-permute-start(bf16[8,2,144,128]{3,2,1,0:T(8,128)(2,1)S(1)} %collective-permute-done.10.refs_4_), channel_id=1, source_target_pairs={{0,128},{8,136},{16,144},{24,152},{32,160},{40,168},{48,176},{56,1... | collective-permute-start | bytes 1769480 | tf_op jit(solution)/shard_map/ppermute | solution.py:175
  120.2 2.8 %collective-permute-start.1 = (bf16[8,2,144,128]{3,2,1,0:T(8,128)(2,1)}, bf16[8,2,144,128]{3,2,1,0:T(8,128)(2,1)}, u32[]{:S(2)}, u32[]{:S(2)}) collective-permute-start(bf16[8,2,144,128]{3,2,1,0:T(8,128)(2,1)} %get-tuple-element.10), channel_id=1, source_target_pairs={{0,8},{8,16},{16,24},{24,32},{32,40},{40,48},{48,56},{64,72},{72,8... | collective-permute-start | bytes 1769480 | tf_op jit(solution)/shard_map/ppermute | solution.py:175
  123.0 2.9 %collective-permute-start.2 = (bf16[8,2,144,128]{3,2,1,0:T(8,128)(2,1)}, bf16[8,2,144,128]{3,2,1,0:T(8,128)(2,1)}, u32[]{:S(2)}, u32[]{:S(2)}) collective-permute-start(bf16[8,2,144,128]{3,2,1,0:T(8,128)(2,1)} %get-tuple-element.10), channel_id=1, source_target_pairs={{8,0},{16,8},{24,16},{32,24},{40,32},{48,40},{56,48},{72,64},{80,7... | collective-permute-start | bytes 1769480 | tf_op jit(solution)/shard_map/ppermute | solution.py:175
  125.9 3.3 %collective-permute-start.3 = (bf16[8,2,144,128]{3,2,1,0:T(8,128)(2,1)}, bf16[8,2,144,128]{3,2,1,0:T(8,128)(2,1)}, u32[]{:S(2)}, u32[]{:S(2)}) collective-permute-start(bf16[8,2,144,128]{3,2,1,0:T(8,128)(2,1)} %get-tuple-element.9), channel_id=1, source_target_pairs={{0,128},{8,136},{16,144},{24,152},{32,160},{40,168},{48,176},{56,1... | collective-permute-start | bytes 1769480 | tf_op jit(solution)/shard_map/ppermute | solution.py:175
  129.9 7.7 %attend.4 = bf16[8,144,128]{2,1,0:T(8,128)(2,1)} custom-call(s32[3,5]{1,0:T(4,128)} %fusion.1.idx_ref, s32[3,5]{1,0:T(4,128)} %fusion.4.live_ref, bf16[8,7,144,128]{3,2,1,0:T(8,128)(2,1)} %copy-done, bf16[8,4,144,128]{3,2,1,0:T(8,128)(2,1)} %copy-done.1, bf16[8,2,144,128]{3,2,1,0:T(8,128)(2,1)} %collective-permute-done.4.refs_2_, ...), custom_call_target="tpu_custom_call" | custom-call | flops 1132462080 | bytes 4128768 | tf_op jit(solution)/shard_map/attend/pallas_call | solution.py:139
  137.6 6.9 %all-to-all-start.3 = ((bf16[8,144,128]{2,1,0:T(8,128)(2,1)}), bf16[8,144,128]{2,1,0:T(8,128)(2,1)S(1)}, u32[]{:S(2)}, u32[]{:S(2)}) async-start(bf16[8,144,128]{2,1,0:T(8,128)(2,1)} %attend.4), calls=%async_computation.3 | async-start | bytes 589824 | tf_op jit(solution)/shard_map/all_to_all | solution.py:178
  144.6 7.7 %attend.5 = bf16[8,144,128]{2,1,0:T(8,128)(2,1)} custom-call(s32[3,5]{1,0:T(4,128)} %fusion.1.idx_ref, s32[3,5]{1,0:T(4,128)} %fusion.4.live_ref, bf16[8,7,144,128]{3,2,1,0:T(8,128)(2,1)} %copy-done, bf16[8,4,144,128]{3,2,1,0:T(8,128)(2,1)} %copy-done.1, bf16[8,2,144,128]{3,2,1,0:T(8,128)(2,1)} %collective-permute-done.8.refs_2_, ...), custom_call_target="tpu_custom_call" | custom-call | flops 1132462080 | bytes 4128768 | tf_op jit(solution)/shard_map/attend/pallas_call | solution.py:139
  152.3 3.2 %all-to-all-done.3.refs_1_ = bf16[8,144,128]{2,1,0:T(8,128)(2,1)S(1)} async-done(((bf16[8,144,128]{2,1,0:T(8,128)(2,1)}), bf16[8,144,128]{2,1,0:T(8,128)(2,1)S(1)}, u32[]{:S(2)}, u32[]{:S(2)}) %all-to-all-start.3) | async-done | bytes 294944 | tf_op jit(solution)/shard_map/all_to_all | solution.py:178
  155.6 4.0 %all-to-all-start.4 = ((bf16[8,144,128]{2,1,0:T(8,128)(2,1)}), bf16[8,144,128]{2,1,0:T(8,128)(2,1)S(1)}, u32[]{:S(2)}, u32[]{:S(2)}) async-start(bf16[8,144,128]{2,1,0:T(8,128)(2,1)} %attend.5), calls=%async_computation.4 | async-start | bytes 589824 | tf_op jit(solution)/shard_map/all_to_all | solution.py:178
  159.6 7.7 %attend.3 = bf16[8,144,128]{2,1,0:T(8,128)(2,1)} custom-call(s32[3,5]{1,0:T(4,128)} %fusion.1.idx_ref, s32[3,5]{1,0:T(4,128)} %fusion.4.live_ref, bf16[8,7,144,128]{3,2,1,0:T(8,128)(2,1)} %copy-done, bf16[8,7,144,128]{3,2,1,0:T(8,128)(2,1)} %copy-done, bf16[8,2,144,128]{3,2,1,0:T(8,128)(2,1)} %collective-permute-done.1.refs_2_, ...), custom_call_target="tpu_custom_call" | custom-call | flops 1132462080 | bytes 4128768 | tf_op jit(solution)/shard_map/attend/pallas_call | solution.py:139
  168.5 15.3 %all_to_all.25.refs_0_ = bf16[8,144,128]{2,1,0:T(8,128)(2,1)} all-to-all(bf16[8,144,128]{2,1,0:T(8,128)(2,1)} %attend.3), channel_id=1, replica_groups=mesh['seq'=32,'head'=8] {'head'}, dimensions={0} | all-to-all | bytes 589824 | tf_op jit(solution)/shard_map/all_to_all | solution.py:178
  (36 shorter events, 14.3 us)
Async XLA Ops:
  2.6 45.5 %all-to-all-start.2 = ((bf16[8,4,144,128]{3,2,1,0:T(8,128)(2,1)}), bf16[8,4,144,128]{3,2,1,0:T(8,128)(2,1)S(1)}, u32[]{:S(2)}, u32[]{:S(2)}) async-start(bf16[8,4,144,128]{3,2,1,0:T(8,128)(2,1)} %pack.5), calls=%async_computation.2 | async-start | bytes 2359296 | tf_op jit(solution)/shard_map/all_to_all | solution.py:178
  11.5 32.3 %collective-permute-start = (bf16[8,2,144,128]{3,2,1,0:T(8,128)(2,1)}, bf16[8,2,144,128]{3,2,1,0:T(8,128)(2,1)S(1)}, u32[]{:S(2)}, u32[]{:S(2)}) collective-permute-start(bf16[8,2,144,128]{3,2,1,0:T(8,128)(2,1)} %pack.3), channel_id=1, source_target_pairs={{0,64},{8,72},{16,80},{24,88},{32,96},{40,104},{48,112},{56,120},{... | collective-permute-start | bytes 1769480 | tf_op jit(solution)/shard_map/ppermute | solution.py:175
  43.9 0.8 copy-start.6
  48.1 7.0 %copy-start.1 = (bf16[8,4,144,128]{3,2,1,0:T(8,128)(2,1)}, bf16[8,4,144,128]{3,2,1,0:T(8,128)(2,1)S(1)}, u32[]{:S(2)}) copy-start(bf16[8,4,144,128]{3,2,1,0:T(8,128)(2,1)S(1)} %all-to-all-done.2.refs_1_) | copy-start | bytes 3538948
  48.1 70.2 %all-to-all-start = ((bf16[8,7,144,128]{3,2,1,0:T(8,128)(2,1)}), bf16[8,7,144,128]{3,2,1,0:T(8,128)(2,1)S(1)}, u32[]{:S(2)}, u32[]{:S(2)}) async-start(bf16[8,7,144,128]{3,2,1,0:T(8,128)(2,1)} %pack.4), calls=%async_computation | async-start | bytes 4128768 | tf_op jit(solution)/shard_map/all_to_all | solution.py:178
  55.0 53.4 %copy-start.7 = (s32[3,5]{1,0:T(4,128)S(1)}, s32[3,5]{1,0:T(4,128)}, u32[]{:S(2)}) copy-start(s32[3,5]{1,0:T(4,128)} %param.7) | copy-start | bytes 184
  56.2 39.5 %collective-permute-start.6 = (bf16[8,2,144,128]{3,2,1,0:T(8,128)(2,1)}, bf16[8,2,144,128]{3,2,1,0:T(8,128)(2,1)S(1)}, u32[]{:S(2)}, u32[]{:S(2)}) collective-permute-start(bf16[8,2,144,128]{3,2,1,0:T(8,128)(2,1)} %get-tuple-element.7), channel_id=1, source_target_pairs={{0,64},{8,72},{16,80},{24,88},{32,96},{40,104},{48,112},{56,120},{... | collective-permute-start | bytes 1769480 | tf_op jit(solution)/shard_map/ppermute | solution.py:175
  61.8 47.3 %collective-permute-start.4 = (bf16[8,2,144,128]{3,2,1,0:T(8,128)(2,1)}, bf16[8,2,144,128]{3,2,1,0:T(8,128)(2,1)}, u32[]{:S(2)}, u32[]{:S(2)}) collective-permute-start(bf16[8,2,144,128]{3,2,1,0:T(8,128)(2,1)} %get-tuple-element.7), channel_id=1, source_target_pairs={{0,8},{8,16},{16,24},{24,32},{32,40},{40,48},{48,56},{64,72},{72,8... | collective-permute-start | bytes 1769480 | tf_op jit(solution)/shard_map/ppermute | solution.py:175
  95.7 34.2 %copy-start.5 = (bf16[8,2,144,128]{3,2,1,0:T(8,128)(2,1)}, bf16[8,2,144,128]{3,2,1,0:T(8,128)(2,1)S(1)}, u32[]{:S(2)}) copy-start(bf16[8,2,144,128]{3,2,1,0:T(8,128)(2,1)S(1)} %collective-permute-done.6.refs_4_) | copy-start | bytes 1769476
  95.7 19.3 %collective-permute-start.10 = (bf16[8,2,144,128]{3,2,1,0:T(8,128)(2,1)}, bf16[8,2,144,128]{3,2,1,0:T(8,128)(2,1)S(1)}, u32[]{:S(2)}, u32[]{:S(2)}) collective-permute-start(bf16[8,2,144,128]{3,2,1,0:T(8,128)(2,1)} %get-tuple-element.8), channel_id=1, source_target_pairs={{0,64},{8,72},{16,80},{24,88},{32,96},{40,104},{48,112},{56,120},{... | collective-permute-start | bytes 1769480 | tf_op jit(solution)/shard_map/ppermute | solution.py:175
  100.8 19.4 %collective-permute-start.5 = (bf16[8,2,144,128]{3,2,1,0:T(8,128)(2,1)}, bf16[8,2,144,128]{3,2,1,0:T(8,128)(2,1)}, u32[]{:S(2)}, u32[]{:S(2)}) collective-permute-start(bf16[8,2,144,128]{3,2,1,0:T(8,128)(2,1)} %get-tuple-element.7), channel_id=1, source_target_pairs={{8,0},{16,8},{24,16},{32,24},{40,32},{48,40},{56,48},{72,64},{80,7... | collective-permute-start | bytes 1769480 | tf_op jit(solution)/shard_map/ppermute | solution.py:175
  102.7 20.3 %collective-permute-start.8 = (bf16[8,2,144,128]{3,2,1,0:T(8,128)(2,1)}, bf16[8,2,144,128]{3,2,1,0:T(8,128)(2,1)}, u32[]{:S(2)}, u32[]{:S(2)}) collective-permute-start(bf16[8,2,144,128]{3,2,1,0:T(8,128)(2,1)} %get-tuple-element.8), channel_id=1, source_target_pairs={{0,8},{8,16},{16,24},{24,32},{32,40},{40,48},{48,56},{64,72},{72,8... | collective-permute-start | bytes 1769480 | tf_op jit(solution)/shard_map/ppermute | solution.py:175
  105.1 20.8 %collective-permute-start.7 = (bf16[8,2,144,128]{3,2,1,0:T(8,128)(2,1)S(1)}, bf16[8,2,144,128]{3,2,1,0:T(8,128)(2,1)}, u32[]{:S(2)}, u32[]{:S(2)}) collective-permute-start(bf16[8,2,144,128]{3,2,1,0:T(8,128)(2,1)S(1)} %collective-permute-done.6.refs_4_), channel_id=1, source_target_pairs={{0,128},{8,136},{16,144},{24,152},{32,160},{40,168},{48,176},{56,1... | collective-permute-start | bytes 1769480 | tf_op jit(solution)/shard_map/ppermute | solution.py:175
  109.0 35.5 %collective-permute-start.9 = (bf16[8,2,144,128]{3,2,1,0:T(8,128)(2,1)}, bf16[8,2,144,128]{3,2,1,0:T(8,128)(2,1)}, u32[]{:S(2)}, u32[]{:S(2)}) collective-permute-start(bf16[8,2,144,128]{3,2,1,0:T(8,128)(2,1)} %get-tuple-element.8), channel_id=1, source_target_pairs={{8,0},{16,8},{24,16},{32,24},{40,32},{48,40},{56,48},{72,64},{80,7... | collective-permute-start | bytes 1769480 | tf_op jit(solution)/shard_map/ppermute | solution.py:175
  115.0 29.6 %copy-start.4 = (bf16[8,2,144,128]{3,2,1,0:T(8,128)(2,1)}, bf16[8,2,144,128]{3,2,1,0:T(8,128)(2,1)S(1)}, u32[]{:S(2)}) copy-start(bf16[8,2,144,128]{3,2,1,0:T(8,128)(2,1)S(1)} %collective-permute-done.10.refs_4_) | copy-start | bytes 1769476
  115.0 29.6 %collective-permute-start.11 = (bf16[8,2,144,128]{3,2,1,0:T(8,128)(2,1)S(1)}, bf16[8,2,144,128]{3,2,1,0:T(8,128)(2,1)}, u32[]{:S(2)}, u32[]{:S(2)}) collective-permute-start(bf16[8,2,144,128]{3,2,1,0:T(8,128)(2,1)S(1)} %collective-permute-done.10.refs_4_), channel_id=1, source_target_pairs={{0,128},{8,136},{16,144},{24,152},{32,160},{40,168},{48,176},{56,1... | collective-permute-start | bytes 1769480 | tf_op jit(solution)/shard_map/ppermute | solution.py:175
  118.3 11.6 %copy-start = (bf16[8,7,144,128]{3,2,1,0:T(8,128)(2,1)}, bf16[8,7,144,128]{3,2,1,0:T(8,128)(2,1)S(1)}, u32[]{:S(2)}) copy-start(bf16[8,7,144,128]{3,2,1,0:T(8,128)(2,1)S(1)} %all-to-all-done.refs_0_.refs_1_.refs_4_) | copy-start | bytes 6193156
  120.2 39.4 %collective-permute-start.1 = (bf16[8,2,144,128]{3,2,1,0:T(8,128)(2,1)}, bf16[8,2,144,128]{3,2,1,0:T(8,128)(2,1)}, u32[]{:S(2)}, u32[]{:S(2)}) collective-permute-start(bf16[8,2,144,128]{3,2,1,0:T(8,128)(2,1)} %get-tuple-element.10), channel_id=1, source_target_pairs={{0,8},{8,16},{16,24},{24,32},{32,40},{40,48},{48,56},{64,72},{72,8... | collective-permute-start | bytes 1769480 | tf_op jit(solution)/shard_map/ppermute | solution.py:175
  123.0 36.5 %collective-permute-start.2 = (bf16[8,2,144,128]{3,2,1,0:T(8,128)(2,1)}, bf16[8,2,144,128]{3,2,1,0:T(8,128)(2,1)}, u32[]{:S(2)}, u32[]{:S(2)}) collective-permute-start(bf16[8,2,144,128]{3,2,1,0:T(8,128)(2,1)} %get-tuple-element.10), channel_id=1, source_target_pairs={{8,0},{16,8},{24,16},{32,24},{40,32},{48,40},{56,48},{72,64},{80,7... | collective-permute-start | bytes 1769480 | tf_op jit(solution)/shard_map/ppermute | solution.py:175
  125.9 33.6 %collective-permute-start.3 = (bf16[8,2,144,128]{3,2,1,0:T(8,128)(2,1)}, bf16[8,2,144,128]{3,2,1,0:T(8,128)(2,1)}, u32[]{:S(2)}, u32[]{:S(2)}) collective-permute-start(bf16[8,2,144,128]{3,2,1,0:T(8,128)(2,1)} %get-tuple-element.9), channel_id=1, source_target_pairs={{0,128},{8,136},{16,144},{24,152},{32,160},{40,168},{48,176},{56,1... | collective-permute-start | bytes 1769480 | tf_op jit(solution)/shard_map/ppermute | solution.py:175
  137.6 17.9 %all-to-all-start.3 = ((bf16[8,144,128]{2,1,0:T(8,128)(2,1)}), bf16[8,144,128]{2,1,0:T(8,128)(2,1)S(1)}, u32[]{:S(2)}, u32[]{:S(2)}) async-start(bf16[8,144,128]{2,1,0:T(8,128)(2,1)} %attend.4), calls=%async_computation.3 | async-start | bytes 589824 | tf_op jit(solution)/shard_map/all_to_all | solution.py:178
  155.6 11.7 %copy-start.2 = (bf16[8,144,128]{2,1,0:T(8,128)(2,1)}, bf16[8,144,128]{2,1,0:T(8,128)(2,1)S(1)}, u32[]{:S(2)}) copy-start(bf16[8,144,128]{2,1,0:T(8,128)(2,1)S(1)} %all-to-all-done.3.refs_1_) | copy-start | bytes 884740
  155.6 13.0 %all-to-all-start.4 = ((bf16[8,144,128]{2,1,0:T(8,128)(2,1)}), bf16[8,144,128]{2,1,0:T(8,128)(2,1)S(1)}, u32[]{:S(2)}, u32[]{:S(2)}) async-start(bf16[8,144,128]{2,1,0:T(8,128)(2,1)} %attend.5), calls=%async_computation.4 | async-start | bytes 589824 | tf_op jit(solution)/shard_map/all_to_all | solution.py:178
  168.5 15.3 %copy-start.3 = (bf16[8,144,128]{2,1,0:T(8,128)(2,1)}, bf16[8,144,128]{2,1,0:T(8,128)(2,1)S(1)}, u32[]{:S(2)}) copy-start(bf16[8,144,128]{2,1,0:T(8,128)(2,1)S(1)} %all-to-all-done.4.refs_2_) | copy-start | bytes 884740

commit v4 on v3

v4 whole, which is shorter than its diff:
```python
import functools

import jax
import jax.numpy as jnp
from jax import lax
from jax.experimental import pallas as pl
from jax.experimental.pallas import tpu as pltpu
from jax.sharding import PartitionSpec as P


HD = 128
TFR = 4
PIECES = 2
SCALE2 = 1.4426950408889634 / HD**0.5


ANY = pl.BlockSpec(memory_space=pl.ANY)


def after(value, *first):
    return lax.optimization_barrier((value,) + first)[0]


def pack_kernel(picks, local, count, *refs):
    arrays, o_ref, sems = refs[:count], refs[count], refs[count + 1]
    copies = []
    for at, (array, head) in enumerate(picks):
        for g in range(o_ref.shape[0]):
            source = arrays[array]
            piece = source.at[:, pl.ds((g * local + head) * HD, HD)] if len(source.shape) == 2 else source.at[g, head]
            copy = pltpu.make_async_copy(piece, o_ref.at[g, at], sems.at[at, g])
            copy.start()
            copies.append(copy)
    for copy in copies:
        copy.wait()


def pack(arrays, picks, groups):
    rows, width = arrays[0].shape
    shape = (groups, len(picks), rows, HD)
    return pl.pallas_call(
        functools.partial(pack_kernel, picks, width // (groups * HD), len(arrays)),
        out_shape=jax.ShapeDtypeStruct(shape, arrays[0].dtype),
        grid=(1,),
        in_specs=[ANY] * len(arrays),
        out_specs=pl.BlockSpec(shape, lambda i: (0, 0, 0, 0)),
        scratch_shapes=[pltpu.SemaphoreType.DMA((len(picks), groups))],
        cost_estimate=pl.CostEstimate(
            flops=0, bytes_accessed=4 * groups * len(picks) * rows * HD, transcendentals=0
        ),
        name="pack",
    )(*arrays)


def unpack_kernel(part, o_ref, sems):
    groups, local = part.shape[:2]
    copies = []
    for head in range(local):
        for g in range(groups):
            copy = pltpu.make_async_copy(
                part.at[g, head], o_ref.at[:, pl.ds((g * local + head) * HD, HD)], sems.at[head, g]
            )
            copy.start()
            copies.append(copy)
    for copy in copies:
        copy.wait()


def unpack(part):
    groups, local, rows, _ = part.shape
    return pl.pallas_call(
        unpack_kernel,
        out_shape=jax.ShapeDtypeStruct((rows, groups * local * HD), part.dtype),
        grid=(1,),
        in_specs=[pl.BlockSpec(part.shape, lambda i: (0, 0, 0, 0))],
        out_specs=ANY,
        scratch_shapes=[pltpu.SemaphoreType.DMA((local, groups))],
        cost_estimate=pl.CostEstimate(
            flops=0, bytes_accessed=4 * groups * local * rows * HD, transcendentals=0
        ),
        name="unpack",
    )(part)


def attend_kernel(tile, per_slab, plan, count, idx_ref, live_ref, *refs):
    sources, o_ref, held, q_held, o_held, s_held, sems, o_sems = refs[:count], *refs[count:]
    heads = len(plan)
    blocks, rows = sources[0].shape[0], sources[0].shape[2]
    slab = blocks * rows
    copies = []
    for h, taken in enumerate(plan):
        for at, (source, *parts) in enumerate(taken):
            for n, part in enumerate(parts):
                into = q_held.at[h] if at == 0 else held.at[h, n, pl.ds((at - 1) * blocks, blocks)]
                copy = pltpu.make_async_copy(sources[source].at[:, part], into, sems.at[h, at, n])
                copy.start()
                copies.append((h, copy))
    flat = held.reshape(heads, 2, held.shape[2] * rows, HD)
    q_flat = q_held.reshape(heads, slab, HD)
    o_flat = o_held.reshape(heads, slab, HD)
    slots = idx_ref.shape[1]
    spans = tile // HD
    block = tile // PIECES

    def one_tile(h, t):
        start = pl.multiple_of(t * tile, 128)
        begins = [pl.multiple_of(idx_ref[t, j] * tile, 128) for j in range(slots)]
        alive = [live_ref[t, j] > 0 for j in range(slots)]
        for p in range(PIECES):
            q = q_flat[h, pl.ds(start + p * block, block), :]
            most = None
            for j in range(slots):
                k = flat[h, 0, pl.ds(begins[j], tile), :]
                s = lax.dot_general(q, k, (((1,), (1,)), ((), ())), preferred_element_type=jnp.float32)
                s_held[p, j] = s
                top = functools.reduce(jnp.maximum, [s[:, c * HD : (c + 1) * HD] for c in range(spans)])
                if j:
                    top = jnp.where(alive[j], top, -jnp.inf)
                most = top if most is None else jnp.maximum(most, top)
            top = jnp.max(most, axis=1, keepdims=True) * SCALE2
            total = mixed = None
            for j in range(slots):
                shift = jnp.where(alive[j], top, jnp.inf) if j else top
                expo = jnp.exp2(s_held[p, j] * SCALE2 - shift)
                part = functools.reduce(jnp.add, [expo[:, c * HD : (c + 1) * HD] for c in range(spans)])
                v = flat[h, 1, pl.ds(begins[j], tile), :]
                pv = jnp.dot(expo.astype(jnp.bfloat16), v, preferred_element_type=jnp.float32)
                total = part if total is None else total + part
                mixed = pv if mixed is None else mixed + pv
            total = jnp.sum(total, axis=1, keepdims=True)
            o_flat[h, pl.ds(start + p * block, block), :] = (mixed / total).astype(o_flat.dtype)

    outs = []
    for h in range(heads):
        for g, copy in copies:
            if g == h:
                copy.wait()

        def step(t, carry, h=h):
            one_tile(h, t)
            return carry

        lax.fori_loop(0, per_slab, step, 0)
        copy = pltpu.make_async_copy(o_held.at[h], o_ref.at[:, h], o_sems.at[h])
        copy.start()
        outs.append(copy)
    for copy in outs:
        copy.wait()


def attend(idx, live, sources, plan):
    per_slab, slots = idx.shape
    blocks, _, rows, _ = sources[0].shape
    slab = blocks * rows
    tile = slab // per_slab
    keys = slots * tile
    heads, columns = len(plan), len(plan[0]) - 1
    dtype = sources[0].dtype
    return pl.pallas_call(
        functools.partial(attend_kernel, tile, per_slab, plan, len(sources)),
        out_shape=jax.ShapeDtypeStruct((blocks, heads, rows, HD), dtype),
        grid_spec=pltpu.PrefetchScalarGridSpec(
            num_scalar_prefetch=2,
            grid=(1,),
            in_specs=[ANY] * len(sources),
            out_specs=ANY,
            scratch_shapes=[
                pltpu.VMEM((heads, 2, columns * blocks, rows, HD), dtype),
                pltpu.VMEM((heads, blocks, rows, HD), dtype),
                pltpu.VMEM((heads, blocks, rows, HD), dtype),
                pltpu.VMEM((PIECES, slots, tile // PIECES, tile), jnp.float32),
                pltpu.SemaphoreType.DMA((heads, columns + 1, 2)),
                pltpu.SemaphoreType.DMA((heads,)),
            ],
        ),
        cost_estimate=pl.CostEstimate(
            flops=4 * heads * slab * keys * HD,
            bytes_accessed=4 * heads * slab * HD * (columns + 1),
            transcendentals=heads * slab * keys,
        ),
        name="attend",
    )(idx, live, *sources)


def body(query, keys, values, windows):
    groups = lax.axis_size("head")
    peers = lax.axis_size("seq")
    columns = peers // TFR
    per_slab = windows.shape[0]

    across = [(s, s ^ columns) for s in range(peers)]
    right = [(s, s + 1) for s in range(peers) if (s + 1) % columns]
    left = [(s, s - 1) for s in range(peers) if s % columns]
    middle = [(s, s + 2 * columns) for s in range(columns)] + [
        (s, s - 2 * columns) for s in range(3 * columns, peers)
    ]

    def send(x, pairs):
        return lax.ppermute(x, "seq", pairs)

    def exchange(x):
        return lax.all_to_all(x, "head", split_axis=0, concat_axis=0, tiled=True)

    here = lax.axis_index("seq")
    live = windows >= 0
    delta = windows // per_slab - here
    partner = jnp.where(here // columns % 2 == 0, columns, -columns)
    code = jnp.where(
        delta == 0,
        0,
        jnp.where(delta == -1, 1, jnp.where(delta == 1, 2, jnp.where(delta == partner, 3, 4))),
    )
    idx = jnp.where(live, code * per_slab + windows % per_slab, 0)
    live = live.astype(jnp.int32)

    first = pack([keys, values], [(0, 0), (1, 0)], groups)
    crossed = send(first, across)
    rest = pack([keys, values], [(0, 1), (1, 1), (0, 2), (1, 2)], groups)
    rest = exchange(rest)
    most = pack(
        [keys, values, query, crossed],
        [(0, 0), (1, 0), (2, 0), (2, 1), (2, 2), (3, 0), (3, 1)],
        groups,
    )
    most = exchange(most)
    far1 = send(after(rest[:, 0:2], crossed), across)
    far2 = send(after(rest[:, 2:4], crossed), across)
    own0 = most[:, 0:2]
    before12 = send(rest, right)
    behind12 = send(rest, left)
    before0 = send(own0, right)
    behind0 = send(own0, left)
    second0 = send(most[:, 5:7], middle)
    second1 = send(far1, middle)
    second2 = send(far2, middle)
    sources = [most, rest, before0, behind0, before12, behind12, far1, far2, second0, second1, second2]
    plan = [
        [(0, 2), (0, 0, 1), (2, 0, 1), (3, 0, 1), (0, 5, 6), (8, 0, 1)],
        [(0, 3), (1, 0, 1), (4, 0, 1), (5, 0, 1), (6, 0, 1), (9, 0, 1)],
        [(0, 4), (1, 2, 3), (4, 2, 3), (5, 2, 3), (7, 0, 1), (10, 0, 1)],
    ]
    o = attend(idx, live, sources, plan)
    o = exchange(o)
    return unpack(o)


def solution(mesh):
    return jax.shard_map(
        body,
        mesh=mesh,
        in_specs=(
            P(("seq", "head"), None),
            P(("seq", "head"), None),
            P(("seq", "head"), None),
            P("seq", None),
        ),
        out_specs=P(("seq", "head"), None),
        check_vma=False,
    )
```

time: 187 us -> 181 us (0.968)
  starting transfers between devices: 66.7 us -> 41.9 us
  waiting for transfers between devices: 66.2 us -> 81.4 us
  blocking collectives: 15.3 us -> 22.5 us
  Pallas kernels: 33.4 us -> 28.6 us
    ppermute x12 -> x10, waiting for transfers between devices: 61.7 us -> 81.3 us  [send(): return lax.ppermute(x, 'seq', pairs)]
    ppermute x12 -> x10, starting transfers between devices: 41.9 us -> 28 us  [send(): return lax.ppermute(x, 'seq', pairs)]
    all_to_all x4 -> x2, starting transfers between devices: 24.8 us -> 13.9 us  [exchange(): return lax.all_to_all(x, 'head', split_axis=0, concat_axis=0, tiled=True)]
    all_to_all x1, blocking collectives: 15.3 us -> 22.5 us  [exchange(): return lax.all_to_all(x, 'head', split_axis=0, concat_axis=0, tiled=True)]
    pallas_call x4 -> x2, Pallas kernels: 25.4 us -> 20.6 us  [the longest x1 18.3 us: attend(): pl.pallas_call(functools.partial(attend_kernel, tile, per_slab, plan, len...]
    all_to_all x4 -> x2, waiting for transfers between devices: 4.46 us -> 0.01 us  [exchange(): return lax.all_to_all(x, 'head', split_axis=0, concat_axis=0, tiled=True)]
    unnamed x16 -> x14, local copies, waits for them, and re-layouts: 0.84 us -> 3.27 us
  transfers between devices with their start and end apart: 16 -> 12, of which waited for: 6 -> 5; matrix products, arithmetic and copies ran while one was open for 2% -> 1% of each run, Pallas kernels for 15% -> 3%
where the time goes in v4:
time: 181 us; the launch traced here: 180 us
  waiting for transfers between devices  81.4 us (45%)
  starting transfers between devices  41.9 us (23%)
  Pallas kernels  28.6 us (16%)
  blocking collectives  22.5 us (12%)
  local copies, waits for them, and re-layouts  4.49 us (2%)
    ppermute x10, waiting for transfers between devices, send(): return lax.ppermute(x, 'seq', pairs)  81.3 us
    ppermute x10, starting transfers between devices, send(): return lax.ppermute(x, 'seq', pairs)  28 us
    all_to_all x1, blocking collectives, exchange(): return lax.all_to_all(x, 'head', split_axis=0, concat_axis=0, tiled=True)  22.5 us
    pallas_call x1, Pallas kernels, attend(): pl.pallas_call(functools.partial(attend_kernel, tile, per_slab, plan, len...  18.3 us
    all_to_all x2, starting transfers between devices, exchange(): return lax.all_to_all(x, 'head', split_axis=0, concat_axis=0, tiled=True)  13.9 us
    pallas_call x3, Pallas kernels, pack(): pl.pallas_call(functools.partial(pack_kernel, picks, width // (groups * H...  7.96 us
  transfers between devices with their start and end apart: 12, of which 5 were waited for; matrix products, arithmetic and copies ran while one was open for 1% of the time, Pallas kernels for 3%

profile of v4, /device:TPU:32, one launch (start us, length us, event | category | flops | bytes accessed | tf_op | source)
XLA Modules:
  0.0 180.1 jit_solution(14842944178799603794)
XLA Ops:
  0.0 2.6 %pack.5 = bf16[8,4,144,128]{3,2,1,0:T(8,128)(2,1)} custom-call(bf16[144,3072]{1,0:T(8,128)(2,1)} %refs_0_.5, bf16[144,3072]{1,0:T(8,128)(2,1)} %refs_1_.5), custom_call_target="tpu_custom_call" | custom-call | bytes 2359296 | tf_op jit(solution)/shard_map/pack/pallas_call | solution.py:41
  2.6 6.9 %all-to-all-start.1 = ((bf16[8,4,144,128]{3,2,1,0:T(8,128)(2,1)}), bf16[8,4,144,128]{3,2,1,0:T(8,128)(2,1)S(1)}, u32[]{:S(2)}, u32[]{:S(2)}) async-start(bf16[8,4,144,128]{3,2,1,0:T(8,128)(2,1)} %pack.5), calls=%async_computation.1 | async-start | bytes 2359296 | tf_op jit(solution)/shard_map/all_to_all | solution.py:202
  9.5 2.0 %pack.3 = bf16[8,2,144,128]{3,2,1,0:T(8,128)(2,1)} custom-call(bf16[144,3072]{1,0:T(8,128)(2,1)} %refs_0_.5, bf16[144,3072]{1,0:T(8,128)(2,1)} %refs_1_.5), custom_call_target="tpu_custom_call" | custom-call | bytes 1179648 | tf_op jit(solution)/shard_map/pack/pallas_call | solution.py:41
  11.5 6.4 %collective-permute-start = (bf16[8,2,144,128]{3,2,1,0:T(8,128)(2,1)}, bf16[8,2,144,128]{3,2,1,0:T(8,128)(2,1)S(1)}, u32[]{:S(2)}, u32[]{:S(2)}) collective-permute-start(bf16[8,2,144,128]{3,2,1,0:T(8,128)(2,1)} %pack.3), channel_id=1, source_target_pairs={{0,64},{8,72},{16,80},{24,88},{32,96},{40,104},{48,112},{56,120},{... | collective-permute-start | bytes 1769480 | tf_op jit(solution)/shard_map/ppermute | solution.py:199
  17.9 26.0 %collective-permute-done.refs_3_ = bf16[8,2,144,128]{3,2,1,0:T(8,128)(2,1)S(1)} collective-permute-done((bf16[8,2,144,128]{3,2,1,0:T(8,128)(2,1)}, bf16[8,2,144,128]{3,2,1,0:T(8,128)(2,1)S(1)}, u32[]{:S(2)}, u32[]{:S(2)}) %collective-permute-start) | collective-permute-done | bytes 589856 | tf_op jit(solution)/shard_map/ppermute | solution.py:199
  44.7 3.4 %pack.4 = bf16[8,7,144,128]{3,2,1,0:T(8,128)(2,1)} custom-call(bf16[144,3072]{1,0:T(8,128)(2,1)} %refs_0_.5, bf16[144,3072]{1,0:T(8,128)(2,1)} %refs_1_.5, bf16[144,3072]{1,0:T(8,128)(2,1)} %refs_2_.1, bf16[8,2,144,128]{3,2,1,0:T(8,128)(2,1)} %copy-done.2), custom_call_target="tpu_custom_call" | custom-call | bytes 4128768 | tf_op jit(solution)/shard_map/pack/pallas_call | solution.py:41
  48.1 6.9 %all-to-all-start = ((bf16[8,7,144,128]{3,2,1,0:T(8,128)(2,1)}), bf16[8,7,144,128]{3,2,1,0:T(8,128)(2,1)S(1)}, u32[]{:S(2)}, u32[]{:S(2)}) async-start(bf16[8,7,144,128]{3,2,1,0:T(8,128)(2,1)} %pack.4), calls=%async_computation | async-start | bytes 4128768 | tf_op jit(solution)/shard_map/all_to_all | solution.py:202
  55.1 5.7 %collective-permute-start.5 = (bf16[8,2,144,128]{3,2,1,0:T(8,128)(2,1)S(1)}, bf16[8,2,144,128]{3,2,1,0:T(8,128)(2,1)}, u32[]{:S(2)}, u32[]{:S(2)}) collective-permute-start(bf16[8,2,144,128]{3,2,1,0:T(8,128)(2,1)S(1)} %get-tuple-element.7), channel_id=1, source_target_pairs={{0,64},{8,72},{16,80},{24,88},{32,96},{40,104},{48,112},{56,120},{... | collective-permute-start | bytes 1769480 | tf_op jit(solution)/shard_map/ppermute | solution.py:199
  61.1 1.9 %collective-permute-start.4 = (bf16[8,4,144,128]{3,2,1,0:T(8,128)(2,1)S(1)}, bf16[8,4,144,128]{3,2,1,0:T(8,128)(2,1)}, u32[]{:S(2)}, u32[]{:S(2)}) collective-permute-start(bf16[8,4,144,128]{3,2,1,0:T(8,128)(2,1)S(1)} %all-to-all-done.1.refs_1_), channel_id=1, source_target_pairs={{8,0},{16,8},{24,16},{32,24},{40,32},{48,40},{56,48},{72,64},{80,7... | collective-permute-start | bytes 3538952 | tf_op jit(solution)/shard_map/ppermute | solution.py:199
  63.1 31.4 %collective-permute-done.5.refs_6_ = bf16[8,2,144,128]{3,2,1,0:T(8,128)(2,1)} collective-permute-done((bf16[8,2,144,128]{3,2,1,0:T(8,128)(2,1)S(1)}, bf16[8,2,144,128]{3,2,1,0:T(8,128)(2,1)}, u32[]{:S(2)}, u32[]{:S(2)}) %collective-permute-start.5) | collective-permute-done | bytes 589856 | tf_op jit(solution)/shard_map/ppermute | solution.py:199
  94.4 3.3 %collective-permute-start.8 = (bf16[8,2,144,128]{3,2,1,0:T(8,128)(2,1)}, bf16[8,2,144,128]{3,2,1,0:T(8,128)(2,1)}, u32[]{:S(2)}, u32[]{:S(2)}) collective-permute-start(bf16[8,2,144,128]{3,2,1,0:T(8,128)(2,1)} %collective-permute-done.5.refs_6_), channel_id=1, source_target_pairs={{0,128},{8,136},{16,144},{24,152},{32,160},{40,168},{48,176},{56,1... | collective-permute-start | bytes 1769480 | tf_op jit(solution)/shard_map/ppermute | solution.py:199
  97.7 1.9 %collective-permute-start.3 = (bf16[8,4,144,128]{3,2,1,0:T(8,128)(2,1)S(1)}, bf16[8,4,144,128]{3,2,1,0:T(8,128)(2,1)}, u32[]{:S(2)}, u32[]{:S(2)}) collective-permute-start(bf16[8,4,144,128]{3,2,1,0:T(8,128)(2,1)S(1)} %all-to-all-done.1.refs_1_), channel_id=1, source_target_pairs={{0,8},{8,16},{16,24},{24,32},{32,40},{40,48},{48,56},{64,72},{72,8... | collective-permute-start | bytes 3538952 | tf_op jit(solution)/shard_map/ppermute | solution.py:199
  99.7 7.3 %collective-permute-done.6.refs_7_ = bf16[8,2,144,128]{3,2,1,0:T(8,128)(2,1)} collective-permute-done((bf16[8,2,144,128]{3,2,1,0:T(8,128)(2,1)S(1)}, bf16[8,2,144,128]{3,2,1,0:T(8,128)(2,1)}, u32[]{:S(2)}, u32[]{:S(2)}) %collective-permute-start.6) | collective-permute-done | bytes 589856 | tf_op jit(solution)/shard_map/ppermute | solution.py:199
  107.0 3.3 %collective-permute-start.9 = (bf16[8,2,144,128]{3,2,1,0:T(8,128)(2,1)}, bf16[8,2,144,128]{3,2,1,0:T(8,128)(2,1)}, u32[]{:S(2)}, u32[]{:S(2)}) collective-permute-start(bf16[8,2,144,128]{3,2,1,0:T(8,128)(2,1)} %collective-permute-done.6.refs_7_), channel_id=1, source_target_pairs={{0,128},{8,136},{16,144},{24,152},{32,160},{40,168},{48,176},{56,1... | collective-permute-start | bytes 1769480 | tf_op jit(solution)/shard_map/ppermute | solution.py:199
  110.3 1.1 fusion.5
  112.0 1.3 collective-permute-start.7
  113.3 1.9 %collective-permute-start.2 = (bf16[8,2,144,128]{3,2,1,0:T(8,128)(2,1)}, bf16[8,2,144,128]{3,2,1,0:T(8,128)(2,1)S(1)}, u32[]{:S(2)}, u32[]{:S(2)}) collective-permute-start(bf16[8,2,144,128]{3,2,1,0:T(8,128)(2,1)} %get-tuple-element.10), channel_id=1, source_target_pairs={{8,0},{16,8},{24,16},{32,24},{40,32},{48,40},{56,48},{72,64},{80,7... | collective-permute-start | bytes 1769480 | tf_op jit(solution)/shard_map/ppermute | solution.py:199
  115.3 8.2 %collective-permute-done.9.refs_10_ = bf16[8,2,144,128]{3,2,1,0:T(8,128)(2,1)} collective-permute-done((bf16[8,2,144,128]{3,2,1,0:T(8,128)(2,1)}, bf16[8,2,144,128]{3,2,1,0:T(8,128)(2,1)}, u32[]{:S(2)}, u32[]{:S(2)}) %collective-permute-start.9) | collective-permute-done | bytes 589856 | tf_op jit(solution)/shard_map/ppermute | solution.py:199
  123.5 1.9 %collective-permute-start.1 = (bf16[8,2,144,128]{3,2,1,0:T(8,128)(2,1)}, bf16[8,2,144,128]{3,2,1,0:T(8,128)(2,1)S(1)}, u32[]{:S(2)}, u32[]{:S(2)}) collective-permute-start(bf16[8,2,144,128]{3,2,1,0:T(8,128)(2,1)} %get-tuple-element.10), channel_id=1, source_target_pairs={{0,8},{8,16},{16,24},{24,32},{32,40},{40,48},{48,56},{64,72},{72,8... | collective-permute-start | bytes 1769480 | tf_op jit(solution)/shard_map/ppermute | solution.py:199
  126.6 8.4 %collective-permute-done.7.refs_8_ = bf16[8,2,144,128]{3,2,1,0:T(8,128)(2,1)S(1)} collective-permute-done((bf16[8,2,144,128]{3,2,1,0:T(8,128)(2,1)}, bf16[8,2,144,128]{3,2,1,0:T(8,128)(2,1)S(1)}, u32[]{:S(2)}, u32[]{:S(2)}) %collective-permute-start.7) | collective-permute-done | bytes 589856 | tf_op jit(solution)/shard_map/ppermute | solution.py:199
  135.1 0.9 copy-done.4
  137.0 18.3 %attend.1 = bf16[8,3,144,128]{3,2,1,0:T(8,128)(2,1)} custom-call(s32[3,5]{1,0:T(4,128)} %fusion.1.idx_ref, s32[3,5]{1,0:T(4,128)} %fusion.4.live_ref, bf16[8,7,144,128]{3,2,1,0:T(8,128)(2,1)} %copy-done, bf16[8,4,144,128]{3,2,1,0:T(8,128)(2,1)} %copy-done.1, bf16[8,2,144,128]{3,2,1,0:T(8,128)(2,1)} %copy-done.6, bf16[8,2,144,128]{3,2,1,0:T(8,128)(2,1)} %copy-done.5, ...), custom_call_target="tpu_custom_call" | custom-call | flops 3397386240 | bytes 10616832 | tf_op jit(solution)/shard_map/attend/pallas_call | solution.py:159
  155.3 22.5 %all_to_all.15.part = bf16[8,3,144,128]{3,2,1,0:T(8,128)(2,1)} all-to-all(bf16[8,3,144,128]{3,2,1,0:T(8,128)(2,1)} %attend.1), channel_id=1, replica_groups=mesh['seq'=32,'head'=8] {'head'}, dimensions={0} | all-to-all | bytes 1769472 | tf_op jit(solution)/shard_map/all_to_all | solution.py:202
  177.8 2.3 %unpack.1 = bf16[144,3072]{1,0:T(8,128)(2,1)} custom-call(bf16[8,3,144,128]{3,2,1,0:T(8,128)(2,1)} %all_to_all.15.part), custom_call_target="tpu_custom_call" | custom-call | bytes 1769472 | tf_op jit(solution)/shard_map/unpack/pallas_call | solution.py:71
  (24 shorter events, 4.0 us)
Async XLA Ops:
  2.6 45.5 %all-to-all-start.1 = ((bf16[8,4,144,128]{3,2,1,0:T(8,128)(2,1)}), bf16[8,4,144,128]{3,2,1,0:T(8,128)(2,1)S(1)}, u32[]{:S(2)}, u32[]{:S(2)}) async-start(bf16[8,4,144,128]{3,2,1,0:T(8,128)(2,1)} %pack.5), calls=%async_computation.1 | async-start | bytes 2359296 | tf_op jit(solution)/shard_map/all_to_all | solution.py:202
  11.5 32.3 %collective-permute-start = (bf16[8,2,144,128]{3,2,1,0:T(8,128)(2,1)}, bf16[8,2,144,128]{3,2,1,0:T(8,128)(2,1)S(1)}, u32[]{:S(2)}, u32[]{:S(2)}) collective-permute-start(bf16[8,2,144,128]{3,2,1,0:T(8,128)(2,1)} %pack.3), channel_id=1, source_target_pairs={{0,64},{8,72},{16,80},{24,88},{32,96},{40,104},{48,112},{56,120},{... | collective-permute-start | bytes 1769480 | tf_op jit(solution)/shard_map/ppermute | solution.py:199
  43.9 0.8 copy-start.2
  48.1 49.7 %copy-start.1 = (bf16[8,4,144,128]{3,2,1,0:T(8,128)(2,1)}, bf16[8,4,144,128]{3,2,1,0:T(8,128)(2,1)S(1)}, u32[]{:S(2)}) copy-start(bf16[8,4,144,128]{3,2,1,0:T(8,128)(2,1)S(1)} %all-to-all-done.1.refs_1_) | copy-start | bytes 3538948
  48.1 62.2 %all-to-all-start = ((bf16[8,7,144,128]{3,2,1,0:T(8,128)(2,1)}), bf16[8,7,144,128]{3,2,1,0:T(8,128)(2,1)S(1)}, u32[]{:S(2)}, u32[]{:S(2)}) async-start(bf16[8,7,144,128]{3,2,1,0:T(8,128)(2,1)} %pack.4), calls=%async_computation | async-start | bytes 4128768 | tf_op jit(solution)/shard_map/all_to_all | solution.py:202
  55.1 39.3 %collective-permute-start.5 = (bf16[8,2,144,128]{3,2,1,0:T(8,128)(2,1)S(1)}, bf16[8,2,144,128]{3,2,1,0:T(8,128)(2,1)}, u32[]{:S(2)}, u32[]{:S(2)}) collective-permute-start(bf16[8,2,144,128]{3,2,1,0:T(8,128)(2,1)S(1)} %get-tuple-element.7), channel_id=1, source_target_pairs={{0,64},{8,72},{16,80},{24,88},{32,96},{40,104},{48,112},{56,120},{... | collective-permute-start | bytes 1769480 | tf_op jit(solution)/shard_map/ppermute | solution.py:199
  60.8 64.7 %copy-start.3 = (s32[3,5]{1,0:T(4,128)S(1)}, s32[3,5]{1,0:T(4,128)}, u32[]{:S(2)}) copy-start(s32[3,5]{1,0:T(4,128)} %param.7) | copy-start | bytes 184
  60.8 46.2 %collective-permute-start.6 = (bf16[8,2,144,128]{3,2,1,0:T(8,128)(2,1)S(1)}, bf16[8,2,144,128]{3,2,1,0:T(8,128)(2,1)}, u32[]{:S(2)}, u32[]{:S(2)}) collective-permute-start(bf16[8,2,144,128]{3,2,1,0:T(8,128)(2,1)S(1)} %get-tuple-element.8), channel_id=1, source_target_pairs={{0,64},{8,72},{16,80},{24,88},{32,96},{40,104},{48,112},{56,120},{... | collective-permute-start | bytes 1769480 | tf_op jit(solution)/shard_map/ppermute | solution.py:199
  61.1 65.5 %collective-permute-start.4 = (bf16[8,4,144,128]{3,2,1,0:T(8,128)(2,1)S(1)}, bf16[8,4,144,128]{3,2,1,0:T(8,128)(2,1)}, u32[]{:S(2)}, u32[]{:S(2)}) collective-permute-start(bf16[8,4,144,128]{3,2,1,0:T(8,128)(2,1)S(1)} %all-to-all-done.1.refs_1_), channel_id=1, source_target_pairs={{8,0},{16,8},{24,16},{32,24},{40,32},{48,40},{56,48},{72,64},{80,7... | collective-permute-start | bytes 3538952 | tf_op jit(solution)/shard_map/ppermute | solution.py:199
  94.4 18.9 %collective-permute-start.8 = (bf16[8,2,144,128]{3,2,1,0:T(8,128)(2,1)}, bf16[8,2,144,128]{3,2,1,0:T(8,128)(2,1)}, u32[]{:S(2)}, u32[]{:S(2)}) collective-permute-start(bf16[8,2,144,128]{3,2,1,0:T(8,128)(2,1)} %collective-permute-done.5.refs_6_), channel_id=1, source_target_pairs={{0,128},{8,136},{16,144},{24,152},{32,160},{40,168},{48,176},{56,1... | collective-permute-start | bytes 1769480 | tf_op jit(solution)/shard_map/ppermute | solution.py:199
  97.7 28.9 %collective-permute-start.3 = (bf16[8,4,144,128]{3,2,1,0:T(8,128)(2,1)S(1)}, bf16[8,4,144,128]{3,2,1,0:T(8,128)(2,1)}, u32[]{:S(2)}, u32[]{:S(2)}) collective-permute-start(bf16[8,4,144,128]{3,2,1,0:T(8,128)(2,1)S(1)} %all-to-all-done.1.refs_1_), channel_id=1, source_target_pairs={{0,8},{8,16},{16,24},{24,32},{32,40},{40,48},{48,56},{64,72},{72,8... | collective-permute-start | bytes 3538952 | tf_op jit(solution)/shard_map/ppermute | solution.py:199
  107.0 16.5 %collective-permute-start.9 = (bf16[8,2,144,128]{3,2,1,0:T(8,128)(2,1)}, bf16[8,2,144,128]{3,2,1,0:T(8,128)(2,1)}, u32[]{:S(2)}, u32[]{:S(2)}) collective-permute-start(bf16[8,2,144,128]{3,2,1,0:T(8,128)(2,1)} %collective-permute-done.6.refs_7_), channel_id=1, source_target_pairs={{0,128},{8,136},{16,144},{24,152},{32,160},{40,168},{48,176},{56,1... | collective-permute-start | bytes 1769480 | tf_op jit(solution)/shard_map/ppermute | solution.py:199
  110.3 1.7 copy-start
  112.0 23.0 %collective-permute-start.7 = (bf16[8,2,144,128]{3,2,1,0:T(8,128)(2,1)}, bf16[8,2,144,128]{3,2,1,0:T(8,128)(2,1)S(1)}, u32[]{:S(2)}, u32[]{:S(2)}) collective-permute-start(bf16[8,2,144,128]{3,2,1,0:T(8,128)(2,1)} %get-tuple-element.9), channel_id=1, source_target_pairs={{0,128},{8,136},{16,144},{24,152},{32,160},{40,168},{48,176},{56,1... | collective-permute-start | bytes 1769480 | tf_op jit(solution)/shard_map/ppermute | solution.py:199
  113.3 21.7 %collective-permute-start.2 = (bf16[8,2,144,128]{3,2,1,0:T(8,128)(2,1)}, bf16[8,2,144,128]{3,2,1,0:T(8,128)(2,1)S(1)}, u32[]{:S(2)}, u32[]{:S(2)}) collective-permute-start(bf16[8,2,144,128]{3,2,1,0:T(8,128)(2,1)} %get-tuple-element.10), channel_id=1, source_target_pairs={{8,0},{16,8},{24,16},{32,24},{40,32},{48,40},{56,48},{72,64},{80,7... | collective-permute-start | bytes 1769480 | tf_op jit(solution)/shard_map/ppermute | solution.py:199
  123.5 11.5 %collective-permute-start.1 = (bf16[8,2,144,128]{3,2,1,0:T(8,128)(2,1)}, bf16[8,2,144,128]{3,2,1,0:T(8,128)(2,1)S(1)}, u32[]{:S(2)}, u32[]{:S(2)}) collective-permute-start(bf16[8,2,144,128]{3,2,1,0:T(8,128)(2,1)} %get-tuple-element.10), channel_id=1, source_target_pairs={{0,8},{8,16},{16,24},{24,32},{32,40},{40,48},{48,56},{64,72},{72,8... | collective-permute-start | bytes 1769480 | tf_op jit(solution)/shard_map/ppermute | solution.py:199
  135.0 0.9 copy-start.4
  135.0 1.1 copy-start.5
  136.1 0.8 copy-start.6

commit v5 on v4

v5 whole, which is shorter than its diff:
```python
import functools

import jax
import jax.numpy as jnp
from jax import lax
from jax.experimental import pallas as pl
from jax.experimental.pallas import tpu as pltpu
from jax.sharding import PartitionSpec as P


HD = 128
TFR = 4
PIECES = 1
SWAPPED = 2
SCALE2 = 1.4426950408889634 / HD**0.5


ANY = pl.BlockSpec(memory_space=pl.ANY)


def after(value, *first):
    return lax.optimization_barrier((value,) + first)[0]


def lane(g, head, local, swap):
    return pl.multiple_of(((g if swap is None else jnp.bitwise_xor(g, swap)) * local + head) * HD, HD)


def pack_kernel(picks, local, count, swap_ref, *refs):
    arrays, o_ref, sems = refs[:count], refs[count], refs[count + 1]
    copies = []
    for at, (array, head) in enumerate(picks):
        swap = swap_ref[0] if head == SWAPPED else None
        for g in range(o_ref.shape[0]):
            piece = arrays[array].at[:, pl.ds(lane(g, head, local, swap), HD)]
            copy = pltpu.make_async_copy(piece, o_ref.at[g, at], sems.at[at, g])
            copy.start()
            copies.append(copy)
    for copy in copies:
        copy.wait()


def pack(swap, arrays, picks, groups):
    rows, width = arrays[0].shape
    shape = (groups, len(picks), rows, HD)
    return pl.pallas_call(
        functools.partial(pack_kernel, picks, width // (groups * HD), len(arrays)),
        out_shape=jax.ShapeDtypeStruct(shape, arrays[0].dtype),
        grid_spec=pltpu.PrefetchScalarGridSpec(
            num_scalar_prefetch=1,
            grid=(1,),
            in_specs=[ANY] * len(arrays),
            out_specs=pl.BlockSpec(shape, lambda i, *_: (0, 0, 0, 0)),
            scratch_shapes=[pltpu.SemaphoreType.DMA((len(picks), groups))],
        ),
        cost_estimate=pl.CostEstimate(
            flops=0, bytes_accessed=4 * groups * len(picks) * rows * HD, transcendentals=0
        ),
        name="pack",
    )(swap, *arrays)


def unpack_kernel(swap_ref, part, o_ref, sems):
    groups, local = part.shape[:2]
    copies = []
    for head in range(local):
        swap = swap_ref[0] if head == SWAPPED else None
        for g in range(groups):
            copy = pltpu.make_async_copy(
                part.at[g, head], o_ref.at[:, pl.ds(lane(g, head, local, swap), HD)], sems.at[head, g]
            )
            copy.start()
            copies.append(copy)
    for copy in copies:
        copy.wait()


def unpack(swap, part):
    groups, local, rows, _ = part.shape
    return pl.pallas_call(
        unpack_kernel,
        out_shape=jax.ShapeDtypeStruct((rows, groups * local * HD), part.dtype),
        grid_spec=pltpu.PrefetchScalarGridSpec(
            num_scalar_prefetch=1,
            grid=(1,),
            in_specs=[pl.BlockSpec(part.shape, lambda i, *_: (0, 0, 0, 0))],
            out_specs=ANY,
            scratch_shapes=[pltpu.SemaphoreType.DMA((local, groups))],
        ),
        cost_estimate=pl.CostEstimate(
            flops=0, bytes_accessed=4 * groups * local * rows * HD, transcendentals=0
        ),
        name="unpack",
    )(swap, part)


def attend_kernel(tile, per_slab, plan, outs_at, count, idx_ref, live_ref, *refs):
    sources, refs = refs[:count], refs[count:]
    o_ref, held, q_held, o_held, s_held, sems, o_sems = refs[-7:]
    heads = len(plan)
    blocks, rows = sources[0].shape[0], sources[0].shape[2]
    slab = blocks * rows
    copies = []
    for h, taken in enumerate(plan):
        for at, parts in enumerate(taken):
            for n, (source, part) in enumerate(parts):
                into = q_held.at[h] if at == 0 else held.at[h, n, pl.ds((at - 1) * blocks, blocks)]
                copy = pltpu.make_async_copy(sources[source].at[:, part], into, sems.at[h, at, n])
                copy.start()
                copies.append((h, copy))
    flat = held.reshape(heads, 2, held.shape[2] * rows, HD)
    q_flat = q_held.reshape(heads, slab, HD)
    o_flat = o_held.reshape(heads, slab, HD)
    slots = idx_ref.shape[1]
    spans = tile // HD
    block = tile // PIECES

    begins = [[pl.multiple_of(idx_ref[t, j] * tile, 128) for j in range(slots)] for t in range(per_slab)]
    alive = [[live_ref[t, j] > 0 for j in range(slots)] for t in range(per_slab)]
    items = [(h, t, p) for h in range(heads) for t in range(per_slab) for p in range(PIECES)]

    def score(n, j, most):
        h, t, p = items[n]
        q = q_flat[h, pl.ds(t * tile + p * block, block), :]
        k = flat[h, 0, pl.ds(begins[t][j], tile), :]
        s = lax.dot_general(q, k, (((1,), (1,)), ((), ())), preferred_element_type=jnp.float32)
        s_held[n % 2, j] = s
        top = functools.reduce(jnp.maximum, [s[:, c * HD : (c + 1) * HD] for c in range(spans)])
        if j:
            top = jnp.where(alive[t][j], top, -jnp.inf)
        return top if most is None else jnp.maximum(most, top)

    def mix(n, j, top, total, mixed):
        h, t, _ = items[n]
        shift = jnp.where(alive[t][j], top, jnp.inf) if j else top
        expo = jnp.exp2(s_held[n % 2, j] * SCALE2 - shift)
        part = functools.reduce(jnp.add, [expo[:, c * HD : (c + 1) * HD] for c in range(spans)])
        v = flat[h, 1, pl.ds(begins[t][j], tile), :]
        pv = jnp.dot(expo.astype(jnp.bfloat16), v, preferred_element_type=jnp.float32)
        return (part, pv) if total is None else (total + part, mixed + pv)

    def arrive(head):
        for h, copy in copies:
            if h == head:
                copy.wait()

    arrive(0)
    most = None
    for j in range(slots):
        most = score(0, j, most)
    outs = []
    for n, (h, t, p) in enumerate(items):
        if n + 1 < len(items) and items[n + 1][0] != h:
            arrive(h + 1)
        top = jnp.max(most, axis=1, keepdims=True) * SCALE2
        most = total = mixed = None
        for j in range(slots):
            if n + 1 < len(items):
                most = score(n + 1, j, most)
            total, mixed = mix(n, j, top, total, mixed)
        total = jnp.sum(total, axis=1, keepdims=True)
        o_flat[h, pl.ds(t * tile + p * block, block), :] = (mixed / total).astype(o_flat.dtype)
        if t == per_slab - 1 and p == PIECES - 1:
            copy = pltpu.make_async_copy(o_held.at[h], o_ref.at[:, outs_at[h]], o_sems.at[h])
            copy.start()
            outs.append(copy)
    for copy in outs:
        copy.wait()


def attend(idx, live, sources, plan, outs_at, parts, into=None):
    per_slab, slots = idx.shape
    blocks, _, rows, _ = sources[0].shape
    slab = blocks * rows
    tile = slab // per_slab
    keys = slots * tile
    heads, columns = len(plan), len(plan[0]) - 1
    dtype = sources[0].dtype
    count = len(sources)
    held = [] if into is None else [into]
    return pl.pallas_call(
        functools.partial(attend_kernel, tile, per_slab, plan, outs_at, count),
        out_shape=jax.ShapeDtypeStruct((blocks, parts, rows, HD), dtype),
        grid_spec=pltpu.PrefetchScalarGridSpec(
            num_scalar_prefetch=2,
            grid=(1,),
            in_specs=[ANY] * (count + len(held)),
            out_specs=ANY,
            scratch_shapes=[
                pltpu.VMEM((heads, 2, columns * blocks, rows, HD), dtype),
                pltpu.VMEM((heads, blocks, rows, HD), dtype),
                pltpu.VMEM((heads, blocks, rows, HD), dtype),
                pltpu.VMEM((2, slots, tile // PIECES, tile), jnp.float32),
                pltpu.SemaphoreType.DMA((heads, columns + 1, 2)),
                pltpu.SemaphoreType.DMA((heads,)),
            ],
        ),
        input_output_aliases={2 + count: 0} if held else {},
        cost_estimate=pl.CostEstimate(
            flops=4 * heads * slab * keys * HD,
            bytes_accessed=4 * heads * slab * HD * (columns + 1),
            transcendentals=heads * slab * keys,
        ),
        name="attend",
    )(idx, live, *sources, *held)


def body(query, keys, values, windows):
    groups = lax.axis_size("head")
    peers = lax.axis_size("seq")
    columns = peers // TFR
    local = query.shape[1] // (groups * HD)
    per_slab = windows.shape[0]

    across = [(s, s ^ columns) for s in range(peers)]
    right = [(s, s + 1) for s in range(peers) if (s + 1) % columns]
    left = [(s, s - 1) for s in range(peers) if s % columns]
    middle = [(s, s + 2 * columns) for s in range(columns)] + [
        (s, s - 2 * columns) for s in range(3 * columns, peers)
    ]

    def send(x, pairs):
        return lax.ppermute(x, "seq", pairs)

    def exchange(x):
        return lax.all_to_all(x, "head", split_axis=0, concat_axis=0, tiled=True)

    here = lax.axis_index("seq")
    live = windows >= 0
    delta = windows // per_slab - here
    partner = jnp.where(here // columns % 2 == 0, columns, -columns)
    code = jnp.where(
        delta == 0,
        0,
        jnp.where(delta == -1, 1, jnp.where(delta == 1, 2, jnp.where(delta == partner, 3, 4))),
    )
    idx = jnp.where(live, code * per_slab + windows % per_slab, 0)
    live = live.astype(jnp.int32)

    swap = (here >= peers // 2).astype(jnp.int32).reshape(1)
    hop = [(s * groups + h, d * groups + (h ^ 1)) for s, d in middle for h in range(groups)]

    first = pack(swap, [keys, values], [(0, 0), (1, 0), (0, 1)], groups)
    crossed = send(first, across)
    rest = pack(swap, [keys, values], [(1, 1), (0, 2), (1, 2)], groups)
    rest = exchange(rest)
    most = pack(swap, [keys, values, query], [(2, 0), (2, 1), (2, 2), (0, 0), (1, 0), (0, 1)], groups)
    most = exchange(most)
    far = send(after(rest, crossed), across)
    crossed = exchange(crossed)
    before_a = send(rest, right)
    behind_a = send(rest, left)
    own = most[:, 3:6]
    before_b = send(own, right)
    behind_b = send(own, left)
    second_2 = lax.ppermute(far[:, 1:3], ("seq", "head"), hop)
    second_1 = send(far[:, 0:1], middle)
    second_b = send(crossed, middle)
    parts = local
    plan_2 = [[((0, 2),), ((1, 1), (1, 2)), ((2, 1), (2, 2)), ((3, 1), (3, 2)), ((4, 1), (4, 2)), ((5, 0), (5, 1))]]
    o = attend(idx, live, [most, rest, before_a, behind_a, far, second_2], plan_2, (2,), parts)
    sources = [most, rest, before_a, behind_a, far, second_1, before_b, behind_b, crossed, second_b]
    plan = [
        [((0, 0),), ((0, 3), (0, 4)), ((6, 0), (6, 1)), ((7, 0), (7, 1)), ((8, 0), (8, 1)), ((9, 0), (9, 1))],
        [((0, 1),), ((0, 5), (1, 0)), ((6, 2), (2, 0)), ((7, 2), (3, 0)), ((8, 2), (4, 0)), ((9, 2), (5, 0))],
    ]
    o = attend(idx, live, sources, plan, (0, 1), parts, o)
    o = exchange(o)
    return unpack(swap, o)


def solution(mesh):
    return jax.shard_map(
        body,
        mesh=mesh,
        in_specs=(
            P(("seq", "head"), None),
            P(("seq", "head"), None),
            P(("seq", "head"), None),
            P("seq", None),
        ),
        out_specs=P(("seq", "head"), None),
        check_vma=False,
    )
```

time: 181 us -> 182 us (level)
  starting transfers between devices: 41.9 us -> 55.2 us
  waiting for transfers between devices: 81.4 us -> 72.5 us
  blocking collectives: 22.5 us -> 19.5 us
    ppermute x10 -> x8, waiting for transfers between devices: 81.3 us -> 55.5 us  [send(): return lax.ppermute(x, 'seq', pairs)]
    all_to_all x2 -> x3, waiting for transfers between devices: 0.01 us -> 12.4 us  [exchange(): return lax.all_to_all(x, 'head', split_axis=0, concat_axis=0, tiled=True)]
    ppermute x0 -> x1, starting transfers between devices: none -> 6.03 us  [body(): second_2 = lax.ppermute(far[:, 1:3], ('seq', 'head'), hop)]
    ppermute x0 -> x1, waiting for transfers between devices: none -> 4.61 us  [body(): second_2 = lax.ppermute(far[:, 1:3], ('seq', 'head'), hop)]
    ppermute x10 -> x8, starting transfers between devices: 28 us -> 31.8 us  [send(): return lax.ppermute(x, 'seq', pairs)]
    all_to_all x2 -> x3, starting transfers between devices: 13.9 us -> 17.5 us  [exchange(): return lax.all_to_all(x, 'head', split_axis=0, concat_axis=0, tiled=True)]
    all_to_all x1, blocking collectives: 22.5 us -> 19.5 us  [exchange(): return lax.all_to_all(x, 'head', split_axis=0, concat_axis=0, tiled=True)]
    pallas_call x1 -> x2, Pallas kernels: 18.3 us -> 17.1 us  [attend(): pl.pallas_call(functools.partial(attend_kernel, tile, per_slab, plan, out...]
  transfers between devices with their start and end apart: 12 -> 12, of which waited for: 5 -> 6; matrix products, arithmetic and copies ran while one was open for 1% -> 2% of each run, Pallas kernels for 3% -> 7%
where the time goes in v5:
time: 182 us; the launch traced here: 180 us
  waiting for transfers between devices  72.5 us (40%)
  starting transfers between devices  55.2 us (30%)
  Pallas kernels  27.1 us (15%)
  blocking collectives  19.5 us (11%)
  local copies, waits for them, and re-layouts  4.54 us (2%)
    ppermute x8, waiting for transfers between devices, send(): return lax.ppermute(x, 'seq', pairs)  55.5 us
    ppermute x8, starting transfers between devices, send(): return lax.ppermute(x, 'seq', pairs)  31.8 us
    all_to_all x1, blocking collectives, exchange(): return lax.all_to_all(x, 'head', split_axis=0, concat_axis=0, tiled=True)  19.5 us
    all_to_all x3, starting transfers between devices, exchange(): return lax.all_to_all(x, 'head', split_axis=0, concat_axis=0, tiled=True)  17.5 us
    pallas_call x2, Pallas kernels, attend(): pl.pallas_call(functools.partial(attend_kernel, tile, per_slab, plan, out...  17.1 us
    all_to_all x3, waiting for transfers between devices, exchange(): return lax.all_to_all(x, 'head', split_axis=0, concat_axis=0, tiled=True)  12.4 us
    pallas_call x3, Pallas kernels, pack(): pl.pallas_call(functools.partial(pack_kernel, picks, width // (groups * H...  7.71 us
    ppermute x1, starting transfers between devices, body(): second_2 = lax.ppermute(far[:, 1:3], ('seq', 'head'), hop)  6.03 us
  transfers between devices with their start and end apart: 12, of which 6 were waited for; matrix products, arithmetic and copies ran while one was open for 2% of the time, Pallas kernels for 7%

profile of v5, /device:TPU:32, one launch (start us, length us, event | category | flops | bytes accessed | tf_op | source)
XLA Modules:
  0.0 180.3 jit_solution(10076403884492066526)
XLA Ops:
  0.0 2.3 %pack.4 = bf16[8,3,144,128]{3,2,1,0:T(8,128)(2,1)} custom-call(s32[1]{0:T(128)} %bitcast.swap_ref, bf16[144,3072]{1,0:T(8,128)(2,1)} %refs_0_.5, bf16[144,3072]{1,0:T(8,128)(2,1)} %refs_1_.5), custom_call_target="tpu_custom_call" | custom-call | bytes 1769472 | tf_op jit(solution)/shard_map/pack/pallas_call | solution.py:46
  2.3 6.9 %all-to-all-start.1 = ((bf16[8,3,144,128]{3,2,1,0:T(8,128)(2,1)}), bf16[8,3,144,128]{3,2,1,0:T(8,128)(2,1)S(1)}, u32[]{:S(2)}, u32[]{:S(2)}) async-start(bf16[8,3,144,128]{3,2,1,0:T(8,128)(2,1)} %pack.4), calls=%async_computation.1 | async-start | bytes 1769472 | tf_op jit(solution)/shard_map/all_to_all | solution.py:226
  9.2 3.1 %pack.3 = bf16[8,6,144,128]{3,2,1,0:T(8,128)(2,1)} custom-call(s32[1]{0:T(128)} %bitcast.swap_ref, bf16[144,3072]{1,0:T(8,128)(2,1)} %refs_0_.5, bf16[144,3072]{1,0:T(8,128)(2,1)} %refs_1_.5, bf16[144,3072]{1,0:T(8,128)(2,1)} %refs_2_.1), custom_call_target="tpu_custom_call" | custom-call | bytes 3538944 | tf_op jit(solution)/shard_map/pack/pallas_call | solution.py:46
  12.4 12.3 %all-to-all-done.1.refs_1_ = bf16[8,3,144,128]{3,2,1,0:T(8,128)(2,1)S(1)} async-done(((bf16[8,3,144,128]{3,2,1,0:T(8,128)(2,1)}), bf16[8,3,144,128]{3,2,1,0:T(8,128)(2,1)S(1)}, u32[]{:S(2)}, u32[]{:S(2)}) %all-to-all-start.1) | async-done | bytes 884768 | tf_op jit(solution)/shard_map/all_to_all | solution.py:226
  24.7 3.6 %all-to-all-start = ((bf16[8,6,144,128]{3,2,1,0:T(8,128)(2,1)}), bf16[8,6,144,128]{3,2,1,0:T(8,128)(2,1)S(1)}, u32[]{:S(2)}, u32[]{:S(2)}) async-start(bf16[8,6,144,128]{3,2,1,0:T(8,128)(2,1)} %pack.3), calls=%async_computation | async-start | bytes 3538944 | tf_op jit(solution)/shard_map/all_to_all | solution.py:226
  28.3 2.3 %pack.5 = bf16[8,3,144,128]{3,2,1,0:T(8,128)(2,1)} custom-call(s32[1]{0:T(128)} %bitcast.swap_ref, bf16[144,3072]{1,0:T(8,128)(2,1)} %refs_0_.5, bf16[144,3072]{1,0:T(8,128)(2,1)} %refs_1_.5), custom_call_target="tpu_custom_call" | custom-call | bytes 1769472 | tf_op jit(solution)/shard_map/pack/pallas_call | solution.py:46
  30.6 6.4 %collective-permute-start.2 = (bf16[8,3,144,128]{3,2,1,0:T(8,128)(2,1)}, bf16[8,3,144,128]{3,2,1,0:T(8,128)(2,1)}, u32[]{:S(2)}, u32[]{:S(2)}) collective-permute-start(bf16[8,3,144,128]{3,2,1,0:T(8,128)(2,1)} %pack.5), channel_id=1, source_target_pairs={{0,64},{8,72},{16,80},{24,88},{32,96},{40,104},{48,112},{56,120},{... | collective-permute-start | bytes 2654216 | tf_op jit(solution)/shard_map/ppermute | solution.py:223
  37.0 38.0 %collective-permute-done.2 = bf16[8,3,144,128]{3,2,1,0:T(8,128)(2,1)} collective-permute-done((bf16[8,3,144,128]{3,2,1,0:T(8,128)(2,1)}, bf16[8,3,144,128]{3,2,1,0:T(8,128)(2,1)}, u32[]{:S(2)}, u32[]{:S(2)}) %collective-permute-start.2) | collective-permute-done | bytes 884768 | tf_op jit(solution)/shard_map/ppermute | solution.py:223
  75.0 10.3 %collective-permute-start.3 = (bf16[8,3,144,128]{3,2,1,0:T(8,128)(2,1)S(1)}, bf16[8,3,144,128]{3,2,1,0:T(8,128)(2,1)S(1)}, u32[]{:S(2)}, u32[]{:S(2)}) collective-permute-start(bf16[8,3,144,128]{3,2,1,0:T(8,128)(2,1)S(1)} %all-to-all-done.1.refs_1_), channel_id=1, source_target_pairs={{0,64},{8,72},{16,80},{24,88},{32,96},{40,104},{48,112},{56,120},{... | collective-permute-start | bytes 2654216 | tf_op jit(solution)/shard_map/ppermute | solution.py:223
  85.3 6.9 %all-to-all-start.2 = ((bf16[8,3,144,128]{3,2,1,0:T(8,128)(2,1)}), bf16[8,3,144,128]{3,2,1,0:T(8,128)(2,1)}, u32[]{:S(2)}, u32[]{:S(2)}) async-start(bf16[8,3,144,128]{3,2,1,0:T(8,128)(2,1)} %collective-permute-done.2), calls=%async_computation.2 | async-start | bytes 1769472 | tf_op jit(solution)/shard_map/all_to_all | solution.py:226
  92.2 1.9 %collective-permute-start = (bf16[8,3,144,128]{3,2,1,0:T(8,128)(2,1)S(1)}, bf16[8,3,144,128]{3,2,1,0:T(8,128)(2,1)}, u32[]{:S(2)}, u32[]{:S(2)}) collective-permute-start(bf16[8,3,144,128]{3,2,1,0:T(8,128)(2,1)S(1)} %all-to-all-done.1.refs_1_), channel_id=1, source_target_pairs={{0,8},{8,16},{16,24},{24,32},{32,40},{40,48},{48,56},{64,72},{72,8... | collective-permute-start | bytes 2654216 | tf_op jit(solution)/shard_map/ppermute | solution.py:223
  94.1 3.6 %collective-permute-start.1 = (bf16[8,3,144,128]{3,2,1,0:T(8,128)(2,1)S(1)}, bf16[8,3,144,128]{3,2,1,0:T(8,128)(2,1)}, u32[]{:S(2)}, u32[]{:S(2)}) collective-permute-start(bf16[8,3,144,128]{3,2,1,0:T(8,128)(2,1)S(1)} %all-to-all-done.1.refs_1_), channel_id=1, source_target_pairs={{8,0},{16,8},{24,16},{32,24},{40,32},{48,40},{56,48},{72,64},{80,7... | collective-permute-start | bytes 2654216 | tf_op jit(solution)/shard_map/ppermute | solution.py:223
  98.8 1.9 %collective-permute-start.5 = (bf16[8,3,144,128]{3,2,1,0:T(8,128)(2,1)}, bf16[8,3,144,128]{3,2,1,0:T(8,128)(2,1)}, u32[]{:S(2)}, u32[]{:S(2)}) collective-permute-start(bf16[8,3,144,128]{3,2,1,0:T(8,128)(2,1)} %slice.13), channel_id=1, source_target_pairs={{0,8},{8,16},{16,24},{24,32},{32,40},{40,48},{48,56},{64,72},{72,8... | collective-permute-start | bytes 2654216 | tf_op jit(solution)/shard_map/ppermute | solution.py:223
  100.7 3.6 %collective-permute-start.6 = (bf16[8,3,144,128]{3,2,1,0:T(8,128)(2,1)}, bf16[8,3,144,128]{3,2,1,0:T(8,128)(2,1)S(1)}, u32[]{:S(2)}, u32[]{:S(2)}) collective-permute-start(bf16[8,3,144,128]{3,2,1,0:T(8,128)(2,1)} %slice.13), channel_id=1, source_target_pairs={{8,0},{16,8},{24,16},{32,24},{40,32},{48,40},{56,48},{72,64},{80,7... | collective-permute-start | bytes 2654216 | tf_op jit(solution)/shard_map/ppermute | solution.py:223
  104.4 12.3 %collective-permute-done.3.refs_4_ = bf16[8,3,144,128]{3,2,1,0:T(8,128)(2,1)S(1)} collective-permute-done((bf16[8,3,144,128]{3,2,1,0:T(8,128)(2,1)S(1)}, bf16[8,3,144,128]{3,2,1,0:T(8,128)(2,1)S(1)}, u32[]{:S(2)}, u32[]{:S(2)}) %collective-permute-start.3) | collective-permute-done | bytes 884768 | tf_op jit(solution)/shard_map/ppermute | solution.py:223
  116.7 2.5 %collective-permute-start.7 = (bf16[8,3,144,128]{3,2,1,0:T(8,128)(2,1)}, bf16[8,3,144,128]{3,2,1,0:T(8,128)(2,1)S(1)}, u32[]{:S(2)}, u32[]{:S(2)}) collective-permute-start(bf16[8,3,144,128]{3,2,1,0:T(8,128)(2,1)} %all-to-all-done.2.refs_8_), channel_id=1, source_target_pairs={{0,128},{8,136},{16,144},{24,152},{32,160},{40,168},{48,176},{56,1... | collective-permute-start | bytes 2654216 | tf_op jit(solution)/shard_map/ppermute | solution.py:223
  120.1 5.1 %collective-permute-done.refs_2_ = bf16[8,3,144,128]{3,2,1,0:T(8,128)(2,1)} collective-permute-done((bf16[8,3,144,128]{3,2,1,0:T(8,128)(2,1)S(1)}, bf16[8,3,144,128]{3,2,1,0:T(8,128)(2,1)}, u32[]{:S(2)}, u32[]{:S(2)}) %collective-permute-start) | collective-permute-done | bytes 884768 | tf_op jit(solution)/shard_map/ppermute | solution.py:223
  125.2 6.0 %collective-permute-start.8 = (bf16[8,2,144,128]{3,2,1,0:T(8,128)(2,1)}, bf16[8,2,144,128]{3,2,1,0:T(8,128)(2,1)}, u32[]{:S(2)}, u32[]{:S(2)}) collective-permute-start(bf16[8,2,144,128]{3,2,1,0:T(8,128)(2,1)} %slice.14), channel_id=1, source_target_pairs={{0,129},{1,128},{2,131},{3,130},{4,133},{5,132},{6,135},{7,134},{8... | collective-permute-start | bytes 1769480 | tf_op jit(solution)/shard_map/ppermute | solution.py:256
  132.6 1.5 collective-permute-start.4
  134.7 4.6 %collective-permute-done.8.refs_5_ = bf16[8,2,144,128]{3,2,1,0:T(8,128)(2,1)} collective-permute-done((bf16[8,2,144,128]{3,2,1,0:T(8,128)(2,1)}, bf16[8,2,144,128]{3,2,1,0:T(8,128)(2,1)}, u32[]{:S(2)}, u32[]{:S(2)}) %collective-permute-start.8) | collective-permute-done | bytes 589856 | tf_op jit(solution)/shard_map/ppermute | solution.py:256
  139.3 6.9 %attend.2.refs_10_ = bf16[8,3,144,128]{3,2,1,0:T(8,128)(2,1)} custom-call(s32[3,5]{1,0:T(4,128)} %fusion.1.idx_ref, s32[3,5]{1,0:T(4,128)} %fusion.4.live_ref, bf16[8,6,144,128]{3,2,1,0:T(8,128)(2,1)} %copy-done, bf16[8,3,144,128]{3,2,1,0:T(8,128)(2,1)} %copy-done.1, bf16[8,3,144,128]{3,2,1,0:T(8,128)(2,1)} %collective-permute-done.refs_2_, ...), custom_call_target="tpu_custom_call" | custom-call | flops 1132462080 | bytes 3538944 | tf_op jit(solution)/shard_map/attend/pallas_call | solution.py:181
  148.2 10.2 %attend.3 = bf16[8,3,144,128]{3,2,1,0:T(8,128)(2,1)} custom-call(s32[3,5]{1,0:T(4,128)} %fusion.1.idx_ref, s32[3,5]{1,0:T(4,128)} %fusion.4.live_ref, bf16[8,6,144,128]{3,2,1,0:T(8,128)(2,1)} %copy-done, bf16[8,3,144,128]{3,2,1,0:T(8,128)(2,1)} %copy-done.1, bf16[8,3,144,128]{3,2,1,0:T(8,128)(2,1)} %collective-permute-done.refs_2_, ...), custom_call_target="tpu_custom_call", output_to_operand_aliasing={{}: (12, {})} | custom-call | flops 2264924160 | bytes 7077888 | tf_op jit(solution)/shard_map/attend/pallas_call | solution.py:181
  158.4 19.5 %all_to_all.20.part = bf16[8,3,144,128]{3,2,1,0:T(8,128)(2,1)} all-to-all(bf16[8,3,144,128]{3,2,1,0:T(8,128)(2,1)} %attend.3), channel_id=1, replica_groups=mesh['seq'=32,'head'=8] {'head'}, dimensions={0} | all-to-all | bytes 1769472 | tf_op jit(solution)/shard_map/all_to_all | solution.py:226
  177.9 2.3 %unpack.1 = bf16[144,3072]{1,0:T(8,128)(2,1)} custom-call(s32[1]{0:T(128)} %bitcast.swap_ref, bf16[8,3,144,128]{3,2,1,0:T(8,128)(2,1)} %all_to_all.20.part), custom_call_target="tpu_custom_call" | custom-call | bytes 1769472 | tf_op jit(solution)/shard_map/unpack/pallas_call | solution.py:80
  (26 shorter events, 5.8 us)
Async XLA Ops:
  2.3 22.4 %all-to-all-start.1 = ((bf16[8,3,144,128]{3,2,1,0:T(8,128)(2,1)}), bf16[8,3,144,128]{3,2,1,0:T(8,128)(2,1)S(1)}, u32[]{:S(2)}, u32[]{:S(2)}) async-start(bf16[8,3,144,128]{3,2,1,0:T(8,128)(2,1)} %pack.4), calls=%async_computation.1 | async-start | bytes 1769472 | tf_op jit(solution)/shard_map/all_to_all | solution.py:226
  24.7 69.4 %copy-start.1 = (bf16[8,3,144,128]{3,2,1,0:T(8,128)(2,1)}, bf16[8,3,144,128]{3,2,1,0:T(8,128)(2,1)S(1)}, u32[]{:S(2)}) copy-start(bf16[8,3,144,128]{3,2,1,0:T(8,128)(2,1)S(1)} %all-to-all-done.1.refs_1_) | copy-start | bytes 2654212
  24.7 60.6 %all-to-all-start = ((bf16[8,6,144,128]{3,2,1,0:T(8,128)(2,1)}), bf16[8,6,144,128]{3,2,1,0:T(8,128)(2,1)S(1)}, u32[]{:S(2)}, u32[]{:S(2)}) async-start(bf16[8,6,144,128]{3,2,1,0:T(8,128)(2,1)} %pack.3), calls=%async_computation | async-start | bytes 3538944 | tf_op jit(solution)/shard_map/all_to_all | solution.py:226
  30.6 44.4 %collective-permute-start.2 = (bf16[8,3,144,128]{3,2,1,0:T(8,128)(2,1)}, bf16[8,3,144,128]{3,2,1,0:T(8,128)(2,1)}, u32[]{:S(2)}, u32[]{:S(2)}) collective-permute-start(bf16[8,3,144,128]{3,2,1,0:T(8,128)(2,1)} %pack.5), channel_id=1, source_target_pairs={{0,64},{8,72},{16,80},{24,88},{32,96},{40,104},{48,112},{56,120},{... | collective-permute-start | bytes 2654216 | tf_op jit(solution)/shard_map/ppermute | solution.py:223
  75.0 41.7 %collective-permute-start.3 = (bf16[8,3,144,128]{3,2,1,0:T(8,128)(2,1)S(1)}, bf16[8,3,144,128]{3,2,1,0:T(8,128)(2,1)S(1)}, u32[]{:S(2)}, u32[]{:S(2)}) collective-permute-start(bf16[8,3,144,128]{3,2,1,0:T(8,128)(2,1)S(1)} %all-to-all-done.1.refs_1_), channel_id=1, source_target_pairs={{0,64},{8,72},{16,80},{24,88},{32,96},{40,104},{48,112},{56,120},{... | collective-permute-start | bytes 2654216 | tf_op jit(solution)/shard_map/ppermute | solution.py:223
  85.3 13.5 %copy-start = (bf16[8,6,144,128]{3,2,1,0:T(8,128)(2,1)}, bf16[8,6,144,128]{3,2,1,0:T(8,128)(2,1)S(1)}, u32[]{:S(2)}) copy-start(bf16[8,6,144,128]{3,2,1,0:T(8,128)(2,1)S(1)} %all-to-all-done.refs_0_) | copy-start | bytes 5308420
  85.3 19.2 %all-to-all-start.2 = ((bf16[8,3,144,128]{3,2,1,0:T(8,128)(2,1)}), bf16[8,3,144,128]{3,2,1,0:T(8,128)(2,1)}, u32[]{:S(2)}, u32[]{:S(2)}) async-start(bf16[8,3,144,128]{3,2,1,0:T(8,128)(2,1)} %collective-permute-done.2), calls=%async_computation.2 | async-start | bytes 1769472 | tf_op jit(solution)/shard_map/all_to_all | solution.py:226
  92.2 39.1 %copy-start.6 = (s32[3,5]{1,0:T(4,128)S(1)}, s32[3,5]{1,0:T(4,128)}, u32[]{:S(2)}) copy-start(s32[3,5]{1,0:T(4,128)} %param.7) | copy-start | bytes 184
  92.2 33.0 %collective-permute-start = (bf16[8,3,144,128]{3,2,1,0:T(8,128)(2,1)S(1)}, bf16[8,3,144,128]{3,2,1,0:T(8,128)(2,1)}, u32[]{:S(2)}, u32[]{:S(2)}) collective-permute-start(bf16[8,3,144,128]{3,2,1,0:T(8,128)(2,1)S(1)} %all-to-all-done.1.refs_1_), channel_id=1, source_target_pairs={{0,8},{8,16},{16,24},{24,32},{32,40},{40,48},{48,56},{64,72},{72,8... | collective-permute-start | bytes 2654216 | tf_op jit(solution)/shard_map/ppermute | solution.py:223
  94.1 38.5 %collective-permute-start.1 = (bf16[8,3,144,128]{3,2,1,0:T(8,128)(2,1)S(1)}, bf16[8,3,144,128]{3,2,1,0:T(8,128)(2,1)}, u32[]{:S(2)}, u32[]{:S(2)}) collective-permute-start(bf16[8,3,144,128]{3,2,1,0:T(8,128)(2,1)S(1)} %all-to-all-done.1.refs_1_), channel_id=1, source_target_pairs={{8,0},{16,8},{24,16},{32,24},{40,32},{48,40},{56,48},{72,64},{80,7... | collective-permute-start | bytes 2654216 | tf_op jit(solution)/shard_map/ppermute | solution.py:223
  98.8 47.4 %collective-permute-start.5 = (bf16[8,3,144,128]{3,2,1,0:T(8,128)(2,1)}, bf16[8,3,144,128]{3,2,1,0:T(8,128)(2,1)}, u32[]{:S(2)}, u32[]{:S(2)}) collective-permute-start(bf16[8,3,144,128]{3,2,1,0:T(8,128)(2,1)} %slice.13), channel_id=1, source_target_pairs={{0,8},{8,16},{16,24},{24,32},{32,40},{40,48},{48,56},{64,72},{72,8... | collective-permute-start | bytes 2654216 | tf_op jit(solution)/shard_map/ppermute | solution.py:223
  100.7 45.5 %collective-permute-start.6 = (bf16[8,3,144,128]{3,2,1,0:T(8,128)(2,1)}, bf16[8,3,144,128]{3,2,1,0:T(8,128)(2,1)S(1)}, u32[]{:S(2)}, u32[]{:S(2)}) collective-permute-start(bf16[8,3,144,128]{3,2,1,0:T(8,128)(2,1)} %slice.13), channel_id=1, source_target_pairs={{8,0},{16,8},{24,16},{32,24},{40,32},{48,40},{56,48},{72,64},{80,7... | collective-permute-start | bytes 2654216 | tf_op jit(solution)/shard_map/ppermute | solution.py:223
  116.7 22.6 %copy-start.2 = (bf16[8,3,144,128]{3,2,1,0:T(8,128)(2,1)}, bf16[8,3,144,128]{3,2,1,0:T(8,128)(2,1)S(1)}, u32[]{:S(2)}) copy-start(bf16[8,3,144,128]{3,2,1,0:T(8,128)(2,1)S(1)} %collective-permute-done.3.refs_4_) | copy-start | bytes 2654212
  116.7 29.5 %collective-permute-start.7 = (bf16[8,3,144,128]{3,2,1,0:T(8,128)(2,1)}, bf16[8,3,144,128]{3,2,1,0:T(8,128)(2,1)S(1)}, u32[]{:S(2)}, u32[]{:S(2)}) collective-permute-start(bf16[8,3,144,128]{3,2,1,0:T(8,128)(2,1)} %all-to-all-done.2.refs_8_), channel_id=1, source_target_pairs={{0,128},{8,136},{16,144},{24,152},{32,160},{40,168},{48,176},{56,1... | collective-permute-start | bytes 2654216 | tf_op jit(solution)/shard_map/ppermute | solution.py:223
  125.2 14.1 %collective-permute-start.8 = (bf16[8,2,144,128]{3,2,1,0:T(8,128)(2,1)}, bf16[8,2,144,128]{3,2,1,0:T(8,128)(2,1)}, u32[]{:S(2)}, u32[]{:S(2)}) collective-permute-start(bf16[8,2,144,128]{3,2,1,0:T(8,128)(2,1)} %slice.14), channel_id=1, source_target_pairs={{0,129},{1,128},{2,131},{3,130},{4,133},{5,132},{6,135},{7,134},{8... | collective-permute-start | bytes 1769480 | tf_op jit(solution)/shard_map/ppermute | solution.py:256
  132.6 13.6 %collective-permute-start.4 = (bf16[8,1,144,128]{3,2,1,0:T(8,128)(2,1)}, bf16[8,1,144,128]{3,2,1,0:T(8,128)(2,1)S(1)}, u32[]{:S(2)}, u32[]{:S(2)}) collective-permute-start(bf16[8,1,144,128]{3,2,1,0:T(8,128)(2,1)} %slice.12), channel_id=1, source_target_pairs={{0,128},{8,136},{16,144},{24,152},{32,160},{40,168},{48,176},{56,1... | collective-permute-start | bytes 884744 | tf_op jit(solution)/shard_map/ppermute | solution.py:223
  146.2 0.7 copy-start.5
  146.2 1.0 copy-start.3
  147.2 1.0 copy-start.4

commit v6 on v5

--- a/solution.py
+++ b/solution.py
@@ -257,14 +257,14 @@
     second_1 = send(far[:, 0:1], middle)
     second_b = send(crossed, middle)
     parts = local
-    plan_2 = [[((0, 2),), ((1, 1), (1, 2)), ((2, 1), (2, 2)), ((3, 1), (3, 2)), ((4, 1), (4, 2)), ((5, 0), (5, 1))]]
-    o = attend(idx, live, [most, rest, before_a, behind_a, far, second_2], plan_2, (2,), parts)
-    sources = [most, rest, before_a, behind_a, far, second_1, before_b, behind_b, crossed, second_b]
+    plan_0 = [[((0, 0),), ((0, 3), (0, 4)), ((1, 0), (1, 1)), ((2, 0), (2, 1)), ((3, 0), (3, 1)), ((4, 0), (4, 1))]]
+    o = attend(idx, live, [most, before_b, behind_b, crossed, second_b], plan_0, (0,), parts)
+    sources = [most, rest, before_a, behind_a, far, second_1, before_b, behind_b, crossed, second_b, second_2]
     plan = [
-        [((0, 0),), ((0, 3), (0, 4)), ((6, 0), (6, 1)), ((7, 0), (7, 1)), ((8, 0), (8, 1)), ((9, 0), (9, 1))],
         [((0, 1),), ((0, 5), (1, 0)), ((6, 2), (2, 0)), ((7, 2), (3, 0)), ((8, 2), (4, 0)), ((9, 2), (5, 0))],
+        [((0, 2),), ((1, 1), (1, 2)), ((2, 1), (2, 2)), ((3, 1), (3, 2)), ((4, 1), (4, 2)), ((10, 0), (10, 1))],
     ]
-    o = attend(idx, live, sources, plan, (0, 1), parts, o)
+    o = attend(idx, live, sources, plan, (1, 2), parts, o)
     o = exchange(o)
     return unpack(swap, o)
 

time: 182 us -> 177 us (0.973)
  waiting for transfers between devices: 72.5 us -> 66.6 us
  starting transfers between devices: 55.2 us -> 52.4 us
    ppermute x8, waiting for transfers between devices: 55.5 us -> 47 us  [send(): return lax.ppermute(x, 'seq', pairs)]
    all_to_all x3, waiting for transfers between devices: 12.4 us -> 19.1 us  [exchange(): return lax.all_to_all(x, 'head', split_axis=0, concat_axis=0, tiled=True)]
    ppermute x1, waiting for transfers between devices: 4.61 us -> 0.49 us  [body(): second_2 = lax.ppermute(far[:, 1:3], ('seq', 'head'), hop)]
    ppermute x8, starting transfers between devices: 31.8 us -> 29.3 us  [send(): return lax.ppermute(x, 'seq', pairs)]
  transfers between devices with their start and end apart: 12 -> 12, of which waited for: 6 -> 6; matrix products, arithmetic and copies ran while one was open for 2% -> 3% of each run, Pallas kernels for 7% -> 7%
where the time goes in v6:
time: 177 us; the launch traced here: 174 us
  waiting for transfers between devices  66.6 us (38%)
  starting transfers between devices  52.4 us (30%)
  Pallas kernels  27.1 us (15%)
  blocking collectives  20.5 us (12%)
  local copies, waits for them, and re-layouts  5.56 us (3%)
    ppermute x8, waiting for transfers between devices, send(): return lax.ppermute(x, 'seq', pairs)  47 us
    ppermute x8, starting transfers between devices, send(): return lax.ppermute(x, 'seq', pairs)  29.3 us
    all_to_all x1, blocking collectives, exchange(): return lax.all_to_all(x, 'head', split_axis=0, concat_axis=0, tiled=True)  20.5 us
    all_to_all x3, waiting for transfers between devices, exchange(): return lax.all_to_all(x, 'head', split_axis=0, concat_axis=0, tiled=True)  19.1 us
    all_to_all x3, starting transfers between devices, exchange(): return lax.all_to_all(x, 'head', split_axis=0, concat_axis=0, tiled=True)  17.4 us
    pallas_call x2, Pallas kernels, attend(): pl.pallas_call(functools.partial(attend_kernel, tile, per_slab, plan, out...  17.1 us
    pallas_call x3, Pallas kernels, pack(): pl.pallas_call(functools.partial(pack_kernel, picks, width // (groups * H...  7.71 us
    ppermute x1, starting transfers between devices, body(): second_2 = lax.ppermute(far[:, 1:3], ('seq', 'head'), hop)  5.72 us
  transfers between devices with their start and end apart: 12, of which 6 were waited for; matrix products, arithmetic and copies ran while one was open for 3% of the time, Pallas kernels for 7%

profile of v6, /device:TPU:32, one launch (start us, length us, event | category | flops | bytes accessed | tf_op | source)
XLA Modules:
  0.0 173.5 jit_solution(7847640794181187918)
XLA Ops:
  0.0 2.3 %pack.4 = bf16[8,3,144,128]{3,2,1,0:T(8,128)(2,1)} custom-call(s32[1]{0:T(128)} %bitcast.swap_ref, bf16[144,3072]{1,0:T(8,128)(2,1)} %refs_0_.5, bf16[144,3072]{1,0:T(8,128)(2,1)} %refs_1_.5), custom_call_target="tpu_custom_call" | custom-call | bytes 1769472 | tf_op jit(solution)/shard_map/pack/pallas_call | solution.py:46
  2.3 6.9 %all-to-all-start.1 = ((bf16[8,3,144,128]{3,2,1,0:T(8,128)(2,1)}), bf16[8,3,144,128]{3,2,1,0:T(8,128)(2,1)S(1)}, u32[]{:S(2)}, u32[]{:S(2)}) async-start(bf16[8,3,144,128]{3,2,1,0:T(8,128)(2,1)} %pack.4), calls=%async_computation.1 | async-start | bytes 1769472 | tf_op jit(solution)/shard_map/all_to_all | solution.py:226
  9.2 3.1 %pack.3 = bf16[8,6,144,128]{3,2,1,0:T(8,128)(2,1)} custom-call(s32[1]{0:T(128)} %bitcast.swap_ref, bf16[144,3072]{1,0:T(8,128)(2,1)} %refs_0_.5, bf16[144,3072]{1,0:T(8,128)(2,1)} %refs_1_.5, bf16[144,3072]{1,0:T(8,128)(2,1)} %refs_2_.1), custom_call_target="tpu_custom_call" | custom-call | bytes 3538944 | tf_op jit(solution)/shard_map/pack/pallas_call | solution.py:46
  12.4 12.3 %all-to-all-done.1.refs_1_ = bf16[8,3,144,128]{3,2,1,0:T(8,128)(2,1)S(1)} async-done(((bf16[8,3,144,128]{3,2,1,0:T(8,128)(2,1)}), bf16[8,3,144,128]{3,2,1,0:T(8,128)(2,1)S(1)}, u32[]{:S(2)}, u32[]{:S(2)}) %all-to-all-start.1) | async-done | bytes 884768 | tf_op jit(solution)/shard_map/all_to_all | solution.py:226
  24.7 3.6 %all-to-all-start = ((bf16[8,6,144,128]{3,2,1,0:T(8,128)(2,1)}), bf16[8,6,144,128]{3,2,1,0:T(8,128)(2,1)S(1)}, u32[]{:S(2)}, u32[]{:S(2)}) async-start(bf16[8,6,144,128]{3,2,1,0:T(8,128)(2,1)} %pack.3), calls=%async_computation | async-start | bytes 3538944 | tf_op jit(solution)/shard_map/all_to_all | solution.py:226
  28.3 2.3 %pack.5 = bf16[8,3,144,128]{3,2,1,0:T(8,128)(2,1)} custom-call(s32[1]{0:T(128)} %bitcast.swap_ref, bf16[144,3072]{1,0:T(8,128)(2,1)} %refs_0_.5, bf16[144,3072]{1,0:T(8,128)(2,1)} %refs_1_.5), custom_call_target="tpu_custom_call" | custom-call | bytes 1769472 | tf_op jit(solution)/shard_map/pack/pallas_call | solution.py:46
  30.6 6.4 %collective-permute-start.2 = (bf16[8,3,144,128]{3,2,1,0:T(8,128)(2,1)}, bf16[8,3,144,128]{3,2,1,0:T(8,128)(2,1)S(1)}, u32[]{:S(2)}, u32[]{:S(2)}) collective-permute-start(bf16[8,3,144,128]{3,2,1,0:T(8,128)(2,1)} %pack.5), channel_id=1, source_target_pairs={{0,64},{8,72},{16,80},{24,88},{32,96},{40,104},{48,112},{56,120},{... | collective-permute-start | bytes 2654216 | tf_op jit(solution)/shard_map/ppermute | solution.py:223
  37.0 37.9 %collective-permute-done.2 = bf16[8,3,144,128]{3,2,1,0:T(8,128)(2,1)S(1)} collective-permute-done((bf16[8,3,144,128]{3,2,1,0:T(8,128)(2,1)}, bf16[8,3,144,128]{3,2,1,0:T(8,128)(2,1)S(1)}, u32[]{:S(2)}, u32[]{:S(2)}) %collective-permute-start.2) | collective-permute-done | bytes 884768 | tf_op jit(solution)/shard_map/ppermute | solution.py:223
  74.9 10.2 %collective-permute-start.3 = (bf16[8,3,144,128]{3,2,1,0:T(8,128)(2,1)S(1)}, bf16[8,3,144,128]{3,2,1,0:T(8,128)(2,1)}, u32[]{:S(2)}, u32[]{:S(2)}) collective-permute-start(bf16[8,3,144,128]{3,2,1,0:T(8,128)(2,1)S(1)} %all-to-all-done.1.refs_1_), channel_id=1, source_target_pairs={{0,64},{8,72},{16,80},{24,88},{32,96},{40,104},{48,112},{56,120},{... | collective-permute-start | bytes 2654216 | tf_op jit(solution)/shard_map/ppermute | solution.py:223
  85.1 6.9 %all-to-all-start.2 = ((bf16[8,3,144,128]{3,2,1,0:T(8,128)(2,1)}), bf16[8,3,144,128]{3,2,1,0:T(8,128)(2,1)S(1)}, u32[]{:S(2)}, u32[]{:S(2)}) async-start(bf16[8,3,144,128]{3,2,1,0:T(8,128)(2,1)} %copy-done.5), calls=%async_computation.2 | async-start | bytes 1769472 | tf_op jit(solution)/shard_map/all_to_all | solution.py:226
  93.0 1.9 %collective-permute-start.6 = (bf16[8,3,144,128]{3,2,1,0:T(8,128)(2,1)}, bf16[8,3,144,128]{3,2,1,0:T(8,128)(2,1)}, u32[]{:S(2)}, u32[]{:S(2)}) collective-permute-start(bf16[8,3,144,128]{3,2,1,0:T(8,128)(2,1)} %slice.13), channel_id=1, source_target_pairs={{8,0},{16,8},{24,16},{32,24},{40,32},{48,40},{56,48},{72,64},{80,7... | collective-permute-start | bytes 2654216 | tf_op jit(solution)/shard_map/ppermute | solution.py:223
  94.9 2.4 %collective-permute-start.5 = (bf16[8,3,144,128]{3,2,1,0:T(8,128)(2,1)}, bf16[8,3,144,128]{3,2,1,0:T(8,128)(2,1)S(1)}, u32[]{:S(2)}, u32[]{:S(2)}) collective-permute-start(bf16[8,3,144,128]{3,2,1,0:T(8,128)(2,1)} %slice.13), channel_id=1, source_target_pairs={{0,8},{8,16},{16,24},{24,32},{32,40},{40,48},{48,56},{64,72},{72,8... | collective-permute-start | bytes 2654216 | tf_op jit(solution)/shard_map/ppermute | solution.py:223
  97.3 6.8 %all-to-all-done.2.refs_3_.refs_8_ = bf16[8,3,144,128]{3,2,1,0:T(8,128)(2,1)S(1)} async-done(((bf16[8,3,144,128]{3,2,1,0:T(8,128)(2,1)}), bf16[8,3,144,128]{3,2,1,0:T(8,128)(2,1)S(1)}, u32[]{:S(2)}, u32[]{:S(2)}) %all-to-all-start.2) | async-done | bytes 884768 | tf_op jit(solution)/shard_map/all_to_all | solution.py:226
  104.1 2.5 %collective-permute-start.7 = (bf16[8,3,144,128]{3,2,1,0:T(8,128)(2,1)S(1)}, bf16[8,3,144,128]{3,2,1,0:T(8,128)(2,1)S(1)}, u32[]{:S(2)}, u32[]{:S(2)}) collective-permute-start(bf16[8,3,144,128]{3,2,1,0:T(8,128)(2,1)S(1)} %all-to-all-done.2.refs_3_.refs_8_), channel_id=1, source_target_pairs={{0,128},{8,136},{16,144},{24,152},{32,160},{40,168},{48,176},{56,1... | collective-permute-start | bytes 2654216 | tf_op jit(solution)/shard_map/ppermute | solution.py:223
  106.7 1.9 %collective-permute-start.1 = (bf16[8,3,144,128]{3,2,1,0:T(8,128)(2,1)S(1)}, bf16[8,3,144,128]{3,2,1,0:T(8,128)(2,1)}, u32[]{:S(2)}, u32[]{:S(2)}) collective-permute-start(bf16[8,3,144,128]{3,2,1,0:T(8,128)(2,1)S(1)} %all-to-all-done.1.refs_1_), channel_id=1, source_target_pairs={{8,0},{16,8},{24,16},{32,24},{40,32},{48,40},{56,48},{72,64},{80,7... | collective-permute-start | bytes 2654216 | tf_op jit(solution)/shard_map/ppermute | solution.py:223
  108.6 8.0 %collective-permute-done.3.refs_4_ = bf16[8,3,144,128]{3,2,1,0:T(8,128)(2,1)} collective-permute-done((bf16[8,3,144,128]{3,2,1,0:T(8,128)(2,1)S(1)}, bf16[8,3,144,128]{3,2,1,0:T(8,128)(2,1)}, u32[]{:S(2)}, u32[]{:S(2)}) %collective-permute-start.3) | collective-permute-done | bytes 884768 | tf_op jit(solution)/shard_map/ppermute | solution.py:223
  116.6 1.9 %collective-permute-start = (bf16[8,3,144,128]{3,2,1,0:T(8,128)(2,1)S(1)}, bf16[8,3,144,128]{3,2,1,0:T(8,128)(2,1)}, u32[]{:S(2)}, u32[]{:S(2)}) collective-permute-start(bf16[8,3,144,128]{3,2,1,0:T(8,128)(2,1)S(1)} %all-to-all-done.1.refs_1_), channel_id=1, source_target_pairs={{0,8},{8,16},{16,24},{24,32},{32,40},{40,48},{48,56},{64,72},{72,8... | collective-permute-start | bytes 2654216 | tf_op jit(solution)/shard_map/ppermute | solution.py:223
  118.6 1.9 %slice.14 = bf16[8,2,144,128]{3,2,1,0:T(8,128)(2,1)} slice(bf16[8,3,144,128]{3,2,1,0:T(8,128)(2,1)} %collective-permute-done.3.refs_4_), slice={[0:8], [1:3], [0:144], [0:128]} | slice | bytes 1179648 | tf_op jit(solution)/shard_map/slice | solution.py:256
  121.5 5.7 %collective-permute-start.8 = (bf16[8,2,144,128]{3,2,1,0:T(8,128)(2,1)}, bf16[8,2,144,128]{3,2,1,0:T(8,128)(2,1)}, u32[]{:S(2)}, u32[]{:S(2)}) collective-permute-start(bf16[8,2,144,128]{3,2,1,0:T(8,128)(2,1)} %slice.14), channel_id=1, source_target_pairs={{0,129},{1,128},{2,131},{3,130},{4,133},{5,132},{6,135},{7,134},{8... | collective-permute-start | bytes 1769480 | tf_op jit(solution)/shard_map/ppermute | solution.py:256
  129.5 2.0 %collective-permute-start.4 = (bf16[8,1,144,128]{3,2,1,0:T(8,128)(2,1)}, bf16[8,1,144,128]{3,2,1,0:T(8,128)(2,1)}, u32[]{:S(2)}, u32[]{:S(2)}) collective-permute-start(bf16[8,1,144,128]{3,2,1,0:T(8,128)(2,1)} %slice.12), channel_id=1, source_target_pairs={{0,128},{8,136},{16,144},{24,152},{32,160},{40,168},{48,176},{56,1... | collective-permute-start | bytes 884744 | tf_op jit(solution)/shard_map/ppermute | solution.py:223
  133.0 6.9 %attend.2.refs_11_ = bf16[8,3,144,128]{3,2,1,0:T(8,128)(2,1)} custom-call(s32[3,5]{1,0:T(4,128)} %fusion.1.idx_ref, s32[3,5]{1,0:T(4,128)} %fusion.4.live_ref, bf16[8,6,144,128]{3,2,1,0:T(8,128)(2,1)} %copy-done, bf16[8,3,144,128]{3,2,1,0:T(8,128)(2,1)} %copy-done.3, bf16[8,3,144,128]{3,2,1,0:T(8,128)(2,1)} %collective-permute-done.6.refs_2_.refs_7_, ...), custom_call_target="tpu_custom_call" | custom-call | flops 1132462080 | bytes 3538944 | tf_op jit(solution)/shard_map/attend/pallas_call | solution.py:181
  140.4 10.2 %attend.3 = bf16[8,3,144,128]{3,2,1,0:T(8,128)(2,1)} custom-call(s32[3,5]{1,0:T(4,128)} %fusion.1.idx_ref, s32[3,5]{1,0:T(4,128)} %fusion.4.live_ref, bf16[8,6,144,128]{3,2,1,0:T(8,128)(2,1)} %copy-done, bf16[8,3,144,128]{3,2,1,0:T(8,128)(2,1)} %copy-done.2, bf16[8,3,144,128]{3,2,1,0:T(8,128)(2,1)} %collective-permute-done.refs_2_, ...), custom_call_target="tpu_custom_call", output_to_operand_aliasing={{}: (13, {})} | custom-call | flops 2264924160 | bytes 7077888 | tf_op jit(solution)/shard_map/attend/pallas_call | solution.py:181
  150.6 20.5 %all_to_all.20.part = bf16[8,3,144,128]{3,2,1,0:T(8,128)(2,1)} all-to-all(bf16[8,3,144,128]{3,2,1,0:T(8,128)(2,1)} %attend.3), channel_id=1, replica_groups=mesh['seq'=32,'head'=8] {'head'}, dimensions={0} | all-to-all | bytes 1769472 | tf_op jit(solution)/shard_map/all_to_all | solution.py:226
  171.1 2.3 %unpack.1 = bf16[144,3072]{1,0:T(8,128)(2,1)} custom-call(s32[1]{0:T(128)} %bitcast.swap_ref, bf16[8,3,144,128]{3,2,1,0:T(8,128)(2,1)} %all_to_all.20.part), custom_call_target="tpu_custom_call" | custom-call | bytes 1769472 | tf_op jit(solution)/shard_map/unpack/pallas_call | solution.py:80
  (26 shorter events, 6.3 us)
Async XLA Ops:
  2.3 22.4 %all-to-all-start.1 = ((bf16[8,3,144,128]{3,2,1,0:T(8,128)(2,1)}), bf16[8,3,144,128]{3,2,1,0:T(8,128)(2,1)S(1)}, u32[]{:S(2)}, u32[]{:S(2)}) async-start(bf16[8,3,144,128]{3,2,1,0:T(8,128)(2,1)} %pack.4), calls=%async_computation.1 | async-start | bytes 1769472 | tf_op jit(solution)/shard_map/all_to_all | solution.py:226
  24.7 92.0 %copy-start.2 = (bf16[8,3,144,128]{3,2,1,0:T(8,128)(2,1)}, bf16[8,3,144,128]{3,2,1,0:T(8,128)(2,1)S(1)}, u32[]{:S(2)}) copy-start(bf16[8,3,144,128]{3,2,1,0:T(8,128)(2,1)S(1)} %all-to-all-done.1.refs_1_) | copy-start | bytes 2654212
  24.7 60.5 %all-to-all-start = ((bf16[8,6,144,128]{3,2,1,0:T(8,128)(2,1)}), bf16[8,6,144,128]{3,2,1,0:T(8,128)(2,1)S(1)}, u32[]{:S(2)}, u32[]{:S(2)}) async-start(bf16[8,6,144,128]{3,2,1,0:T(8,128)(2,1)} %pack.3), calls=%async_computation | async-start | bytes 3538944 | tf_op jit(solution)/shard_map/all_to_all | solution.py:226
  30.6 44.3 %collective-permute-start.2 = (bf16[8,3,144,128]{3,2,1,0:T(8,128)(2,1)}, bf16[8,3,144,128]{3,2,1,0:T(8,128)(2,1)S(1)}, u32[]{:S(2)}, u32[]{:S(2)}) collective-permute-start(bf16[8,3,144,128]{3,2,1,0:T(8,128)(2,1)} %pack.5), channel_id=1, source_target_pairs={{0,64},{8,72},{16,80},{24,88},{32,96},{40,104},{48,112},{56,120},{... | collective-permute-start | bytes 2654216 | tf_op jit(solution)/shard_map/ppermute | solution.py:223
  74.9 10.2 %copy-start.5 = (bf16[8,3,144,128]{3,2,1,0:T(8,128)(2,1)}, bf16[8,3,144,128]{3,2,1,0:T(8,128)(2,1)S(1)}, u32[]{:S(2)}) copy-start(bf16[8,3,144,128]{3,2,1,0:T(8,128)(2,1)S(1)} %collective-permute-done.2) | copy-start | bytes 2654212
  74.9 41.7 %collective-permute-start.3 = (bf16[8,3,144,128]{3,2,1,0:T(8,128)(2,1)S(1)}, bf16[8,3,144,128]{3,2,1,0:T(8,128)(2,1)}, u32[]{:S(2)}, u32[]{:S(2)}) collective-permute-start(bf16[8,3,144,128]{3,2,1,0:T(8,128)(2,1)S(1)} %all-to-all-done.1.refs_1_), channel_id=1, source_target_pairs={{0,64},{8,72},{16,80},{24,88},{32,96},{40,104},{48,112},{56,120},{... | collective-permute-start | bytes 2654216 | tf_op jit(solution)/shard_map/ppermute | solution.py:223
  85.1 7.9 %copy-start = (bf16[8,6,144,128]{3,2,1,0:T(8,128)(2,1)}, bf16[8,6,144,128]{3,2,1,0:T(8,128)(2,1)S(1)}, u32[]{:S(2)}) copy-start(bf16[8,6,144,128]{3,2,1,0:T(8,128)(2,1)S(1)} %all-to-all-done.refs_0_) | copy-start | bytes 5308420
  85.1 19.0 %all-to-all-start.2 = ((bf16[8,3,144,128]{3,2,1,0:T(8,128)(2,1)}), bf16[8,3,144,128]{3,2,1,0:T(8,128)(2,1)S(1)}, u32[]{:S(2)}, u32[]{:S(2)}) async-start(bf16[8,3,144,128]{3,2,1,0:T(8,128)(2,1)} %copy-done.5), calls=%async_computation.2 | async-start | bytes 1769472 | tf_op jit(solution)/shard_map/all_to_all | solution.py:226
  92.0 35.2 %copy-start.6 = (s32[3,5]{1,0:T(4,128)S(1)}, s32[3,5]{1,0:T(4,128)}, u32[]{:S(2)}) copy-start(s32[3,5]{1,0:T(4,128)} %param.7) | copy-start | bytes 184
  93.0 28.5 %collective-permute-start.6 = (bf16[8,3,144,128]{3,2,1,0:T(8,128)(2,1)}, bf16[8,3,144,128]{3,2,1,0:T(8,128)(2,1)}, u32[]{:S(2)}, u32[]{:S(2)}) collective-permute-start(bf16[8,3,144,128]{3,2,1,0:T(8,128)(2,1)} %slice.13), channel_id=1, source_target_pairs={{8,0},{16,8},{24,16},{32,24},{40,32},{48,40},{56,48},{72,64},{80,7... | collective-permute-start | bytes 2654216 | tf_op jit(solution)/shard_map/ppermute | solution.py:223
  94.9 34.6 %collective-permute-start.5 = (bf16[8,3,144,128]{3,2,1,0:T(8,128)(2,1)}, bf16[8,3,144,128]{3,2,1,0:T(8,128)(2,1)S(1)}, u32[]{:S(2)}, u32[]{:S(2)}) collective-permute-start(bf16[8,3,144,128]{3,2,1,0:T(8,128)(2,1)} %slice.13), channel_id=1, source_target_pairs={{0,8},{8,16},{16,24},{24,32},{32,40},{40,48},{48,56},{64,72},{72,8... | collective-permute-start | bytes 2654216 | tf_op jit(solution)/shard_map/ppermute | solution.py:223
  104.1 27.9 %copy-start.1 = (bf16[8,3,144,128]{3,2,1,0:T(8,128)(2,1)}, bf16[8,3,144,128]{3,2,1,0:T(8,128)(2,1)S(1)}, u32[]{:S(2)}) copy-start(bf16[8,3,144,128]{3,2,1,0:T(8,128)(2,1)S(1)} %all-to-all-done.2.refs_3_.refs_8_) | copy-start | bytes 2654212
  104.1 27.9 %collective-permute-start.7 = (bf16[8,3,144,128]{3,2,1,0:T(8,128)(2,1)S(1)}, bf16[8,3,144,128]{3,2,1,0:T(8,128)(2,1)S(1)}, u32[]{:S(2)}, u32[]{:S(2)}) collective-permute-start(bf16[8,3,144,128]{3,2,1,0:T(8,128)(2,1)S(1)} %all-to-all-done.2.refs_3_.refs_8_), channel_id=1, source_target_pairs={{0,128},{8,136},{16,144},{24,152},{32,160},{40,168},{48,176},{56,1... | collective-permute-start | bytes 2654216 | tf_op jit(solution)/shard_map/ppermute | solution.py:223
  106.7 33.2 %collective-permute-start.1 = (bf16[8,3,144,128]{3,2,1,0:T(8,128)(2,1)S(1)}, bf16[8,3,144,128]{3,2,1,0:T(8,128)(2,1)}, u32[]{:S(2)}, u32[]{:S(2)}) collective-permute-start(bf16[8,3,144,128]{3,2,1,0:T(8,128)(2,1)S(1)} %all-to-all-done.1.refs_1_), channel_id=1, source_target_pairs={{8,0},{16,8},{24,16},{32,24},{40,32},{48,40},{56,48},{72,64},{80,7... | collective-permute-start | bytes 2654216 | tf_op jit(solution)/shard_map/ppermute | solution.py:223
  116.6 23.2 %collective-permute-start = (bf16[8,3,144,128]{3,2,1,0:T(8,128)(2,1)S(1)}, bf16[8,3,144,128]{3,2,1,0:T(8,128)(2,1)}, u32[]{:S(2)}, u32[]{:S(2)}) collective-permute-start(bf16[8,3,144,128]{3,2,1,0:T(8,128)(2,1)S(1)} %all-to-all-done.1.refs_1_), channel_id=1, source_target_pairs={{0,8},{8,16},{16,24},{24,32},{32,40},{40,48},{48,56},{64,72},{72,8... | collective-permute-start | bytes 2654216 | tf_op jit(solution)/shard_map/ppermute | solution.py:223
  121.5 18.9 %collective-permute-start.8 = (bf16[8,2,144,128]{3,2,1,0:T(8,128)(2,1)}, bf16[8,2,144,128]{3,2,1,0:T(8,128)(2,1)}, u32[]{:S(2)}, u32[]{:S(2)}) collective-permute-start(bf16[8,2,144,128]{3,2,1,0:T(8,128)(2,1)} %slice.14), channel_id=1, source_target_pairs={{0,129},{1,128},{2,131},{3,130},{4,133},{5,132},{6,135},{7,134},{8... | collective-permute-start | bytes 1769480 | tf_op jit(solution)/shard_map/ppermute | solution.py:256
  129.5 2.6 %copy-start.3 = (bf16[8,3,144,128]{3,2,1,0:T(8,128)(2,1)}, bf16[8,3,144,128]{3,2,1,0:T(8,128)(2,1)S(1)}, u32[]{:S(2)}) copy-start(bf16[8,3,144,128]{3,2,1,0:T(8,128)(2,1)S(1)} %collective-permute-done.5.refs_1_.refs_6_) | copy-start | bytes 2654212
  129.5 10.4 %collective-permute-start.4 = (bf16[8,1,144,128]{3,2,1,0:T(8,128)(2,1)}, bf16[8,1,144,128]{3,2,1,0:T(8,128)(2,1)}, u32[]{:S(2)}, u32[]{:S(2)}) collective-permute-start(bf16[8,1,144,128]{3,2,1,0:T(8,128)(2,1)} %slice.12), channel_id=1, source_target_pairs={{0,128},{8,136},{16,144},{24,152},{32,160},{40,168},{48,176},{56,1... | collective-permute-start | bytes 884744 | tf_op jit(solution)/shard_map/ppermute | solution.py:223
  132.1 0.9 copy-start.4

commit v7 on v6

--- a/solution.py
+++ b/solution.py
@@ -16,10 +16,6 @@
 
 
 ANY = pl.BlockSpec(memory_space=pl.ANY)
-
-
-def after(value, *first):
-    return lax.optimization_barrier((value,) + first)[0]
 
 
 def lane(g, head, local, swap):
@@ -60,18 +56,23 @@
     )(swap, *arrays)
 
 
-def unpack_kernel(swap_ref, part, o_ref, sems):
+def unpack_kernel(swap_ref, part, o_ref, held, in_sems, sems):
     groups, local = part.shape[:2]
-    copies = []
-    for head in range(local):
-        swap = swap_ref[0] if head == SWAPPED else None
-        for g in range(groups):
+    arriving, leaving = [], []
+    for g in range(groups):
+        copy = pltpu.make_async_copy(part.at[g], held.at[g], in_sems.at[g])
+        copy.start()
+        arriving.append(copy)
+    for g in range(groups):
+        arriving[g].wait()
+        for head in range(local):
+            swap = swap_ref[0] if head == SWAPPED else None
             copy = pltpu.make_async_copy(
-                part.at[g, head], o_ref.at[:, pl.ds(lane(g, head, local, swap), HD)], sems.at[head, g]
+                held.at[g, head], o_ref.at[:, pl.ds(lane(g, head, local, swap), HD)], sems.at[head, g]
             )
             copy.start()
-            copies.append(copy)
-    for copy in copies:
+            leaving.append(copy)
+    for copy in leaving:
         copy.wait()
 
 
@@ -83,9 +84,13 @@
         grid_spec=pltpu.PrefetchScalarGridSpec(
             num_scalar_prefetch=1,
             grid=(1,),
-            in_specs=[pl.BlockSpec(part.shape, lambda i, *_: (0, 0, 0, 0))],
+            in_specs=[ANY],
             out_specs=ANY,
-            scratch_shapes=[pltpu.SemaphoreType.DMA((local, groups))],
+            scratch_shapes=[
+                pltpu.VMEM(part.shape, part.dtype),
+                pltpu.SemaphoreType.DMA((groups,)),
+                pltpu.SemaphoreType.DMA((local, groups)),
+            ],
         ),
         cost_estimate=pl.CostEstimate(
             flops=0, bytes_accessed=4 * groups * local * rows * HD, transcendentals=0
@@ -246,23 +251,24 @@
     rest = exchange(rest)
     most = pack(swap, [keys, values, query], [(2, 0), (2, 1), (2, 2), (0, 0), (1, 0), (0, 1)], groups)
     most = exchange(most)
-    far = send(after(rest, crossed), across)
+    far_1 = send(rest[:, 0:1], across)
+    far_2 = send(rest[:, 1:3], across)
     crossed = exchange(crossed)
     before_a = send(rest, right)
     behind_a = send(rest, left)
     own = most[:, 3:6]
     before_b = send(own, right)
     behind_b = send(own, left)
-    second_2 = lax.ppermute(far[:, 1:3], ("seq", "head"), hop)
-    second_1 = send(far[:, 0:1], middle)
+    second_2 = lax.ppermute(far_2, ("seq", "head"), hop)
+    second_1 = send(far_1, middle)
     second_b = send(crossed, middle)
     parts = local
     plan_0 = [[((0, 0),), ((0, 3), (0, 4)), ((1, 0), (1, 1)), ((2, 0), (2, 1)), ((3, 0), (3, 1)), ((4, 0), (4, 1))]]
     o = attend(idx, live, [most, before_b, behind_b, crossed, second_b], plan_0, (0,), parts)
-    sources = [most, rest, before_a, behind_a, far, second_1, before_b, behind_b, crossed, second_b, second_2]
+    sources = [most, rest, before_a, behind_a, far_1, second_1, before_b, behind_b, crossed, second_b, second_2, far_2]
     plan = [
         [((0, 1),), ((0, 5), (1, 0)), ((6, 2), (2, 0)), ((7, 2), (3, 0)), ((8, 2), (4, 0)), ((9, 2), (5, 0))],
-        [((0, 2),), ((1, 1), (1, 2)), ((2, 1), (2, 2)), ((3, 1), (3, 2)), ((4, 1), (4, 2)), ((10, 0), (10, 1))],
+        [((0, 2),), ((1, 1), (1, 2)), ((2, 1), (2, 2)), ((3, 1), (3, 2)), ((11, 0), (11, 1)), ((10, 0), (10, 1))],
     ]
     o = attend(idx, live, sources, plan, (1, 2), parts, o)
     o = exchange(o)

time: 177 us -> 192 us (1.085)
  the two profiles are of different devices: /device:TPU:32 before, /device:TPU:2 now
where the time goes in v7:
time: 192 us; the launch traced here: 191 us
  waiting for transfers between devices  82.1 us (43%)
  starting transfers between devices  52.5 us (27%)
  Pallas kernels  27 us (14%)
  blocking collectives  24 us (12%)
  local copies, waits for them, and re-layouts  4.46 us (2%)
    ppermute x9, waiting for transfers between devices, send(): return lax.ppermute(x, 'seq', pairs)  68.6 us
    ppermute x9, starting transfers between devices, send(): return lax.ppermute(x, 'seq', pairs)  34.6 us
    all_to_all x1, blocking collectives, exchange(): return lax.all_to_all(x, 'head', split_axis=0, concat_axis=0, tiled=True)  24 us
    pallas_call x2, Pallas kernels, attend(): pl.pallas_call(functools.partial(attend_kernel, tile, per_slab, plan, out...  17.1 us
    all_to_all x3, starting transfers between devices, exchange(): return lax.all_to_all(x, 'head', split_axis=0, concat_axis=0, tiled=True)  16.6 us
    all_to_all x3, waiting for transfers between devices, exchange(): return lax.all_to_all(x, 'head', split_axis=0, concat_axis=0, tiled=True)  12.3 us
    pallas_call x3, Pallas kernels, pack(): pl.pallas_call(functools.partial(pack_kernel, picks, width // (groups * H...  7.72 us
  transfers between devices with their start and end apart: 13, of which 5 were waited for; matrix products, arithmetic and copies ran while one was open for 2% of the time, Pallas kernels for 6%

profile of v7, /device:TPU:2, one launch (start us, length us, event | category | flops | bytes accessed | tf_op | source)
XLA Modules:
  0.0 191.4 jit_solution(5748489809708583350)
XLA Ops:
  0.0 2.3 %pack.4 = bf16[8,3,144,128]{3,2,1,0:T(8,128)(2,1)} custom-call(s32[1]{0:T(128)} %bitcast.swap_ref, bf16[144,3072]{1,0:T(8,128)(2,1)} %refs_0_.5, bf16[144,3072]{1,0:T(8,128)(2,1)} %refs_1_.5), custom_call_target="tpu_custom_call" | custom-call | bytes 1769472 | tf_op jit(solution)/shard_map/pack/pallas_call | solution.py:42
  2.3 6.0 %all-to-all-start.1 = ((bf16[8,3,144,128]{3,2,1,0:T(8,128)(2,1)}), bf16[8,3,144,128]{3,2,1,0:T(8,128)(2,1)S(1)}, u32[]{:S(2)}, u32[]{:S(2)}) async-start(bf16[8,3,144,128]{3,2,1,0:T(8,128)(2,1)} %pack.4), calls=%async_computation.1 | async-start | bytes 1769472 | tf_op jit(solution)/shard_map/all_to_all | solution.py:231
  8.3 3.1 %pack.3 = bf16[8,6,144,128]{3,2,1,0:T(8,128)(2,1)} custom-call(s32[1]{0:T(128)} %bitcast.swap_ref, bf16[144,3072]{1,0:T(8,128)(2,1)} %refs_0_.5, bf16[144,3072]{1,0:T(8,128)(2,1)} %refs_1_.5, bf16[144,3072]{1,0:T(8,128)(2,1)} %refs_2_.1), custom_call_target="tpu_custom_call" | custom-call | bytes 3538944 | tf_op jit(solution)/shard_map/pack/pallas_call | solution.py:42
  11.5 12.3 %all-to-all-done.1.refs_1_ = bf16[8,3,144,128]{3,2,1,0:T(8,128)(2,1)S(1)} async-done(((bf16[8,3,144,128]{3,2,1,0:T(8,128)(2,1)}), bf16[8,3,144,128]{3,2,1,0:T(8,128)(2,1)S(1)}, u32[]{:S(2)}, u32[]{:S(2)}) %all-to-all-start.1) | async-done | bytes 884768 | tf_op jit(solution)/shard_map/all_to_all | solution.py:231
  23.8 3.6 %all-to-all-start = ((bf16[8,6,144,128]{3,2,1,0:T(8,128)(2,1)}), bf16[8,6,144,128]{3,2,1,0:T(8,128)(2,1)S(1)}, u32[]{:S(2)}, u32[]{:S(2)}) async-start(bf16[8,6,144,128]{3,2,1,0:T(8,128)(2,1)} %pack.3), calls=%async_computation | async-start | bytes 3538944 | tf_op jit(solution)/shard_map/all_to_all | solution.py:231
  27.4 2.3 %pack.5 = bf16[8,3,144,128]{3,2,1,0:T(8,128)(2,1)} custom-call(s32[1]{0:T(128)} %bitcast.swap_ref, bf16[144,3072]{1,0:T(8,128)(2,1)} %refs_0_.5, bf16[144,3072]{1,0:T(8,128)(2,1)} %refs_1_.5), custom_call_target="tpu_custom_call" | custom-call | bytes 1769472 | tf_op jit(solution)/shard_map/pack/pallas_call | solution.py:42
  29.7 7.3 %collective-permute-start.6 = (bf16[8,3,144,128]{3,2,1,0:T(8,128)(2,1)}, bf16[8,3,144,128]{3,2,1,0:T(8,128)(2,1)S(1)}, u32[]{:S(2)}, u32[]{:S(2)}) collective-permute-start(bf16[8,3,144,128]{3,2,1,0:T(8,128)(2,1)} %pack.5), channel_id=1, source_target_pairs={{0,64},{8,72},{16,80},{24,88},{32,96},{40,104},{48,112},{56,120},{... | collective-permute-start | bytes 2654216 | tf_op jit(solution)/shard_map/ppermute | solution.py:228
  37.0 36.6 %collective-permute-done.6 = bf16[8,3,144,128]{3,2,1,0:T(8,128)(2,1)S(1)} collective-permute-done((bf16[8,3,144,128]{3,2,1,0:T(8,128)(2,1)}, bf16[8,3,144,128]{3,2,1,0:T(8,128)(2,1)S(1)}, u32[]{:S(2)}, u32[]{:S(2)}) %collective-permute-start.6) | collective-permute-done | bytes 884768 | tf_op jit(solution)/shard_map/ppermute | solution.py:228
  74.5 6.9 %all-to-all-start.2 = ((bf16[8,3,144,128]{3,2,1,0:T(8,128)(2,1)}), bf16[8,3,144,128]{3,2,1,0:T(8,128)(2,1)S(1)}, u32[]{:S(2)}, u32[]{:S(2)}) async-start(bf16[8,3,144,128]{3,2,1,0:T(8,128)(2,1)} %copy-done.5), calls=%async_computation.2 | async-start | bytes 1769472 | tf_op jit(solution)/shard_map/all_to_all | solution.py:231
  82.3 6.5 %collective-permute-start.8 = (bf16[8,2,144,128]{3,2,1,0:T(8,128)(2,1)}, bf16[8,2,144,128]{3,2,1,0:T(8,128)(2,1)}, u32[]{:S(2)}, u32[]{:S(2)}) collective-permute-start(bf16[8,2,144,128]{3,2,1,0:T(8,128)(2,1)} %slice.14), channel_id=1, source_target_pairs={{0,64},{8,72},{16,80},{24,88},{32,96},{40,104},{48,112},{56,120},{... | collective-permute-start | bytes 1769480 | tf_op jit(solution)/shard_map/ppermute | solution.py:228
  89.8 1.3 collective-permute-start.5
  91.0 3.1 %collective-permute-start.4 = (bf16[8,3,144,128]{3,2,1,0:T(8,128)(2,1)}, bf16[8,3,144,128]{3,2,1,0:T(8,128)(2,1)S(1)}, u32[]{:S(2)}, u32[]{:S(2)}) collective-permute-start(bf16[8,3,144,128]{3,2,1,0:T(8,128)(2,1)} %slice.13), channel_id=1, source_target_pairs={{0,8},{8,16},{16,24},{24,32},{32,40},{40,48},{48,56},{64,72},{72,8... | collective-permute-start | bytes 2654216 | tf_op jit(solution)/shard_map/ppermute | solution.py:228
  94.9 1.3 collective-permute-start.7
  96.2 26.3 %collective-permute-done.2.refs_4_ = bf16[8,1,144,128]{3,2,1,0:T(8,128)(2,1)} collective-permute-done((bf16[8,1,144,128]{3,2,1,0:T(8,128)(2,1)}, bf16[8,1,144,128]{3,2,1,0:T(8,128)(2,1)}, u32[]{:S(2)}, u32[]{:S(2)}) %collective-permute-start.2) | collective-permute-done | bytes 294944 | tf_op jit(solution)/shard_map/ppermute | solution.py:228
  122.5 1.3 collective-permute-start.1
  123.8 12.5 %collective-permute-start = (bf16[8,3,144,128]{3,2,1,0:T(8,128)(2,1)S(1)}, bf16[8,3,144,128]{3,2,1,0:T(8,128)(2,1)}, u32[]{:S(2)}, u32[]{:S(2)}) collective-permute-start(bf16[8,3,144,128]{3,2,1,0:T(8,128)(2,1)S(1)} %all-to-all-done.1.refs_1_), channel_id=1, source_target_pairs={{0,8},{8,16},{16,24},{24,32},{32,40},{40,48},{48,56},{64,72},{72,8... | collective-permute-start | bytes 2654216 | tf_op jit(solution)/shard_map/ppermute | solution.py:228
  136.3 1.3 collective-permute-start.9
  138.2 1.5 collective-permute-start.3
  141.2 6.9 %attend.2.refs_12_ = bf16[8,3,144,128]{3,2,1,0:T(8,128)(2,1)} custom-call(s32[3,5]{1,0:T(4,128)} %fusion.1.idx_ref, s32[3,5]{1,0:T(4,128)} %fusion.4.live_ref, bf16[8,6,144,128]{3,2,1,0:T(8,128)(2,1)} %copy-done, bf16[8,3,144,128]{3,2,1,0:T(8,128)(2,1)} %copy-done.3, bf16[8,3,144,128]{3,2,1,0:T(8,128)(2,1)} %collective-permute-done.5.refs_2_.refs_7_, ...), custom_call_target="tpu_custom_call" | custom-call | flops 1132462080 | bytes 3538944 | tf_op jit(solution)/shard_map/attend/pallas_call | solution.py:186
  148.0 5.7 %collective-permute-done.3.refs_5_ = bf16[8,1,144,128]{3,2,1,0:T(8,128)(2,1)} collective-permute-done((bf16[8,1,144,128]{3,2,1,0:T(8,128)(2,1)}, bf16[8,1,144,128]{3,2,1,0:T(8,128)(2,1)}, u32[]{:S(2)}, u32[]{:S(2)}) %collective-permute-start.3) | collective-permute-done | bytes 294944 | tf_op jit(solution)/shard_map/ppermute | solution.py:228
  153.7 1.2 collective-permute-done.9.refs_10_
  154.9 10.2 %attend.3 = bf16[8,3,144,128]{3,2,1,0:T(8,128)(2,1)} custom-call(s32[3,5]{1,0:T(4,128)} %fusion.1.idx_ref, s32[3,5]{1,0:T(4,128)} %fusion.4.live_ref, bf16[8,6,144,128]{3,2,1,0:T(8,128)(2,1)} %copy-done, bf16[8,3,144,128]{3,2,1,0:T(8,128)(2,1)} %copy-done.1, bf16[8,3,144,128]{3,2,1,0:T(8,128)(2,1)} %collective-permute-done.refs_2_, ...), custom_call_target="tpu_custom_call", output_to_operand_aliasing={{}: (14, {})} | custom-call | flops 2264924160 | bytes 7077888 | tf_op jit(solution)/shard_map/attend/pallas_call | solution.py:186
  165.1 24.0 %all_to_all.20.part = bf16[8,3,144,128]{3,2,1,0:T(8,128)(2,1)} all-to-all(bf16[8,3,144,128]{3,2,1,0:T(8,128)(2,1)} %attend.3), channel_id=1, replica_groups=mesh['seq'=32,'head'=8] {'head'}, dimensions={0} | all-to-all | bytes 1769472 | tf_op jit(solution)/shard_map/all_to_all | solution.py:231
  189.1 2.2 %unpack.1 = bf16[144,3072]{1,0:T(8,128)(2,1)} custom-call(s32[1]{0:T(128)} %bitcast.swap_ref, bf16[8,3,144,128]{3,2,1,0:T(8,128)(2,1)} %all_to_all.20.part), custom_call_target="tpu_custom_call" | custom-call | bytes 1769472 | tf_op jit(solution)/shard_map/unpack/pallas_call | solution.py:81
  (28 shorter events, 5.6 us)
Async XLA Ops:
  2.3 21.5 %all-to-all-start.1 = ((bf16[8,3,144,128]{3,2,1,0:T(8,128)(2,1)}), bf16[8,3,144,128]{3,2,1,0:T(8,128)(2,1)S(1)}, u32[]{:S(2)}, u32[]{:S(2)}) async-start(bf16[8,3,144,128]{3,2,1,0:T(8,128)(2,1)} %pack.4), calls=%async_computation.1 | async-start | bytes 1769472 | tf_op jit(solution)/shard_map/all_to_all | solution.py:231
  23.8 100.0 %copy-start.1 = (bf16[8,3,144,128]{3,2,1,0:T(8,128)(2,1)}, bf16[8,3,144,128]{3,2,1,0:T(8,128)(2,1)S(1)}, u32[]{:S(2)}) copy-start(bf16[8,3,144,128]{3,2,1,0:T(8,128)(2,1)S(1)} %all-to-all-done.1.refs_1_) | copy-start | bytes 2654212
  23.8 50.7 %all-to-all-start = ((bf16[8,6,144,128]{3,2,1,0:T(8,128)(2,1)}), bf16[8,6,144,128]{3,2,1,0:T(8,128)(2,1)S(1)}, u32[]{:S(2)}, u32[]{:S(2)}) async-start(bf16[8,6,144,128]{3,2,1,0:T(8,128)(2,1)} %pack.3), calls=%async_computation | async-start | bytes 3538944 | tf_op jit(solution)/shard_map/all_to_all | solution.py:231
  29.7 43.9 %collective-permute-start.6 = (bf16[8,3,144,128]{3,2,1,0:T(8,128)(2,1)}, bf16[8,3,144,128]{3,2,1,0:T(8,128)(2,1)S(1)}, u32[]{:S(2)}, u32[]{:S(2)}) collective-permute-start(bf16[8,3,144,128]{3,2,1,0:T(8,128)(2,1)} %pack.5), channel_id=1, source_target_pairs={{0,64},{8,72},{16,80},{24,88},{32,96},{40,104},{48,112},{56,120},{... | collective-permute-start | bytes 2654216 | tf_op jit(solution)/shard_map/ppermute | solution.py:228
  73.6 0.9 copy-start.5
  74.5 15.3 %copy-start = (bf16[8,6,144,128]{3,2,1,0:T(8,128)(2,1)}, bf16[8,6,144,128]{3,2,1,0:T(8,128)(2,1)S(1)}, u32[]{:S(2)}) copy-start(bf16[8,6,144,128]{3,2,1,0:T(8,128)(2,1)S(1)} %all-to-all-done.refs_0_) | copy-start | bytes 5308420
  74.5 20.4 %all-to-all-start.2 = ((bf16[8,3,144,128]{3,2,1,0:T(8,128)(2,1)}), bf16[8,3,144,128]{3,2,1,0:T(8,128)(2,1)S(1)}, u32[]{:S(2)}, u32[]{:S(2)}) async-start(bf16[8,3,144,128]{3,2,1,0:T(8,128)(2,1)} %copy-done.5), calls=%async_computation.2 | async-start | bytes 1769472 | tf_op jit(solution)/shard_map/all_to_all | solution.py:231
  81.4 56.1 %copy-start.6 = (s32[3,5]{1,0:T(4,128)S(1)}, s32[3,5]{1,0:T(4,128)}, u32[]{:S(2)}) copy-start(s32[3,5]{1,0:T(4,128)} %param.7) | copy-start | bytes 184
  82.3 41.5 %collective-permute-start.8 = (bf16[8,2,144,128]{3,2,1,0:T(8,128)(2,1)}, bf16[8,2,144,128]{3,2,1,0:T(8,128)(2,1)}, u32[]{:S(2)}, u32[]{:S(2)}) collective-permute-start(bf16[8,2,144,128]{3,2,1,0:T(8,128)(2,1)} %slice.14), channel_id=1, source_target_pairs={{0,64},{8,72},{16,80},{24,88},{32,96},{40,104},{48,112},{56,120},{... | collective-permute-start | bytes 1769480 | tf_op jit(solution)/shard_map/ppermute | solution.py:228
  89.8 46.5 %collective-permute-start.5 = (bf16[8,3,144,128]{3,2,1,0:T(8,128)(2,1)}, bf16[8,3,144,128]{3,2,1,0:T(8,128)(2,1)}, u32[]{:S(2)}, u32[]{:S(2)}) collective-permute-start(bf16[8,3,144,128]{3,2,1,0:T(8,128)(2,1)} %slice.13), channel_id=1, source_target_pairs={{8,0},{16,8},{24,16},{32,24},{40,32},{48,40},{56,48},{72,64},{80,7... | collective-permute-start | bytes 2654216 | tf_op jit(solution)/shard_map/ppermute | solution.py:228
  91.0 47.1 %collective-permute-start.4 = (bf16[8,3,144,128]{3,2,1,0:T(8,128)(2,1)}, bf16[8,3,144,128]{3,2,1,0:T(8,128)(2,1)S(1)}, u32[]{:S(2)}, u32[]{:S(2)}) collective-permute-start(bf16[8,3,144,128]{3,2,1,0:T(8,128)(2,1)} %slice.13), channel_id=1, source_target_pairs={{0,8},{8,16},{16,24},{24,32},{32,40},{40,48},{48,56},{64,72},{72,8... | collective-permute-start | bytes 2654216 | tf_op jit(solution)/shard_map/ppermute | solution.py:228
  94.9 27.6 %collective-permute-start.2 = (bf16[8,1,144,128]{3,2,1,0:T(8,128)(2,1)}, bf16[8,1,144,128]{3,2,1,0:T(8,128)(2,1)}, u32[]{:S(2)}, u32[]{:S(2)}) collective-permute-start(bf16[8,1,144,128]{3,2,1,0:T(8,128)(2,1)} %slice.12), channel_id=1, source_target_pairs={{0,64},{8,72},{16,80},{24,88},{32,96},{40,104},{48,112},{56,120},{... | collective-permute-start | bytes 884744 | tf_op jit(solution)/shard_map/ppermute | solution.py:228
  94.9 45.3 %copy-start.2 = (bf16[8,3,144,128]{3,2,1,0:T(8,128)(2,1)}, bf16[8,3,144,128]{3,2,1,0:T(8,128)(2,1)S(1)}, u32[]{:S(2)}) copy-start(bf16[8,3,144,128]{3,2,1,0:T(8,128)(2,1)S(1)} %all-to-all-done.2.refs_3_.refs_8_) | copy-start | bytes 2654212
  94.9 45.3 %collective-permute-start.7 = (bf16[8,3,144,128]{3,2,1,0:T(8,128)(2,1)S(1)}, bf16[8,3,144,128]{3,2,1,0:T(8,128)(2,1)S(1)}, u32[]{:S(2)}, u32[]{:S(2)}) collective-permute-start(bf16[8,3,144,128]{3,2,1,0:T(8,128)(2,1)S(1)} %all-to-all-done.2.refs_3_.refs_8_), channel_id=1, source_target_pairs={{0,128},{8,136},{16,144},{24,152},{32,160},{40,168},{48,176},{56,1... | collective-permute-start | bytes 2654216 | tf_op jit(solution)/shard_map/ppermute | solution.py:228
  122.5 31.3 %collective-permute-start.1 = (bf16[8,3,144,128]{3,2,1,0:T(8,128)(2,1)S(1)}, bf16[8,3,144,128]{3,2,1,0:T(8,128)(2,1)}, u32[]{:S(2)}, u32[]{:S(2)}) collective-permute-start(bf16[8,3,144,128]{3,2,1,0:T(8,128)(2,1)S(1)} %all-to-all-done.1.refs_1_), channel_id=1, source_target_pairs={{8,0},{16,8},{24,16},{32,24},{40,32},{48,40},{56,48},{72,64},{80,7... | collective-permute-start | bytes 2654216 | tf_op jit(solution)/shard_map/ppermute | solution.py:228
  123.8 30.0 %collective-permute-start = (bf16[8,3,144,128]{3,2,1,0:T(8,128)(2,1)S(1)}, bf16[8,3,144,128]{3,2,1,0:T(8,128)(2,1)}, u32[]{:S(2)}, u32[]{:S(2)}) collective-permute-start(bf16[8,3,144,128]{3,2,1,0:T(8,128)(2,1)S(1)} %all-to-all-done.1.refs_1_), channel_id=1, source_target_pairs={{0,8},{8,16},{16,24},{24,32},{32,40},{40,48},{48,56},{64,72},{72,8... | collective-permute-start | bytes 2654216 | tf_op jit(solution)/shard_map/ppermute | solution.py:228
  136.3 18.7 %collective-permute-start.9 = (bf16[8,2,144,128]{3,2,1,0:T(8,128)(2,1)}, bf16[8,2,144,128]{3,2,1,0:T(8,128)(2,1)}, u32[]{:S(2)}, u32[]{:S(2)}) collective-permute-start(bf16[8,2,144,128]{3,2,1,0:T(8,128)(2,1)} %collective-permute-done.8.refs_11_), channel_id=1, source_target_pairs={{0,129},{1,128},{2,131},{3,130},{4,133},{5,132},{6,135},{7,134},{8... | collective-permute-start | bytes 1769480 | tf_op jit(solution)/shard_map/ppermute | solution.py:262
  138.2 2.0 %copy-start.3 = (bf16[8,3,144,128]{3,2,1,0:T(8,128)(2,1)}, bf16[8,3,144,128]{3,2,1,0:T(8,128)(2,1)S(1)}, u32[]{:S(2)}) copy-start(bf16[8,3,144,128]{3,2,1,0:T(8,128)(2,1)S(1)} %collective-permute-done.4.refs_1_.refs_6_) | copy-start | bytes 2654212
  138.2 15.6 %collective-permute-start.3 = (bf16[8,1,144,128]{3,2,1,0:T(8,128)(2,1)}, bf16[8,1,144,128]{3,2,1,0:T(8,128)(2,1)}, u32[]{:S(2)}, u32[]{:S(2)}) collective-permute-start(bf16[8,1,144,128]{3,2,1,0:T(8,128)(2,1)} %collective-permute-done.2.refs_4_), channel_id=1, source_target_pairs={{0,128},{8,136},{16,144},{24,152},{32,160},{40,168},{48,176},{56,1... | collective-permute-start | bytes 884744 | tf_op jit(solution)/shard_map/ppermute | solution.py:228
  140.2 0.9 copy-start.4

commit v8 on v7

--- a/solution.py
+++ b/solution.py
@@ -16,6 +16,10 @@
 
 
 ANY = pl.BlockSpec(memory_space=pl.ANY)
+
+
+def after(value, *first):
+    return lax.optimization_barrier((value,) + first)[0]
 
 
 def lane(g, head, local, swap):
@@ -249,25 +253,25 @@
     crossed = send(first, across)
     rest = pack(swap, [keys, values], [(1, 1), (0, 2), (1, 2)], groups)
     rest = exchange(rest)
-    most = pack(swap, [keys, values, query], [(2, 0), (2, 1), (2, 2), (0, 0), (1, 0), (0, 1)], groups)
+    own = exchange(first)
+    most = pack(swap, [query], [(0, 0), (0, 1), (0, 2)], groups)
+    far_1 = send(rest[:, 0:1], across)
+    far_2 = send(after(rest[:, 1:3], crossed), across)
+    crossed = exchange(crossed)
     most = exchange(most)
-    far_1 = send(rest[:, 0:1], across)
-    far_2 = send(rest[:, 1:3], across)
-    crossed = exchange(crossed)
     before_a = send(rest, right)
     behind_a = send(rest, left)
-    own = most[:, 3:6]
     before_b = send(own, right)
     behind_b = send(own, left)
     second_2 = lax.ppermute(far_2, ("seq", "head"), hop)
     second_1 = send(far_1, middle)
     second_b = send(crossed, middle)
     parts = local
-    plan_0 = [[((0, 0),), ((0, 3), (0, 4)), ((1, 0), (1, 1)), ((2, 0), (2, 1)), ((3, 0), (3, 1)), ((4, 0), (4, 1))]]
-    o = attend(idx, live, [most, before_b, behind_b, crossed, second_b], plan_0, (0,), parts)
-    sources = [most, rest, before_a, behind_a, far_1, second_1, before_b, behind_b, crossed, second_b, second_2, far_2]
+    plan_0 = [[((0, 0),)] + [((n, 0), (n, 1)) for n in range(1, 6)]]
+    o = attend(idx, live, [most, own, before_b, behind_b, crossed, second_b], plan_0, (0,), parts)
+    sources = [most, rest, before_a, behind_a, far_1, second_1, before_b, behind_b, crossed, second_b, second_2, far_2, own]
     plan = [
-        [((0, 1),), ((0, 5), (1, 0)), ((6, 2), (2, 0)), ((7, 2), (3, 0)), ((8, 2), (4, 0)), ((9, 2), (5, 0))],
+        [((0, 1),), ((12, 2), (1, 0)), ((6, 2), (2, 0)), ((7, 2), (3, 0)), ((8, 2), (4, 0)), ((9, 2), (5, 0))],
         [((0, 2),), ((1, 1), (1, 2)), ((2, 1), (2, 2)), ((3, 1), (3, 2)), ((11, 0), (11, 1)), ((10, 0), (10, 1))],
     ]
     o = attend(idx, live, sources, plan, (1, 2), parts, o)

time: 192 us -> 184 us (0.958)
  the two profiles are of different devices: /device:TPU:2 before, /device:TPU:1 now
where the time goes in v8:
time: 184 us
  starting transfers between devices  68.9 us (37%)
  waiting for transfers between devices  45.9 us (25%)
  blocking collectives  38.8 us (21%)
  Pallas kernels  26.1 us (14%)
  local copies, waits for them, and re-layouts  2.34 us (1%)
    ppermute x9, starting transfers between devices, send(): return lax.ppermute(x, 'seq', pairs)  44.1 us
    all_to_all x2, blocking collectives, exchange(): return lax.all_to_all(x, 'head', split_axis=0, concat_axis=0, tiled=True)  38.8 us
    ppermute x9, waiting for transfers between devices, send(): return lax.ppermute(x, 'seq', pairs)  33.8 us
    all_to_all x3, starting transfers between devices, exchange(): return lax.all_to_all(x, 'head', split_axis=0, concat_axis=0, tiled=True)  19.3 us
    pallas_call x2, Pallas kernels, attend(): pl.pallas_call(functools.partial(attend_kernel, tile, per_slab, plan, out...  17.1 us
    all_to_all x3, waiting for transfers between devices, exchange(): return lax.all_to_all(x, 'head', split_axis=0, concat_axis=0, tiled=True)  12 us
    pallas_call x3, Pallas kernels, pack(): pl.pallas_call(functools.partial(pack_kernel, picks, width // (groups * H...  6.87 us
    ppermute x1, starting transfers between devices, body(): second_2 = lax.ppermute(far_2, ('seq', 'head'), hop)  5.48 us
  transfers between devices with their start and end apart: 13, of which 3 were waited for; matrix products, arithmetic and copies ran while one was open for 1% of the time, Pallas kernels for 6%

profile of v8, /device:TPU:1, one launch (start us, length us, event | category | flops | bytes accessed | tf_op | source)
XLA Modules:
  0.0 183.5 jit_solution(9830513680929488599)
XLA Ops:
  0.0 2.3 %pack.5 = bf16[8,3,144,128]{3,2,1,0:T(8,128)(2,1)} custom-call(s32[1]{0:T(128)} %bitcast.swap_ref, bf16[144,3072]{1,0:T(8,128)(2,1)} %refs_0_.5, bf16[144,3072]{1,0:T(8,128)(2,1)} %refs_1_.3), custom_call_target="tpu_custom_call" | custom-call | bytes 1769472 | tf_op jit(solution)/shard_map/pack/pallas_call | solution.py:46
  2.3 7.6 %all-to-all-start.2 = ((bf16[8,3,144,128]{3,2,1,0:T(8,128)(2,1)}), bf16[8,3,144,128]{3,2,1,0:T(8,128)(2,1)S(1)}, u32[]{:S(2)}, u32[]{:S(2)}) async-start(bf16[8,3,144,128]{3,2,1,0:T(8,128)(2,1)} %pack.5), calls=%async_computation.2 | async-start | bytes 1769472 | tf_op jit(solution)/shard_map/all_to_all | solution.py:235
  9.9 7.0 %collective-permute-start.6 = (bf16[8,3,144,128]{3,2,1,0:T(8,128)(2,1)S(1)}, bf16[8,3,144,128]{3,2,1,0:T(8,128)(2,1)}, u32[]{:S(2)}, u32[]{:S(2)}) collective-permute-start(bf16[8,3,144,128]{3,2,1,0:T(8,128)(2,1)S(1)} %copy-done.4), channel_id=1, source_target_pairs={{0,64},{8,72},{16,80},{24,88},{32,96},{40,104},{48,112},{56,120},{... | collective-permute-start | bytes 2654216 | tf_op jit(solution)/shard_map/ppermute | solution.py:232
  16.9 2.3 %pack.4 = bf16[8,3,144,128]{3,2,1,0:T(8,128)(2,1)} custom-call(s32[1]{0:T(128)} %bitcast.swap_ref, bf16[144,3072]{1,0:T(8,128)(2,1)} %refs_0_.5, bf16[144,3072]{1,0:T(8,128)(2,1)} %refs_1_.3), custom_call_target="tpu_custom_call" | custom-call | bytes 1769472 | tf_op jit(solution)/shard_map/pack/pallas_call | solution.py:46
  19.2 5.2 %all-to-all-done.2.refs_1_.refs_12_ = bf16[8,3,144,128]{3,2,1,0:T(8,128)(2,1)S(1)} async-done(((bf16[8,3,144,128]{3,2,1,0:T(8,128)(2,1)}), bf16[8,3,144,128]{3,2,1,0:T(8,128)(2,1)S(1)}, u32[]{:S(2)}, u32[]{:S(2)}) %all-to-all-start.2) | async-done | bytes 884768 | tf_op jit(solution)/shard_map/all_to_all | solution.py:235
  24.5 17.8 %all_to_all.25.refs_1_ = bf16[8,3,144,128]{3,2,1,0:T(8,128)(2,1)S(1)} all-to-all(bf16[8,3,144,128]{3,2,1,0:T(8,128)(2,1)} %pack.4), channel_id=1, replica_groups=mesh['seq'=32,'head'=8] {'head'}, dimensions={0} | all-to-all | bytes 1769472 | tf_op jit(solution)/shard_map/all_to_all | solution.py:235
  42.3 4.7 %all-to-all-start.3 = ((bf16[8,3,144,128]{3,2,1,0:T(8,128)(2,1)}), bf16[8,3,144,128]{3,2,1,0:T(8,128)(2,1)S(1)}, u32[]{:S(2)}, u32[]{:S(2)}) async-start(bf16[8,3,144,128]{3,2,1,0:T(8,128)(2,1)} %collective-permute-done.6), calls=%async_computation.3 | async-start | bytes 1769472 | tf_op jit(solution)/shard_map/all_to_all | solution.py:235
  47.0 5.9 %collective-permute-start.8 = (bf16[8,2,144,128]{3,2,1,0:T(8,128)(2,1)S(1)}, bf16[8,2,144,128]{3,2,1,0:T(8,128)(2,1)}, u32[]{:S(2)}, u32[]{:S(2)}) collective-permute-start(bf16[8,2,144,128]{3,2,1,0:T(8,128)(2,1)S(1)} %slice.9), channel_id=1, source_target_pairs={{0,64},{8,72},{16,80},{24,88},{32,96},{40,104},{48,112},{56,120},{... | collective-permute-start | bytes 1769480 | tf_op jit(solution)/shard_map/ppermute | solution.py:232
  52.9 18.0 %collective-permute-start.5 = (bf16[8,3,144,128]{3,2,1,0:T(8,128)(2,1)S(1)}, bf16[8,3,144,128]{3,2,1,0:T(8,128)(2,1)}, u32[]{:S(2)}, u32[]{:S(2)}) collective-permute-start(bf16[8,3,144,128]{3,2,1,0:T(8,128)(2,1)S(1)} %all-to-all-done.2.refs_1_.refs_12_), channel_id=1, source_target_pairs={{8,0},{16,8},{24,16},{32,24},{40,32},{48,40},{56,48},{72,64},{80,7... | collective-permute-start | bytes 2654216 | tf_op jit(solution)/shard_map/ppermute | solution.py:232
  70.9 2.8 %collective-permute-start.4 = (bf16[8,3,144,128]{3,2,1,0:T(8,128)(2,1)S(1)}, bf16[8,3,144,128]{3,2,1,0:T(8,128)(2,1)}, u32[]{:S(2)}, u32[]{:S(2)}) collective-permute-start(bf16[8,3,144,128]{3,2,1,0:T(8,128)(2,1)S(1)} %all-to-all-done.2.refs_1_.refs_12_), channel_id=1, source_target_pairs={{0,8},{8,16},{16,24},{24,32},{32,40},{40,48},{48,56},{64,72},{72,8... | collective-permute-start | bytes 2654216 | tf_op jit(solution)/shard_map/ppermute | solution.py:232
  74.0 3.2 %collective-permute-start.7 = (bf16[8,3,144,128]{3,2,1,0:T(8,128)(2,1)S(1)}, bf16[8,3,144,128]{3,2,1,0:T(8,128)(2,1)}, u32[]{:S(2)}, u32[]{:S(2)}) collective-permute-start(bf16[8,3,144,128]{3,2,1,0:T(8,128)(2,1)S(1)} %all-to-all-done.3.refs_4_.refs_8_), channel_id=1, source_target_pairs={{0,128},{8,136},{16,144},{24,152},{32,160},{40,168},{48,176},{56,1... | collective-permute-start | bytes 2654216 | tf_op jit(solution)/shard_map/ppermute | solution.py:232
  77.1 33.8 %collective-permute-done.2.refs_4_ = bf16[8,1,144,128]{3,2,1,0:T(8,128)(2,1)} collective-permute-done((bf16[8,1,144,128]{3,2,1,0:T(8,128)(2,1)S(1)}, bf16[8,1,144,128]{3,2,1,0:T(8,128)(2,1)}, u32[]{:S(2)}, u32[]{:S(2)}) %collective-permute-start.2) | collective-permute-done | bytes 294944 | tf_op jit(solution)/shard_map/ppermute | solution.py:232
  111.0 1.9 %collective-permute-start.1 = (bf16[8,3,144,128]{3,2,1,0:T(8,128)(2,1)S(1)}, bf16[8,3,144,128]{3,2,1,0:T(8,128)(2,1)}, u32[]{:S(2)}, u32[]{:S(2)}) collective-permute-start(bf16[8,3,144,128]{3,2,1,0:T(8,128)(2,1)S(1)} %all_to_all.25.refs_1_), channel_id=1, source_target_pairs={{8,0},{16,8},{24,16},{32,24},{40,32},{48,40},{56,48},{72,64},{80,7... | collective-permute-start | bytes 2654216 | tf_op jit(solution)/shard_map/ppermute | solution.py:232
  112.9 3.6 %collective-permute-start = (bf16[8,3,144,128]{3,2,1,0:T(8,128)(2,1)S(1)}, bf16[8,3,144,128]{3,2,1,0:T(8,128)(2,1)}, u32[]{:S(2)}, u32[]{:S(2)}) collective-permute-start(bf16[8,3,144,128]{3,2,1,0:T(8,128)(2,1)S(1)} %all_to_all.25.refs_1_), channel_id=1, source_target_pairs={{0,8},{8,16},{16,24},{24,32},{32,40},{40,48},{48,56},{64,72},{72,8... | collective-permute-start | bytes 2654216 | tf_op jit(solution)/shard_map/ppermute | solution.py:232
  116.5 2.3 %pack.3 = bf16[8,3,144,128]{3,2,1,0:T(8,128)(2,1)} custom-call(s32[1]{0:T(128)} %bitcast.swap_ref, bf16[144,3072]{1,0:T(8,128)(2,1)} %refs_0_.3), custom_call_target="tpu_custom_call" | custom-call | bytes 1769472 | tf_op jit(solution)/shard_map/pack/pallas_call | solution.py:46
  118.9 7.0 %all-to-all-start = ((bf16[8,3,144,128]{3,2,1,0:T(8,128)(2,1)}), bf16[8,3,144,128]{3,2,1,0:T(8,128)(2,1)S(1)}, u32[]{:S(2)}, u32[]{:S(2)}) async-start(bf16[8,3,144,128]{3,2,1,0:T(8,128)(2,1)} %pack.3), calls=%async_computation | async-start | bytes 1769472 | tf_op jit(solution)/shard_map/all_to_all | solution.py:235
  125.9 5.5 %collective-permute-start.9 = (bf16[8,2,144,128]{3,2,1,0:T(8,128)(2,1)}, bf16[8,2,144,128]{3,2,1,0:T(8,128)(2,1)}, u32[]{:S(2)}, u32[]{:S(2)}) collective-permute-start(bf16[8,2,144,128]{3,2,1,0:T(8,128)(2,1)} %collective-permute-done.8.refs_11_), channel_id=1, source_target_pairs={{0,129},{1,128},{2,131},{3,130},{4,133},{5,132},{6,135},{7,134},{8... | collective-permute-start | bytes 1769480 | tf_op jit(solution)/shard_map/ppermute | solution.py:266
  132.6 1.5 collective-permute-start.3
  134.7 6.8 %all-to-all-done.refs_0_ = bf16[8,3,144,128]{3,2,1,0:T(8,128)(2,1)S(1)} async-done(((bf16[8,3,144,128]{3,2,1,0:T(8,128)(2,1)}), bf16[8,3,144,128]{3,2,1,0:T(8,128)(2,1)S(1)}, u32[]{:S(2)}, u32[]{:S(2)}) %all-to-all-start) | async-done | bytes 884768 | tf_op jit(solution)/shard_map/all_to_all | solution.py:235
  141.4 0.9 copy-done.3
  142.4 6.8 %attend.2.refs_13_ = bf16[8,3,144,128]{3,2,1,0:T(8,128)(2,1)} custom-call(s32[3,5]{1,0:T(4,128)} %fusion.1.idx_ref, s32[3,5]{1,0:T(4,128)} %fusion.4.live_ref, bf16[8,3,144,128]{3,2,1,0:T(8,128)(2,1)} %copy-done.3, bf16[8,3,144,128]{3,2,1,0:T(8,128)(2,1)} %copy-done.1, bf16[8,3,144,128]{3,2,1,0:T(8,128)(2,1)} %collective-permute-done.4.refs_2_.refs_6_, ...), custom_call_target="tpu_custom_call" | custom-call | flops 1132462080 | bytes 3538944 | tf_op jit(solution)/shard_map/attend/pallas_call | solution.py:190
  149.9 10.2 %attend.3 = bf16[8,3,144,128]{3,2,1,0:T(8,128)(2,1)} custom-call(s32[3,5]{1,0:T(4,128)} %fusion.1.idx_ref, s32[3,5]{1,0:T(4,128)} %fusion.4.live_ref, bf16[8,3,144,128]{3,2,1,0:T(8,128)(2,1)} %copy-done.3, bf16[8,3,144,128]{3,2,1,0:T(8,128)(2,1)} %copy-done, bf16[8,3,144,128]{3,2,1,0:T(8,128)(2,1)} %collective-permute-done.refs_2_, ...), custom_call_target="tpu_custom_call", output_to_operand_aliasing={{}: (15, {})} | custom-call | flops 2264924160 | bytes 7077888 | tf_op jit(solution)/shard_map/attend/pallas_call | solution.py:190
  160.2 21.0 %all_to_all.26.part = bf16[8,3,144,128]{3,2,1,0:T(8,128)(2,1)} all-to-all(bf16[8,3,144,128]{3,2,1,0:T(8,128)(2,1)} %attend.3), channel_id=1, replica_groups=mesh['seq'=32,'head'=8] {'head'}, dimensions={0} | all-to-all | bytes 1769472 | tf_op jit(solution)/shard_map/all_to_all | solution.py:235
  181.2 2.2 %unpack.1 = bf16[144,3072]{1,0:T(8,128)(2,1)} custom-call(s32[1]{0:T(128)} %bitcast.swap_ref, bf16[8,3,144,128]{3,2,1,0:T(8,128)(2,1)} %all_to_all.26.part), custom_call_target="tpu_custom_call" | custom-call | bytes 1769472 | tf_op jit(solution)/shard_map/unpack/pallas_call | solution.py:85
  (28 shorter events, 2.8 us)
Async XLA Ops:
  2.3 7.6 %copy-start.4 = (bf16[8,3,144,128]{3,2,1,0:T(8,128)(2,1)S(1)}, bf16[8,3,144,128]{3,2,1,0:T(8,128)(2,1)}, u32[]{:S(2)}) copy-start(bf16[8,3,144,128]{3,2,1,0:T(8,128)(2,1)} %pack.5) | copy-start | bytes 2654212
  2.3 22.2 %all-to-all-start.2 = ((bf16[8,3,144,128]{3,2,1,0:T(8,128)(2,1)}), bf16[8,3,144,128]{3,2,1,0:T(8,128)(2,1)S(1)}, u32[]{:S(2)}, u32[]{:S(2)}) async-start(bf16[8,3,144,128]{3,2,1,0:T(8,128)(2,1)} %pack.5), calls=%async_computation.2 | async-start | bytes 1769472 | tf_op jit(solution)/shard_map/all_to_all | solution.py:235
  9.9 32.4 %collective-permute-start.6 = (bf16[8,3,144,128]{3,2,1,0:T(8,128)(2,1)S(1)}, bf16[8,3,144,128]{3,2,1,0:T(8,128)(2,1)}, u32[]{:S(2)}, u32[]{:S(2)}) collective-permute-start(bf16[8,3,144,128]{3,2,1,0:T(8,128)(2,1)S(1)} %copy-done.4), channel_id=1, source_target_pairs={{0,64},{8,72},{16,80},{24,88},{32,96},{40,104},{48,112},{56,120},{... | collective-permute-start | bytes 2654216 | tf_op jit(solution)/shard_map/ppermute | solution.py:232
  24.5 46.4 %copy-start.1 = (bf16[8,3,144,128]{3,2,1,0:T(8,128)(2,1)}, bf16[8,3,144,128]{3,2,1,0:T(8,128)(2,1)S(1)}, u32[]{:S(2)}) copy-start(bf16[8,3,144,128]{3,2,1,0:T(8,128)(2,1)S(1)} %all-to-all-done.2.refs_1_.refs_12_) | copy-start | bytes 2654212
  42.3 70.6 %copy-start = (bf16[8,3,144,128]{3,2,1,0:T(8,128)(2,1)}, bf16[8,3,144,128]{3,2,1,0:T(8,128)(2,1)S(1)}, u32[]{:S(2)}) copy-start(bf16[8,3,144,128]{3,2,1,0:T(8,128)(2,1)S(1)} %all_to_all.25.refs_1_) | copy-start | bytes 2654212
  42.3 31.7 %all-to-all-start.3 = ((bf16[8,3,144,128]{3,2,1,0:T(8,128)(2,1)}), bf16[8,3,144,128]{3,2,1,0:T(8,128)(2,1)S(1)}, u32[]{:S(2)}, u32[]{:S(2)}) async-start(bf16[8,3,144,128]{3,2,1,0:T(8,128)(2,1)} %collective-permute-done.6), calls=%async_computation.3 | async-start | bytes 1769472 | tf_op jit(solution)/shard_map/all_to_all | solution.py:235
  47.0 65.9 %collective-permute-start.8 = (bf16[8,2,144,128]{3,2,1,0:T(8,128)(2,1)S(1)}, bf16[8,2,144,128]{3,2,1,0:T(8,128)(2,1)}, u32[]{:S(2)}, u32[]{:S(2)}) collective-permute-start(bf16[8,2,144,128]{3,2,1,0:T(8,128)(2,1)S(1)} %slice.9), channel_id=1, source_target_pairs={{0,64},{8,72},{16,80},{24,88},{32,96},{40,104},{48,112},{56,120},{... | collective-permute-start | bytes 1769480 | tf_op jit(solution)/shard_map/ppermute | solution.py:232
  52.9 73.0 %collective-permute-start.5 = (bf16[8,3,144,128]{3,2,1,0:T(8,128)(2,1)S(1)}, bf16[8,3,144,128]{3,2,1,0:T(8,128)(2,1)}, u32[]{:S(2)}, u32[]{:S(2)}) collective-permute-start(bf16[8,3,144,128]{3,2,1,0:T(8,128)(2,1)S(1)} %all-to-all-done.2.refs_1_.refs_12_), channel_id=1, source_target_pairs={{8,0},{16,8},{24,16},{32,24},{40,32},{48,40},{56,48},{72,64},{80,7... | collective-permute-start | bytes 2654216 | tf_op jit(solution)/shard_map/ppermute | solution.py:232
  70.9 61.7 %collective-permute-start.4 = (bf16[8,3,144,128]{3,2,1,0:T(8,128)(2,1)S(1)}, bf16[8,3,144,128]{3,2,1,0:T(8,128)(2,1)}, u32[]{:S(2)}, u32[]{:S(2)}) collective-permute-start(bf16[8,3,144,128]{3,2,1,0:T(8,128)(2,1)S(1)} %all-to-all-done.2.refs_1_.refs_12_), channel_id=1, source_target_pairs={{0,8},{8,16},{16,24},{24,32},{32,40},{40,48},{48,56},{64,72},{72,8... | collective-permute-start | bytes 2654216 | tf_op jit(solution)/shard_map/ppermute | solution.py:232
  73.7 37.2 %collective-permute-start.2 = (bf16[8,1,144,128]{3,2,1,0:T(8,128)(2,1)S(1)}, bf16[8,1,144,128]{3,2,1,0:T(8,128)(2,1)}, u32[]{:S(2)}, u32[]{:S(2)}) collective-permute-start(bf16[8,1,144,128]{3,2,1,0:T(8,128)(2,1)S(1)} %slice.8), channel_id=1, source_target_pairs={{0,64},{8,72},{16,80},{24,88},{32,96},{40,104},{48,112},{56,120},{... | collective-permute-start | bytes 884744 | tf_op jit(solution)/shard_map/ppermute | solution.py:232
  74.0 44.9 %copy-start.2 = (bf16[8,3,144,128]{3,2,1,0:T(8,128)(2,1)}, bf16[8,3,144,128]{3,2,1,0:T(8,128)(2,1)S(1)}, u32[]{:S(2)}) copy-start(bf16[8,3,144,128]{3,2,1,0:T(8,128)(2,1)S(1)} %all-to-all-done.3.refs_4_.refs_8_) | copy-start | bytes 2654212
  74.0 67.5 %collective-permute-start.7 = (bf16[8,3,144,128]{3,2,1,0:T(8,128)(2,1)S(1)}, bf16[8,3,144,128]{3,2,1,0:T(8,128)(2,1)}, u32[]{:S(2)}, u32[]{:S(2)}) collective-permute-start(bf16[8,3,144,128]{3,2,1,0:T(8,128)(2,1)S(1)} %all-to-all-done.3.refs_4_.refs_8_), channel_id=1, source_target_pairs={{0,128},{8,136},{16,144},{24,152},{32,160},{40,168},{48,176},{56,1... | collective-permute-start | bytes 2654216 | tf_op jit(solution)/shard_map/ppermute | solution.py:232
  111.0 38.3 %collective-permute-start.1 = (bf16[8,3,144,128]{3,2,1,0:T(8,128)(2,1)S(1)}, bf16[8,3,144,128]{3,2,1,0:T(8,128)(2,1)}, u32[]{:S(2)}, u32[]{:S(2)}) collective-permute-start(bf16[8,3,144,128]{3,2,1,0:T(8,128)(2,1)S(1)} %all_to_all.25.refs_1_), channel_id=1, source_target_pairs={{8,0},{16,8},{24,16},{32,24},{40,32},{48,40},{56,48},{72,64},{80,7... | collective-permute-start | bytes 2654216 | tf_op jit(solution)/shard_map/ppermute | solution.py:232
  112.9 36.3 %collective-permute-start = (bf16[8,3,144,128]{3,2,1,0:T(8,128)(2,1)S(1)}, bf16[8,3,144,128]{3,2,1,0:T(8,128)(2,1)}, u32[]{:S(2)}, u32[]{:S(2)}) collective-permute-start(bf16[8,3,144,128]{3,2,1,0:T(8,128)(2,1)S(1)} %all_to_all.25.refs_1_), channel_id=1, source_target_pairs={{0,8},{8,16},{16,24},{24,32},{32,40},{40,48},{48,56},{64,72},{72,8... | collective-permute-start | bytes 2654216 | tf_op jit(solution)/shard_map/ppermute | solution.py:232
  118.9 22.6 %all-to-all-start = ((bf16[8,3,144,128]{3,2,1,0:T(8,128)(2,1)}), bf16[8,3,144,128]{3,2,1,0:T(8,128)(2,1)S(1)}, u32[]{:S(2)}, u32[]{:S(2)}) async-start(bf16[8,3,144,128]{3,2,1,0:T(8,128)(2,1)} %pack.3), calls=%async_computation | async-start | bytes 1769472 | tf_op jit(solution)/shard_map/all_to_all | solution.py:235
  125.9 23.4 %collective-permute-start.9 = (bf16[8,2,144,128]{3,2,1,0:T(8,128)(2,1)}, bf16[8,2,144,128]{3,2,1,0:T(8,128)(2,1)}, u32[]{:S(2)}, u32[]{:S(2)}) collective-permute-start(bf16[8,2,144,128]{3,2,1,0:T(8,128)(2,1)} %collective-permute-done.8.refs_11_), channel_id=1, source_target_pairs={{0,129},{1,128},{2,131},{3,130},{4,133},{5,132},{6,135},{7,134},{8... | collective-permute-start | bytes 1769480 | tf_op jit(solution)/shard_map/ppermute | solution.py:266
  131.4 0.7 copy-start.6
  132.6 16.6 %collective-permute-start.3 = (bf16[8,1,144,128]{3,2,1,0:T(8,128)(2,1)}, bf16[8,1,144,128]{3,2,1,0:T(8,128)(2,1)S(1)}, u32[]{:S(2)}, u32[]{:S(2)}) collective-permute-start(bf16[8,1,144,128]{3,2,1,0:T(8,128)(2,1)} %collective-permute-done.2.refs_4_), channel_id=1, source_target_pairs={{0,128},{8,136},{16,144},{24,152},{32,160},{40,168},{48,176},{56,1... | collective-permute-start | bytes 884744 | tf_op jit(solution)/shard_map/ppermute | solution.py:232
  141.4 0.9 copy-start.3
  149.2 0.7 copy-start.5

commit v9 on v7

--- a/solution.py
+++ b/solution.py
@@ -16,6 +16,10 @@
 
 
 ANY = pl.BlockSpec(memory_space=pl.ANY)
+
+
+def after(value, *first):
+    return lax.optimization_barrier((value,) + first)[0]
 
 
 def lane(g, head, local, swap):
@@ -251,8 +255,8 @@
     rest = exchange(rest)
     most = pack(swap, [keys, values, query], [(2, 0), (2, 1), (2, 2), (0, 0), (1, 0), (0, 1)], groups)
     most = exchange(most)
-    far_1 = send(rest[:, 0:1], across)
-    far_2 = send(rest[:, 1:3], across)
+    far_1 = send(after(rest[:, 0:1], crossed), across)
+    far_2 = send(after(rest[:, 1:3], crossed), across)
     crossed = exchange(crossed)
     before_a = send(rest, right)
     behind_a = send(rest, left)

time: 192 us -> 192 us (level)
  no operation moved by 1% of the time
where the time goes in v9:
time: 192 us; the launch traced here: 191 us
  waiting for transfers between devices  82.1 us (43%)
  starting transfers between devices  52.5 us (27%)
  Pallas kernels  27 us (14%)
  blocking collectives  24 us (12%)
  local copies, waits for them, and re-layouts  4.46 us (2%)
    ppermute x9, waiting for transfers between devices, send(): return lax.ppermute(x, 'seq', pairs)  68.6 us
    ppermute x9, starting transfers between devices, send(): return lax.ppermute(x, 'seq', pairs)  34.6 us
    all_to_all x1, blocking collectives, exchange(): return lax.all_to_all(x, 'head', split_axis=0, concat_axis=0, tiled=True)  24 us
    pallas_call x2, Pallas kernels, attend(): pl.pallas_call(functools.partial(attend_kernel, tile, per_slab, plan, out...  17.1 us
    all_to_all x3, starting transfers between devices, exchange(): return lax.all_to_all(x, 'head', split_axis=0, concat_axis=0, tiled=True)  16.6 us
    all_to_all x3, waiting for transfers between devices, exchange(): return lax.all_to_all(x, 'head', split_axis=0, concat_axis=0, tiled=True)  12.3 us
    pallas_call x3, Pallas kernels, pack(): pl.pallas_call(functools.partial(pack_kernel, picks, width // (groups * H...  7.72 us
  transfers between devices with their start and end apart: 13, of which 5 were waited for; matrix products, arithmetic and copies ran while one was open for 2% of the time, Pallas kernels for 6%

profile of v9, /device:TPU:2, one launch (start us, length us, event | category | flops | bytes accessed | tf_op | source)
XLA Modules:
  0.0 191.4 jit_solution(5748489809708583350)
XLA Ops:
  0.0 2.3 %pack.4 = bf16[8,3,144,128]{3,2,1,0:T(8,128)(2,1)} custom-call(s32[1]{0:T(128)} %bitcast.swap_ref, bf16[144,3072]{1,0:T(8,128)(2,1)} %refs_0_.5, bf16[144,3072]{1,0:T(8,128)(2,1)} %refs_1_.5), custom_call_target="tpu_custom_call" | custom-call | bytes 1769472 | tf_op jit(solution)/shard_map/pack/pallas_call | solution.py:46
  2.3 6.0 %all-to-all-start.1 = ((bf16[8,3,144,128]{3,2,1,0:T(8,128)(2,1)}), bf16[8,3,144,128]{3,2,1,0:T(8,128)(2,1)S(1)}, u32[]{:S(2)}, u32[]{:S(2)}) async-start(bf16[8,3,144,128]{3,2,1,0:T(8,128)(2,1)} %pack.4), calls=%async_computation.1 | async-start | bytes 1769472 | tf_op jit(solution)/shard_map/all_to_all | solution.py:235
  8.3 3.1 %pack.3 = bf16[8,6,144,128]{3,2,1,0:T(8,128)(2,1)} custom-call(s32[1]{0:T(128)} %bitcast.swap_ref, bf16[144,3072]{1,0:T(8,128)(2,1)} %refs_0_.5, bf16[144,3072]{1,0:T(8,128)(2,1)} %refs_1_.5, bf16[144,3072]{1,0:T(8,128)(2,1)} %refs_2_.1), custom_call_target="tpu_custom_call" | custom-call | bytes 3538944 | tf_op jit(solution)/shard_map/pack/pallas_call | solution.py:46
  11.5 12.3 %all-to-all-done.1.refs_1_ = bf16[8,3,144,128]{3,2,1,0:T(8,128)(2,1)S(1)} async-done(((bf16[8,3,144,128]{3,2,1,0:T(8,128)(2,1)}), bf16[8,3,144,128]{3,2,1,0:T(8,128)(2,1)S(1)}, u32[]{:S(2)}, u32[]{:S(2)}) %all-to-all-start.1) | async-done | bytes 884768 | tf_op jit(solution)/shard_map/all_to_all | solution.py:235
  23.8 3.6 %all-to-all-start = ((bf16[8,6,144,128]{3,2,1,0:T(8,128)(2,1)}), bf16[8,6,144,128]{3,2,1,0:T(8,128)(2,1)S(1)}, u32[]{:S(2)}, u32[]{:S(2)}) async-start(bf16[8,6,144,128]{3,2,1,0:T(8,128)(2,1)} %pack.3), calls=%async_computation | async-start | bytes 3538944 | tf_op jit(solution)/shard_map/all_to_all | solution.py:235
  27.4 2.3 %pack.5 = bf16[8,3,144,128]{3,2,1,0:T(8,128)(2,1)} custom-call(s32[1]{0:T(128)} %bitcast.swap_ref, bf16[144,3072]{1,0:T(8,128)(2,1)} %refs_0_.5, bf16[144,3072]{1,0:T(8,128)(2,1)} %refs_1_.5), custom_call_target="tpu_custom_call" | custom-call | bytes 1769472 | tf_op jit(solution)/shard_map/pack/pallas_call | solution.py:46
  29.7 7.3 %collective-permute-start.2 = (bf16[8,3,144,128]{3,2,1,0:T(8,128)(2,1)}, bf16[8,3,144,128]{3,2,1,0:T(8,128)(2,1)S(1)}, u32[]{:S(2)}, u32[]{:S(2)}) collective-permute-start(bf16[8,3,144,128]{3,2,1,0:T(8,128)(2,1)} %pack.5), channel_id=1, source_target_pairs={{0,64},{8,72},{16,80},{24,88},{32,96},{40,104},{48,112},{56,120},{... | collective-permute-start | bytes 2654216 | tf_op jit(solution)/shard_map/ppermute | solution.py:232
  37.0 36.6 %collective-permute-done.2 = bf16[8,3,144,128]{3,2,1,0:T(8,128)(2,1)S(1)} collective-permute-done((bf16[8,3,144,128]{3,2,1,0:T(8,128)(2,1)}, bf16[8,3,144,128]{3,2,1,0:T(8,128)(2,1)S(1)}, u32[]{:S(2)}, u32[]{:S(2)}) %collective-permute-start.2) | collective-permute-done | bytes 884768 | tf_op jit(solution)/shard_map/ppermute | solution.py:232
  74.5 6.9 %all-to-all-start.2 = ((bf16[8,3,144,128]{3,2,1,0:T(8,128)(2,1)}), bf16[8,3,144,128]{3,2,1,0:T(8,128)(2,1)S(1)}, u32[]{:S(2)}, u32[]{:S(2)}) async-start(bf16[8,3,144,128]{3,2,1,0:T(8,128)(2,1)} %copy-done.5), calls=%async_computation.2 | async-start | bytes 1769472 | tf_op jit(solution)/shard_map/all_to_all | solution.py:235
  82.3 6.5 %collective-permute-start.8 = (bf16[8,2,144,128]{3,2,1,0:T(8,128)(2,1)}, bf16[8,2,144,128]{3,2,1,0:T(8,128)(2,1)}, u32[]{:S(2)}, u32[]{:S(2)}) collective-permute-start(bf16[8,2,144,128]{3,2,1,0:T(8,128)(2,1)} %slice.14), channel_id=1, source_target_pairs={{0,64},{8,72},{16,80},{24,88},{32,96},{40,104},{48,112},{56,120},{... | collective-permute-start | bytes 1769480 | tf_op jit(solution)/shard_map/ppermute | solution.py:232
  89.8 1.3 collective-permute-start.6
  91.0 3.1 %collective-permute-start.5 = (bf16[8,3,144,128]{3,2,1,0:T(8,128)(2,1)}, bf16[8,3,144,128]{3,2,1,0:T(8,128)(2,1)S(1)}, u32[]{:S(2)}, u32[]{:S(2)}) collective-permute-start(bf16[8,3,144,128]{3,2,1,0:T(8,128)(2,1)} %slice.13), channel_id=1, source_target_pairs={{0,8},{8,16},{16,24},{24,32},{32,40},{40,48},{48,56},{64,72},{72,8... | collective-permute-start | bytes 2654216 | tf_op jit(solution)/shard_map/ppermute | solution.py:232
  94.9 1.3 collective-permute-start.7
  96.2 26.3 %collective-permute-done.3.refs_4_ = bf16[8,1,144,128]{3,2,1,0:T(8,128)(2,1)} collective-permute-done((bf16[8,1,144,128]{3,2,1,0:T(8,128)(2,1)}, bf16[8,1,144,128]{3,2,1,0:T(8,128)(2,1)}, u32[]{:S(2)}, u32[]{:S(2)}) %collective-permute-start.3) | collective-permute-done | bytes 294944 | tf_op jit(solution)/shard_map/ppermute | solution.py:232
  122.5 1.3 collective-permute-start.1
  123.8 12.5 %collective-permute-start = (bf16[8,3,144,128]{3,2,1,0:T(8,128)(2,1)S(1)}, bf16[8,3,144,128]{3,2,1,0:T(8,128)(2,1)}, u32[]{:S(2)}, u32[]{:S(2)}) collective-permute-start(bf16[8,3,144,128]{3,2,1,0:T(8,128)(2,1)S(1)} %all-to-all-done.1.refs_1_), channel_id=1, source_target_pairs={{0,8},{8,16},{16,24},{24,32},{32,40},{40,48},{48,56},{64,72},{72,8... | collective-permute-start | bytes 2654216 | tf_op jit(solution)/shard_map/ppermute | solution.py:232
  136.3 1.3 collective-permute-start.9
  138.2 1.5 collective-permute-start.4
  141.2 6.9 %attend.2.refs_12_ = bf16[8,3,144,128]{3,2,1,0:T(8,128)(2,1)} custom-call(s32[3,5]{1,0:T(4,128)} %fusion.1.idx_ref, s32[3,5]{1,0:T(4,128)} %fusion.4.live_ref, bf16[8,6,144,128]{3,2,1,0:T(8,128)(2,1)} %copy-done, bf16[8,3,144,128]{3,2,1,0:T(8,128)(2,1)} %copy-done.3, bf16[8,3,144,128]{3,2,1,0:T(8,128)(2,1)} %collective-permute-done.6.refs_2_.refs_7_, ...), custom_call_target="tpu_custom_call" | custom-call | flops 1132462080 | bytes 3538944 | tf_op jit(solution)/shard_map/attend/pallas_call | solution.py:190
  148.0 5.7 %collective-permute-done.4.refs_5_ = bf16[8,1,144,128]{3,2,1,0:T(8,128)(2,1)} collective-permute-done((bf16[8,1,144,128]{3,2,1,0:T(8,128)(2,1)}, bf16[8,1,144,128]{3,2,1,0:T(8,128)(2,1)}, u32[]{:S(2)}, u32[]{:S(2)}) %collective-permute-start.4) | collective-permute-done | bytes 294944 | tf_op jit(solution)/shard_map/ppermute | solution.py:232
  153.7 1.2 collective-permute-done.9.refs_10_
  154.9 10.2 %attend.3 = bf16[8,3,144,128]{3,2,1,0:T(8,128)(2,1)} custom-call(s32[3,5]{1,0:T(4,128)} %fusion.1.idx_ref, s32[3,5]{1,0:T(4,128)} %fusion.4.live_ref, bf16[8,6,144,128]{3,2,1,0:T(8,128)(2,1)} %copy-done, bf16[8,3,144,128]{3,2,1,0:T(8,128)(2,1)} %copy-done.1, bf16[8,3,144,128]{3,2,1,0:T(8,128)(2,1)} %collective-permute-done.refs_2_, ...), custom_call_target="tpu_custom_call", output_to_operand_aliasing={{}: (14, {})} | custom-call | flops 2264924160 | bytes 7077888 | tf_op jit(solution)/shard_map/attend/pallas_call | solution.py:190
  165.1 24.0 %all_to_all.20.part = bf16[8,3,144,128]{3,2,1,0:T(8,128)(2,1)} all-to-all(bf16[8,3,144,128]{3,2,1,0:T(8,128)(2,1)} %attend.3), channel_id=1, replica_groups=mesh['seq'=32,'head'=8] {'head'}, dimensions={0} | all-to-all | bytes 1769472 | tf_op jit(solution)/shard_map/all_to_all | solution.py:235
  189.1 2.2 %unpack.1 = bf16[144,3072]{1,0:T(8,128)(2,1)} custom-call(s32[1]{0:T(128)} %bitcast.swap_ref, bf16[8,3,144,128]{3,2,1,0:T(8,128)(2,1)} %all_to_all.20.part), custom_call_target="tpu_custom_call" | custom-call | bytes 1769472 | tf_op jit(solution)/shard_map/unpack/pallas_call | solution.py:85
  (28 shorter events, 5.6 us)
Async XLA Ops:
  2.3 21.5 %all-to-all-start.1 = ((bf16[8,3,144,128]{3,2,1,0:T(8,128)(2,1)}), bf16[8,3,144,128]{3,2,1,0:T(8,128)(2,1)S(1)}, u32[]{:S(2)}, u32[]{:S(2)}) async-start(bf16[8,3,144,128]{3,2,1,0:T(8,128)(2,1)} %pack.4), calls=%async_computation.1 | async-start | bytes 1769472 | tf_op jit(solution)/shard_map/all_to_all | solution.py:235
  23.8 100.0 %copy-start.1 = (bf16[8,3,144,128]{3,2,1,0:T(8,128)(2,1)}, bf16[8,3,144,128]{3,2,1,0:T(8,128)(2,1)S(1)}, u32[]{:S(2)}) copy-start(bf16[8,3,144,128]{3,2,1,0:T(8,128)(2,1)S(1)} %all-to-all-done.1.refs_1_) | copy-start | bytes 2654212
  23.8 50.7 %all-to-all-start = ((bf16[8,6,144,128]{3,2,1,0:T(8,128)(2,1)}), bf16[8,6,144,128]{3,2,1,0:T(8,128)(2,1)S(1)}, u32[]{:S(2)}, u32[]{:S(2)}) async-start(bf16[8,6,144,128]{3,2,1,0:T(8,128)(2,1)} %pack.3), calls=%async_computation | async-start | bytes 3538944 | tf_op jit(solution)/shard_map/all_to_all | solution.py:235
  29.7 43.9 %collective-permute-start.2 = (bf16[8,3,144,128]{3,2,1,0:T(8,128)(2,1)}, bf16[8,3,144,128]{3,2,1,0:T(8,128)(2,1)S(1)}, u32[]{:S(2)}, u32[]{:S(2)}) collective-permute-start(bf16[8,3,144,128]{3,2,1,0:T(8,128)(2,1)} %pack.5), channel_id=1, source_target_pairs={{0,64},{8,72},{16,80},{24,88},{32,96},{40,104},{48,112},{56,120},{... | collective-permute-start | bytes 2654216 | tf_op jit(solution)/shard_map/ppermute | solution.py:232
  73.6 0.9 copy-start.5
  74.5 15.3 %copy-start = (bf16[8,6,144,128]{3,2,1,0:T(8,128)(2,1)}, bf16[8,6,144,128]{3,2,1,0:T(8,128)(2,1)S(1)}, u32[]{:S(2)}) copy-start(bf16[8,6,144,128]{3,2,1,0:T(8,128)(2,1)S(1)} %all-to-all-done.refs_0_) | copy-start | bytes 5308420
  74.5 20.4 %all-to-all-start.2 = ((bf16[8,3,144,128]{3,2,1,0:T(8,128)(2,1)}), bf16[8,3,144,128]{3,2,1,0:T(8,128)(2,1)S(1)}, u32[]{:S(2)}, u32[]{:S(2)}) async-start(bf16[8,3,144,128]{3,2,1,0:T(8,128)(2,1)} %copy-done.5), calls=%async_computation.2 | async-start | bytes 1769472 | tf_op jit(solution)/shard_map/all_to_all | solution.py:235
  81.4 56.1 %copy-start.6 = (s32[3,5]{1,0:T(4,128)S(1)}, s32[3,5]{1,0:T(4,128)}, u32[]{:S(2)}) copy-start(s32[3,5]{1,0:T(4,128)} %param.7) | copy-start | bytes 184
  82.3 41.5 %collective-permute-start.8 = (bf16[8,2,144,128]{3,2,1,0:T(8,128)(2,1)}, bf16[8,2,144,128]{3,2,1,0:T(8,128)(2,1)}, u32[]{:S(2)}, u32[]{:S(2)}) collective-permute-start(bf16[8,2,144,128]{3,2,1,0:T(8,128)(2,1)} %slice.14), channel_id=1, source_target_pairs={{0,64},{8,72},{16,80},{24,88},{32,96},{40,104},{48,112},{56,120},{... | collective-permute-start | bytes 1769480 | tf_op jit(solution)/shard_map/ppermute | solution.py:232
  89.8 46.5 %collective-permute-start.6 = (bf16[8,3,144,128]{3,2,1,0:T(8,128)(2,1)}, bf16[8,3,144,128]{3,2,1,0:T(8,128)(2,1)}, u32[]{:S(2)}, u32[]{:S(2)}) collective-permute-start(bf16[8,3,144,128]{3,2,1,0:T(8,128)(2,1)} %slice.13), channel_id=1, source_target_pairs={{8,0},{16,8},{24,16},{32,24},{40,32},{48,40},{56,48},{72,64},{80,7... | collective-permute-start | bytes 2654216 | tf_op jit(solution)/shard_map/ppermute | solution.py:232
  91.0 47.1 %collective-permute-start.5 = (bf16[8,3,144,128]{3,2,1,0:T(8,128)(2,1)}, bf16[8,3,144,128]{3,2,1,0:T(8,128)(2,1)S(1)}, u32[]{:S(2)}, u32[]{:S(2)}) collective-permute-start(bf16[8,3,144,128]{3,2,1,0:T(8,128)(2,1)} %slice.13), channel_id=1, source_target_pairs={{0,8},{8,16},{16,24},{24,32},{32,40},{40,48},{48,56},{64,72},{72,8... | collective-permute-start | bytes 2654216 | tf_op jit(solution)/shard_map/ppermute | solution.py:232
  94.9 27.6 %collective-permute-start.3 = (bf16[8,1,144,128]{3,2,1,0:T(8,128)(2,1)}, bf16[8,1,144,128]{3,2,1,0:T(8,128)(2,1)}, u32[]{:S(2)}, u32[]{:S(2)}) collective-permute-start(bf16[8,1,144,128]{3,2,1,0:T(8,128)(2,1)} %slice.12), channel_id=1, source_target_pairs={{0,64},{8,72},{16,80},{24,88},{32,96},{40,104},{48,112},{56,120},{... | collective-permute-start | bytes 884744 | tf_op jit(solution)/shard_map/ppermute | solution.py:232
  94.9 45.3 %copy-start.2 = (bf16[8,3,144,128]{3,2,1,0:T(8,128)(2,1)}, bf16[8,3,144,128]{3,2,1,0:T(8,128)(2,1)S(1)}, u32[]{:S(2)}) copy-start(bf16[8,3,144,128]{3,2,1,0:T(8,128)(2,1)S(1)} %all-to-all-done.2.refs_3_.refs_8_) | copy-start | bytes 2654212
  94.9 45.3 %collective-permute-start.7 = (bf16[8,3,144,128]{3,2,1,0:T(8,128)(2,1)S(1)}, bf16[8,3,144,128]{3,2,1,0:T(8,128)(2,1)S(1)}, u32[]{:S(2)}, u32[]{:S(2)}) collective-permute-start(bf16[8,3,144,128]{3,2,1,0:T(8,128)(2,1)S(1)} %all-to-all-done.2.refs_3_.refs_8_), channel_id=1, source_target_pairs={{0,128},{8,136},{16,144},{24,152},{32,160},{40,168},{48,176},{56,1... | collective-permute-start | bytes 2654216 | tf_op jit(solution)/shard_map/ppermute | solution.py:232
  122.5 31.3 %collective-permute-start.1 = (bf16[8,3,144,128]{3,2,1,0:T(8,128)(2,1)S(1)}, bf16[8,3,144,128]{3,2,1,0:T(8,128)(2,1)}, u32[]{:S(2)}, u32[]{:S(2)}) collective-permute-start(bf16[8,3,144,128]{3,2,1,0:T(8,128)(2,1)S(1)} %all-to-all-done.1.refs_1_), channel_id=1, source_target_pairs={{8,0},{16,8},{24,16},{32,24},{40,32},{48,40},{56,48},{72,64},{80,7... | collective-permute-start | bytes 2654216 | tf_op jit(solution)/shard_map/ppermute | solution.py:232
  123.8 30.0 %collective-permute-start = (bf16[8,3,144,128]{3,2,1,0:T(8,128)(2,1)S(1)}, bf16[8,3,144,128]{3,2,1,0:T(8,128)(2,1)}, u32[]{:S(2)}, u32[]{:S(2)}) collective-permute-start(bf16[8,3,144,128]{3,2,1,0:T(8,128)(2,1)S(1)} %all-to-all-done.1.refs_1_), channel_id=1, source_target_pairs={{0,8},{8,16},{16,24},{24,32},{32,40},{40,48},{48,56},{64,72},{72,8... | collective-permute-start | bytes 2654216 | tf_op jit(solution)/shard_map/ppermute | solution.py:232
  136.3 18.7 %collective-permute-start.9 = (bf16[8,2,144,128]{3,2,1,0:T(8,128)(2,1)}, bf16[8,2,144,128]{3,2,1,0:T(8,128)(2,1)}, u32[]{:S(2)}, u32[]{:S(2)}) collective-permute-start(bf16[8,2,144,128]{3,2,1,0:T(8,128)(2,1)} %collective-permute-done.8.refs_11_), channel_id=1, source_target_pairs={{0,129},{1,128},{2,131},{3,130},{4,133},{5,132},{6,135},{7,134},{8... | collective-permute-start | bytes 1769480 | tf_op jit(solution)/shard_map/ppermute | solution.py:266
  138.2 2.0 %copy-start.3 = (bf16[8,3,144,128]{3,2,1,0:T(8,128)(2,1)}, bf16[8,3,144,128]{3,2,1,0:T(8,128)(2,1)S(1)}, u32[]{:S(2)}) copy-start(bf16[8,3,144,128]{3,2,1,0:T(8,128)(2,1)S(1)} %collective-permute-done.5.refs_1_.refs_6_) | copy-start | bytes 2654212
  138.2 15.6 %collective-permute-start.4 = (bf16[8,1,144,128]{3,2,1,0:T(8,128)(2,1)}, bf16[8,1,144,128]{3,2,1,0:T(8,128)(2,1)}, u32[]{:S(2)}, u32[]{:S(2)}) collective-permute-start(bf16[8,1,144,128]{3,2,1,0:T(8,128)(2,1)} %collective-permute-done.3.refs_4_), channel_id=1, source_target_pairs={{0,128},{8,136},{16,144},{24,152},{32,160},{40,168},{48,176},{56,1... | collective-permute-start | bytes 884744 | tf_op jit(solution)/shard_map/ppermute | solution.py:232
  140.2 0.9 copy-start.4

commit v10 on v9

--- a/solution.py
+++ b/solution.py
@@ -258,23 +258,30 @@
     far_1 = send(after(rest[:, 0:1], crossed), across)
     far_2 = send(after(rest[:, 1:3], crossed), across)
     crossed = exchange(crossed)
-    before_a = send(rest, right)
-    behind_a = send(rest, left)
-    own = most[:, 3:6]
-    before_b = send(own, right)
-    behind_b = send(own, left)
+    own = [most[:, 3:5], jnp.concatenate([most[:, 5:6], rest[:, 0:1]], axis=1), rest[:, 1:3]]
+    before, behind = [None] * local, [None] * local
+    for i in range(local):
+        before[i] = send(own[i], right)
+        behind[i] = send(own[i], left)
     second_2 = lax.ppermute(far_2, ("seq", "head"), hop)
     second_1 = send(far_1, middle)
     second_b = send(crossed, middle)
     parts = local
-    plan_0 = [[((0, 0),), ((0, 3), (0, 4)), ((1, 0), (1, 1)), ((2, 0), (2, 1)), ((3, 0), (3, 1)), ((4, 0), (4, 1))]]
-    o = attend(idx, live, [most, before_b, behind_b, crossed, second_b], plan_0, (0,), parts)
-    sources = [most, rest, before_a, behind_a, far_1, second_1, before_b, behind_b, crossed, second_b, second_2, far_2]
-    plan = [
-        [((0, 1),), ((0, 5), (1, 0)), ((6, 2), (2, 0)), ((7, 2), (3, 0)), ((8, 2), (4, 0)), ((9, 2), (5, 0))],
-        [((0, 2),), ((1, 1), (1, 2)), ((2, 1), (2, 2)), ((3, 1), (3, 2)), ((11, 0), (11, 1)), ((10, 0), (10, 1))],
+
+    def both(source, first=0):
+        return ((source, first), (source, first + 1))
+
+    takes = [
+        ([most, before[0], behind[0], crossed, second_b], [both(0, 3), both(1), both(2), both(3), both(4)]),
+        (
+            [most, before[1], behind[1], rest, crossed, far_1, second_b, second_1],
+            [((0, 5), (3, 0)), both(1), both(2), ((4, 2), (5, 0)), ((6, 2), (7, 0))],
+        ),
+        ([most, before[2], behind[2], rest, far_2, second_2], [both(3, 1), both(1), both(2), both(4), both(5)]),
     ]
-    o = attend(idx, live, sources, plan, (1, 2), parts, o)
+    o = None
+    for i, (sources, places) in enumerate(takes):
+        o = attend(idx, live, sources, [[((0, i),)] + places], (i,), parts, o)
     o = exchange(o)
     return unpack(swap, o)
 

time: 192 us -> 182 us (0.948)
  the two profiles are of different devices: /device:TPU:2 before, /device:TPU:32 now
where the time goes in v10:
time: 182 us; the launch traced here: 178 us
  starting transfers between devices  51.9 us (29%)
  waiting for transfers between devices  47 us (26%)
  blocking collectives  42.1 us (23%)
  Pallas kernels  30.5 us (17%)
  local copies, waits for them, and re-layouts  3.37 us (2%)
  other arithmetic  2.97 us (2%)
    all_to_all x2, blocking collectives, exchange(): return lax.all_to_all(x, 'head', split_axis=0, concat_axis=0, tiled=True)  42.1 us
    ppermute x11, starting transfers between devices, send(): return lax.ppermute(x, 'seq', pairs)  35 us
    all_to_all x2, waiting for transfers between devices, exchange(): return lax.all_to_all(x, 'head', split_axis=0, concat_axis=0, tiled=True)  26.8 us
    pallas_call x3, Pallas kernels, attend(): pl.pallas_call(functools.partial(attend_kernel, tile, per_slab, plan, out...  20.6 us
    ppermute x11, waiting for transfers between devices, send(): return lax.ppermute(x, 'seq', pairs)  20.2 us
    all_to_all x2, starting transfers between devices, exchange(): return lax.all_to_all(x, 'head', split_axis=0, concat_axis=0, tiled=True)  10.5 us
    pallas_call x3, Pallas kernels, pack(): pl.pallas_call(functools.partial(pack_kernel, picks, width // (groups * H...  7.71 us
    ppermute x1, starting transfers between devices, body(): second_2 = lax.ppermute(far_2, ('seq', 'head'), hop)  6.39 us
  transfers between devices with their start and end apart: 14, of which 4 were waited for; matrix products, arithmetic and copies ran while one was open for 3% of the time, Pallas kernels for 11%

profile of v10, /device:TPU:32, one launch (start us, length us, event | category | flops | bytes accessed | tf_op | source)
XLA Modules:
  0.0 178.3 jit_solution(3733697853808414422)
XLA Ops:
  0.0 2.3 %pack.5 = bf16[8,3,144,128]{3,2,1,0:T(8,128)(2,1)} custom-call(s32[1]{0:T(128)} %bitcast.swap_ref, bf16[144,3072]{1,0:T(8,128)(2,1)} %refs_0_.5, bf16[144,3072]{1,0:T(8,128)(2,1)} %refs_1_.5), custom_call_target="tpu_custom_call" | custom-call | bytes 1769472 | tf_op jit(solution)/shard_map/pack/pallas_call | solution.py:46
  2.3 6.4 %collective-permute-start.2 = (bf16[8,3,144,128]{3,2,1,0:T(8,128)(2,1)}, bf16[8,3,144,128]{3,2,1,0:T(8,128)(2,1)}, u32[]{:S(2)}, u32[]{:S(2)}) collective-permute-start(bf16[8,3,144,128]{3,2,1,0:T(8,128)(2,1)} %pack.5), channel_id=1, source_target_pairs={{0,64},{8,72},{16,80},{24,88},{32,96},{40,104},{48,112},{56,120},{... | collective-permute-start | bytes 2654216 | tf_op jit(solution)/shard_map/ppermute | solution.py:232
  8.7 2.3 %pack.4 = bf16[8,3,144,128]{3,2,1,0:T(8,128)(2,1)} custom-call(s32[1]{0:T(128)} %bitcast.swap_ref, bf16[144,3072]{1,0:T(8,128)(2,1)} %refs_0_.5, bf16[144,3072]{1,0:T(8,128)(2,1)} %refs_1_.5), custom_call_target="tpu_custom_call" | custom-call | bytes 1769472 | tf_op jit(solution)/shard_map/pack/pallas_call | solution.py:46
  11.0 22.2 %all_to_all.20.refs_3_ = bf16[8,3,144,128]{3,2,1,0:T(8,128)(2,1)S(1)} all-to-all(bf16[8,3,144,128]{3,2,1,0:T(8,128)(2,1)} %pack.4), channel_id=1, replica_groups=mesh['seq'=32,'head'=8] {'head'}, dimensions={0} | all-to-all | bytes 1769472 | tf_op jit(solution)/shard_map/all_to_all | solution.py:235
  33.2 14.6 %collective-permute-done.2 = bf16[8,3,144,128]{3,2,1,0:T(8,128)(2,1)} collective-permute-done((bf16[8,3,144,128]{3,2,1,0:T(8,128)(2,1)}, bf16[8,3,144,128]{3,2,1,0:T(8,128)(2,1)}, u32[]{:S(2)}, u32[]{:S(2)}) %collective-permute-start.2) | collective-permute-done | bytes 884768 | tf_op jit(solution)/shard_map/ppermute | solution.py:232
  47.8 6.9 %all-to-all-start.2 = ((bf16[8,3,144,128]{3,2,1,0:T(8,128)(2,1)}), bf16[8,3,144,128]{3,2,1,0:T(8,128)(2,1)S(1)}, u32[]{:S(2)}, u32[]{:S(2)}) async-start(bf16[8,3,144,128]{3,2,1,0:T(8,128)(2,1)} %collective-permute-done.2), calls=%async_computation.2 | async-start | bytes 1769472 | tf_op jit(solution)/shard_map/all_to_all | solution.py:235
  54.7 3.1 %pack.3 = bf16[8,6,144,128]{3,2,1,0:T(8,128)(2,1)} custom-call(s32[1]{0:T(128)} %bitcast.swap_ref, bf16[144,3072]{1,0:T(8,128)(2,1)} %refs_0_.5, bf16[144,3072]{1,0:T(8,128)(2,1)} %refs_1_.5, bf16[144,3072]{1,0:T(8,128)(2,1)} %refs_2_.1), custom_call_target="tpu_custom_call" | custom-call | bytes 3538944 | tf_op jit(solution)/shard_map/pack/pallas_call | solution.py:46
  57.9 11.6 %all-to-all-done.2.refs_3_.refs_4_ = bf16[8,3,144,128]{3,2,1,0:T(8,128)(2,1)S(1)} async-done(((bf16[8,3,144,128]{3,2,1,0:T(8,128)(2,1)}), bf16[8,3,144,128]{3,2,1,0:T(8,128)(2,1)S(1)}, u32[]{:S(2)}, u32[]{:S(2)}) %all-to-all-start.2) | async-done | bytes 884768 | tf_op jit(solution)/shard_map/all_to_all | solution.py:235
  69.4 3.6 %all-to-all-start = ((bf16[8,6,144,128]{3,2,1,0:T(8,128)(2,1)}), bf16[8,6,144,128]{3,2,1,0:T(8,128)(2,1)S(1)}, u32[]{:S(2)}, u32[]{:S(2)}) async-start(bf16[8,6,144,128]{3,2,1,0:T(8,128)(2,1)} %pack.3), calls=%async_computation | async-start | bytes 3538944 | tf_op jit(solution)/shard_map/all_to_all | solution.py:235
  73.0 3.5 %collective-permute-start.8 = (bf16[8,3,144,128]{3,2,1,0:T(8,128)(2,1)S(1)}, bf16[8,3,144,128]{3,2,1,0:T(8,128)(2,1)}, u32[]{:S(2)}, u32[]{:S(2)}) collective-permute-start(bf16[8,3,144,128]{3,2,1,0:T(8,128)(2,1)S(1)} %all-to-all-done.2.refs_3_.refs_4_), channel_id=1, source_target_pairs={{0,128},{8,136},{16,144},{24,152},{32,160},{40,168},{48,176},{56,1... | collective-permute-start | bytes 2654216 | tf_op jit(solution)/shard_map/ppermute | solution.py:232
  78.1 3.2 %collective-permute-start.7 = (bf16[8,1,144,128]{3,2,1,0:T(8,128)(2,1)}, bf16[8,1,144,128]{3,2,1,0:T(8,128)(2,1)S(1)}, u32[]{:S(2)}, u32[]{:S(2)}) collective-permute-start(bf16[8,1,144,128]{3,2,1,0:T(8,128)(2,1)} %slice.20), channel_id=1, source_target_pairs={{0,64},{8,72},{16,80},{24,88},{32,96},{40,104},{48,112},{56,120},{... | collective-permute-start | bytes 884744 | tf_op jit(solution)/shard_map/ppermute | solution.py:232
  81.3 2.7 %collective-permute-start.3 = (bf16[8,2,144,128]{3,2,1,0:T(8,128)(2,1)}, bf16[8,2,144,128]{3,2,1,0:T(8,128)(2,1)S(1)}, u32[]{:S(2)}, u32[]{:S(2)}) collective-permute-start(bf16[8,2,144,128]{3,2,1,0:T(8,128)(2,1)} %slice.18), channel_id=1, source_target_pairs={{0,64},{8,72},{16,80},{24,88},{32,96},{40,104},{48,112},{56,120},{... | collective-permute-start | bytes 1769480 | tf_op jit(solution)/shard_map/ppermute | solution.py:232
  84.0 15.3 %all-to-all-done.refs_0_ = bf16[8,6,144,128]{3,2,1,0:T(8,128)(2,1)S(1)} async-done(((bf16[8,6,144,128]{3,2,1,0:T(8,128)(2,1)}), bf16[8,6,144,128]{3,2,1,0:T(8,128)(2,1)S(1)}, u32[]{:S(2)}, u32[]{:S(2)}) %all-to-all-start) | async-done | bytes 1769504 | tf_op jit(solution)/shard_map/all_to_all | solution.py:235
  102.1 3.6 %collective-permute-start.11 = (bf16[8,2,144,128]{3,2,1,0:T(8,128)(2,1)}, bf16[8,2,144,128]{3,2,1,0:T(8,128)(2,1)}, u32[]{:S(2)}, u32[]{:S(2)}) collective-permute-start(bf16[8,2,144,128]{3,2,1,0:T(8,128)(2,1)} %slice.21), channel_id=1, source_target_pairs={{8,0},{16,8},{24,16},{32,24},{40,32},{48,40},{56,48},{72,64},{80,7... | collective-permute-start | bytes 1769480 | tf_op jit(solution)/shard_map/ppermute | solution.py:232
  105.8 2.6 %collective-permute-start.9 = (bf16[8,1,144,128]{3,2,1,0:T(8,128)(2,1)S(1)}, bf16[8,1,144,128]{3,2,1,0:T(8,128)(2,1)S(1)}, u32[]{:S(2)}, u32[]{:S(2)}) collective-permute-start(bf16[8,1,144,128]{3,2,1,0:T(8,128)(2,1)S(1)} %collective-permute-done.7.refs_5_), channel_id=1, source_target_pairs={{0,128},{8,136},{16,144},{24,152},{32,160},{40,168},{48,176},{56,1... | collective-permute-start | bytes 884744 | tf_op jit(solution)/shard_map/ppermute | solution.py:232
  110.3 5.6 %collective-permute-done.9.refs_7_ = bf16[8,1,144,128]{3,2,1,0:T(8,128)(2,1)S(1)} collective-permute-done((bf16[8,1,144,128]{3,2,1,0:T(8,128)(2,1)S(1)}, bf16[8,1,144,128]{3,2,1,0:T(8,128)(2,1)S(1)}, u32[]{:S(2)}, u32[]{:S(2)}) %collective-permute-start.9) | collective-permute-done | bytes 294944 | tf_op jit(solution)/shard_map/ppermute | solution.py:232
  117.8 3.6 %collective-permute-start.6 = (bf16[8,2,144,128]{3,2,1,0:T(8,128)(2,1)}, bf16[8,2,144,128]{3,2,1,0:T(8,128)(2,1)}, u32[]{:S(2)}, u32[]{:S(2)}) collective-permute-start(bf16[8,2,144,128]{3,2,1,0:T(8,128)(2,1)} %pad_maximum_fusion), channel_id=1, source_target_pairs={{8,0},{16,8},{24,16},{32,24},{40,32},{48,40},{56,48},{72,64},{80,7... | collective-permute-start | bytes 1769480 | tf_op jit(solution)/shard_map/ppermute | solution.py:232
  123.4 3.6 %collective-permute-start.1 = (bf16[8,2,144,128]{3,2,1,0:T(8,128)(2,1)}, bf16[8,2,144,128]{3,2,1,0:T(8,128)(2,1)}, u32[]{:S(2)}, u32[]{:S(2)}) collective-permute-start(bf16[8,2,144,128]{3,2,1,0:T(8,128)(2,1)} %slice.18), channel_id=1, source_target_pairs={{8,0},{16,8},{24,16},{32,24},{40,32},{48,40},{56,48},{72,64},{80,7... | collective-permute-start | bytes 1769480 | tf_op jit(solution)/shard_map/ppermute | solution.py:232
  127.1 6.4 %collective-permute-start.4 = (bf16[8,2,144,128]{3,2,1,0:T(8,128)(2,1)S(1)}, bf16[8,2,144,128]{3,2,1,0:T(8,128)(2,1)S(1)}, u32[]{:S(2)}, u32[]{:S(2)}) collective-permute-start(bf16[8,2,144,128]{3,2,1,0:T(8,128)(2,1)S(1)} %collective-permute-done.3.refs_4_), channel_id=1, source_target_pairs={{0,129},{1,128},{2,131},{3,130},{4,133},{5,132},{6,135},{7,134},{8... | collective-permute-start | bytes 1769480 | tf_op jit(solution)/shard_map/ppermute | solution.py:266
  134.6 6.9 %attend.3.refs_8_ = bf16[8,3,144,128]{3,2,1,0:T(8,128)(2,1)} custom-call(s32[3,5]{1,0:T(4,128)} %fusion.1.idx_ref, s32[3,5]{1,0:T(4,128)} %fusion.4.live_ref, bf16[8,6,144,128]{3,2,1,0:T(8,128)(2,1)} %copy-done, bf16[8,2,144,128]{3,2,1,0:T(8,128)(2,1)} %collective-permute-done.10.refs_1_, bf16[8,2,144,128]{3,2,1,0:T(8,128)(2,1)} %collective-permute-done.11.refs_2_, ...), custom_call_target="tpu_custom_call" | custom-call | flops 1132462080 | bytes 3538944 | tf_op jit(solution)/shard_map/attend/pallas_call | solution.py:190
  141.6 6.9 %attend.4.refs_6_ = bf16[8,3,144,128]{3,2,1,0:T(8,128)(2,1)} custom-call(s32[3,5]{1,0:T(4,128)} %fusion.1.idx_ref, s32[3,5]{1,0:T(4,128)} %fusion.4.live_ref, bf16[8,6,144,128]{3,2,1,0:T(8,128)(2,1)} %copy-done, bf16[8,2,144,128]{3,2,1,0:T(8,128)(2,1)} %collective-permute-done.5.refs_1_, ...), custom_call_target="tpu_custom_call", output_to_operand_aliasing={{}: (10, {})} | custom-call | flops 1132462080 | bytes 3538944 | tf_op jit(solution)/shard_map/attend/pallas_call | solution.py:190
  149.3 6.8 %attend.5 = bf16[8,3,144,128]{3,2,1,0:T(8,128)(2,1)} custom-call(s32[3,5]{1,0:T(4,128)} %fusion.1.idx_ref, s32[3,5]{1,0:T(4,128)} %fusion.4.live_ref, bf16[8,6,144,128]{3,2,1,0:T(8,128)(2,1)} %copy-done, bf16[8,2,144,128]{3,2,1,0:T(8,128)(2,1)} %collective-permute-done.refs_1_, ...), custom_call_target="tpu_custom_call", output_to_operand_aliasing={{}: (8, {})} | custom-call | flops 1132462080 | bytes 3538944 | tf_op jit(solution)/shard_map/attend/pallas_call | solution.py:190
  156.2 19.9 %all_to_all.21.part = bf16[8,3,144,128]{3,2,1,0:T(8,128)(2,1)} all-to-all(bf16[8,3,144,128]{3,2,1,0:T(8,128)(2,1)} %attend.5), channel_id=1, replica_groups=mesh['seq'=32,'head'=8] {'head'}, dimensions={0} | all-to-all | bytes 1769472 | tf_op jit(solution)/shard_map/all_to_all | solution.py:235
  176.0 2.2 %unpack.1 = bf16[144,3072]{1,0:T(8,128)(2,1)} custom-call(s32[1]{0:T(128)} %bitcast.swap_ref, bf16[8,3,144,128]{3,2,1,0:T(8,128)(2,1)} %all_to_all.21.part), custom_call_target="tpu_custom_call" | custom-call | bytes 1769472 | tf_op jit(solution)/shard_map/unpack/pallas_call | solution.py:85
  (36 shorter events, 12.1 us)
Async XLA Ops:
  2.3 45.5 %collective-permute-start.2 = (bf16[8,3,144,128]{3,2,1,0:T(8,128)(2,1)}, bf16[8,3,144,128]{3,2,1,0:T(8,128)(2,1)}, u32[]{:S(2)}, u32[]{:S(2)}) collective-permute-start(bf16[8,3,144,128]{3,2,1,0:T(8,128)(2,1)} %pack.5), channel_id=1, source_target_pairs={{0,64},{8,72},{16,80},{24,88},{32,96},{40,104},{48,112},{56,120},{... | collective-permute-start | bytes 2654216 | tf_op jit(solution)/shard_map/ppermute | solution.py:232
  33.2 44.0 %copy-start.1 = (bf16[8,3,144,128]{3,2,1,0:T(8,128)(2,1)}, bf16[8,3,144,128]{3,2,1,0:T(8,128)(2,1)S(1)}, u32[]{:S(2)}) copy-start(bf16[8,3,144,128]{3,2,1,0:T(8,128)(2,1)S(1)} %all_to_all.20.refs_3_) | copy-start | bytes 2654212
  47.8 21.6 %all-to-all-start.2 = ((bf16[8,3,144,128]{3,2,1,0:T(8,128)(2,1)}), bf16[8,3,144,128]{3,2,1,0:T(8,128)(2,1)S(1)}, u32[]{:S(2)}, u32[]{:S(2)}) async-start(bf16[8,3,144,128]{3,2,1,0:T(8,128)(2,1)} %collective-permute-done.2), calls=%async_computation.2 | async-start | bytes 1769472 | tf_op jit(solution)/shard_map/all_to_all | solution.py:235
  69.4 7.8 %copy-start.2 = (bf16[8,3,144,128]{3,2,1,0:T(8,128)(2,1)}, bf16[8,3,144,128]{3,2,1,0:T(8,128)(2,1)S(1)}, u32[]{:S(2)}) copy-start(bf16[8,3,144,128]{3,2,1,0:T(8,128)(2,1)S(1)} %all-to-all-done.2.refs_3_.refs_4_) | copy-start | bytes 2654212
  69.4 29.9 %all-to-all-start = ((bf16[8,6,144,128]{3,2,1,0:T(8,128)(2,1)}), bf16[8,6,144,128]{3,2,1,0:T(8,128)(2,1)S(1)}, u32[]{:S(2)}, u32[]{:S(2)}) async-start(bf16[8,6,144,128]{3,2,1,0:T(8,128)(2,1)} %pack.3), calls=%async_computation | async-start | bytes 3538944 | tf_op jit(solution)/shard_map/all_to_all | solution.py:235
  73.0 54.1 %collective-permute-start.8 = (bf16[8,3,144,128]{3,2,1,0:T(8,128)(2,1)S(1)}, bf16[8,3,144,128]{3,2,1,0:T(8,128)(2,1)}, u32[]{:S(2)}, u32[]{:S(2)}) collective-permute-start(bf16[8,3,144,128]{3,2,1,0:T(8,128)(2,1)S(1)} %all-to-all-done.2.refs_3_.refs_4_), channel_id=1, source_target_pairs={{0,128},{8,136},{16,144},{24,152},{32,160},{40,168},{48,176},{56,1... | collective-permute-start | bytes 2654216 | tf_op jit(solution)/shard_map/ppermute | solution.py:232
  78.1 55.4 %copy-start.7 = (s32[3,5]{1,0:T(4,128)S(1)}, s32[3,5]{1,0:T(4,128)}, u32[]{:S(2)}) copy-start(s32[3,5]{1,0:T(4,128)} %param.7) | copy-start | bytes 184
  78.1 27.7 %collective-permute-start.7 = (bf16[8,1,144,128]{3,2,1,0:T(8,128)(2,1)}, bf16[8,1,144,128]{3,2,1,0:T(8,128)(2,1)S(1)}, u32[]{:S(2)}, u32[]{:S(2)}) collective-permute-start(bf16[8,1,144,128]{3,2,1,0:T(8,128)(2,1)} %slice.20), channel_id=1, source_target_pairs={{0,64},{8,72},{16,80},{24,88},{32,96},{40,104},{48,112},{56,120},{... | collective-permute-start | bytes 884744 | tf_op jit(solution)/shard_map/ppermute | solution.py:232
  81.3 36.5 %collective-permute-start.3 = (bf16[8,2,144,128]{3,2,1,0:T(8,128)(2,1)}, bf16[8,2,144,128]{3,2,1,0:T(8,128)(2,1)S(1)}, u32[]{:S(2)}, u32[]{:S(2)}) collective-permute-start(bf16[8,2,144,128]{3,2,1,0:T(8,128)(2,1)} %slice.18), channel_id=1, source_target_pairs={{0,64},{8,72},{16,80},{24,88},{32,96},{40,104},{48,112},{56,120},{... | collective-permute-start | bytes 1769480 | tf_op jit(solution)/shard_map/ppermute | solution.py:232
  99.3 35.3 %copy-start = (bf16[8,6,144,128]{3,2,1,0:T(8,128)(2,1)}, bf16[8,6,144,128]{3,2,1,0:T(8,128)(2,1)S(1)}, u32[]{:S(2)}) copy-start(bf16[8,6,144,128]{3,2,1,0:T(8,128)(2,1)S(1)} %all-to-all-done.refs_0_) | copy-start | bytes 5308420
  100.2 21.3 %collective-permute-start.10 = (bf16[8,2,144,128]{3,2,1,0:T(8,128)(2,1)}, bf16[8,2,144,128]{3,2,1,0:T(8,128)(2,1)}, u32[]{:S(2)}, u32[]{:S(2)}) collective-permute-start(bf16[8,2,144,128]{3,2,1,0:T(8,128)(2,1)} %slice.21), channel_id=1, source_target_pairs={{0,8},{8,16},{16,24},{24,32},{32,40},{40,48},{48,56},{64,72},{72,8... | collective-permute-start | bytes 1769480 | tf_op jit(solution)/shard_map/ppermute | solution.py:232
  102.1 21.3 %collective-permute-start.11 = (bf16[8,2,144,128]{3,2,1,0:T(8,128)(2,1)}, bf16[8,2,144,128]{3,2,1,0:T(8,128)(2,1)}, u32[]{:S(2)}, u32[]{:S(2)}) collective-permute-start(bf16[8,2,144,128]{3,2,1,0:T(8,128)(2,1)} %slice.21), channel_id=1, source_target_pairs={{8,0},{16,8},{24,16},{32,24},{40,32},{48,40},{56,48},{72,64},{80,7... | collective-permute-start | bytes 1769480 | tf_op jit(solution)/shard_map/ppermute | solution.py:232
  105.8 35.7 %copy-start.5 = (bf16[8,1,144,128]{3,2,1,0:T(8,128)(2,1)}, bf16[8,1,144,128]{3,2,1,0:T(8,128)(2,1)S(1)}, u32[]{:S(2)}) copy-start(bf16[8,1,144,128]{3,2,1,0:T(8,128)(2,1)S(1)} %collective-permute-done.7.refs_5_) | copy-start | bytes 884740
  105.8 10.1 %collective-permute-start.9 = (bf16[8,1,144,128]{3,2,1,0:T(8,128)(2,1)S(1)}, bf16[8,1,144,128]{3,2,1,0:T(8,128)(2,1)S(1)}, u32[]{:S(2)}, u32[]{:S(2)}) collective-permute-start(bf16[8,1,144,128]{3,2,1,0:T(8,128)(2,1)S(1)} %collective-permute-done.7.refs_5_), channel_id=1, source_target_pairs={{0,128},{8,136},{16,144},{24,152},{32,160},{40,168},{48,176},{56,1... | collective-permute-start | bytes 884744 | tf_op jit(solution)/shard_map/ppermute | solution.py:232
  115.9 1.9 %copy-start.6 = (bf16[8,1,144,128]{3,2,1,0:T(8,128)(2,1)}, bf16[8,1,144,128]{3,2,1,0:T(8,128)(2,1)S(1)}, u32[]{:S(2)}) copy-start(bf16[8,1,144,128]{3,2,1,0:T(8,128)(2,1)S(1)} %collective-permute-done.9.refs_7_) | copy-start | bytes 884740
  115.9 25.7 %collective-permute-start.5 = (bf16[8,2,144,128]{3,2,1,0:T(8,128)(2,1)}, bf16[8,2,144,128]{3,2,1,0:T(8,128)(2,1)}, u32[]{:S(2)}, u32[]{:S(2)}) collective-permute-start(bf16[8,2,144,128]{3,2,1,0:T(8,128)(2,1)} %pad_maximum_fusion), channel_id=1, source_target_pairs={{0,8},{8,16},{16,24},{24,32},{32,40},{40,48},{48,56},{64,72},{72,8... | collective-permute-start | bytes 1769480 | tf_op jit(solution)/shard_map/ppermute | solution.py:232
  117.8 23.7 %copy-start.3 = (bf16[8,2,144,128]{3,2,1,0:T(8,128)(2,1)}, bf16[8,2,144,128]{3,2,1,0:T(8,128)(2,1)S(1)}, u32[]{:S(2)}) copy-start(bf16[8,2,144,128]{3,2,1,0:T(8,128)(2,1)S(1)} %collective-permute-done.3.refs_4_) | copy-start | bytes 1769476
  117.8 23.8 %collective-permute-start.6 = (bf16[8,2,144,128]{3,2,1,0:T(8,128)(2,1)}, bf16[8,2,144,128]{3,2,1,0:T(8,128)(2,1)}, u32[]{:S(2)}, u32[]{:S(2)}) collective-permute-start(bf16[8,2,144,128]{3,2,1,0:T(8,128)(2,1)} %pad_maximum_fusion), channel_id=1, source_target_pairs={{8,0},{16,8},{24,16},{32,24},{40,32},{48,40},{56,48},{72,64},{80,7... | collective-permute-start | bytes 1769480 | tf_op jit(solution)/shard_map/ppermute | solution.py:232
  121.5 27.0 %collective-permute-start = (bf16[8,2,144,128]{3,2,1,0:T(8,128)(2,1)}, bf16[8,2,144,128]{3,2,1,0:T(8,128)(2,1)}, u32[]{:S(2)}, u32[]{:S(2)}) collective-permute-start(bf16[8,2,144,128]{3,2,1,0:T(8,128)(2,1)} %slice.18), channel_id=1, source_target_pairs={{0,8},{8,16},{16,24},{24,32},{32,40},{40,48},{48,56},{64,72},{72,8... | collective-permute-start | bytes 1769480 | tf_op jit(solution)/shard_map/ppermute | solution.py:232
  123.4 25.0 %collective-permute-start.1 = (bf16[8,2,144,128]{3,2,1,0:T(8,128)(2,1)}, bf16[8,2,144,128]{3,2,1,0:T(8,128)(2,1)}, u32[]{:S(2)}, u32[]{:S(2)}) collective-permute-start(bf16[8,2,144,128]{3,2,1,0:T(8,128)(2,1)} %slice.18), channel_id=1, source_target_pairs={{8,0},{16,8},{24,16},{32,24},{40,32},{48,40},{56,48},{72,64},{80,7... | collective-permute-start | bytes 1769480 | tf_op jit(solution)/shard_map/ppermute | solution.py:232
  127.1 21.4 %collective-permute-start.4 = (bf16[8,2,144,128]{3,2,1,0:T(8,128)(2,1)S(1)}, bf16[8,2,144,128]{3,2,1,0:T(8,128)(2,1)S(1)}, u32[]{:S(2)}, u32[]{:S(2)}) collective-permute-start(bf16[8,2,144,128]{3,2,1,0:T(8,128)(2,1)S(1)} %collective-permute-done.3.refs_4_), channel_id=1, source_target_pairs={{0,129},{1,128},{2,131},{3,130},{4,133},{5,132},{6,135},{7,134},{8... | collective-permute-start | bytes 1769480 | tf_op jit(solution)/shard_map/ppermute | solution.py:266
  148.5 0.8 copy-start.4

commit v11 on v10

--- a/solution.py
+++ b/solution.py
@@ -265,17 +265,18 @@
         behind[i] = send(own[i], left)
     second_2 = lax.ppermute(far_2, ("seq", "head"), hop)
     second_1 = send(far_1, middle)
-    second_b = send(crossed, middle)
+    second_0 = send(crossed[:, 0:2], middle)
+    second_k = send(crossed[:, 2:3], middle)
     parts = local
 
     def both(source, first=0):
         return ((source, first), (source, first + 1))
 
     takes = [
-        ([most, before[0], behind[0], crossed, second_b], [both(0, 3), both(1), both(2), both(3), both(4)]),
+        ([most, before[0], behind[0], crossed, second_0], [both(0, 3), both(1), both(2), both(3), both(4)]),
         (
-            [most, before[1], behind[1], rest, crossed, far_1, second_b, second_1],
-            [((0, 5), (3, 0)), both(1), both(2), ((4, 2), (5, 0)), ((6, 2), (7, 0))],
+            [most, before[1], behind[1], rest, crossed, far_1, second_k, second_1],
+            [((0, 5), (3, 0)), both(1), both(2), ((4, 2), (5, 0)), ((6, 0), (7, 0))],
         ),
         ([most, before[2], behind[2], rest, far_2, second_2], [both(3, 1), both(1), both(2), both(4), both(5)]),
     ]

time: 182 us -> 202 us (1.11); the launches traced: 178 us -> 201 us
  waiting for transfers between devices: 47 us -> 81.6 us
  blocking collectives: 42.1 us -> 19.2 us
  starting transfers between devices: 51.9 us -> 59.8 us
  local copies, waits for them, and re-layouts: 3.37 us -> 7.03 us
    ppermute x11 -> x12, waiting for transfers between devices: 20.2 us -> 69.3 us  [send(): return lax.ppermute(x, 'seq', pairs)]
    all_to_all x2 -> x1, blocking collectives: 42.1 us -> 19.2 us  [exchange(): return lax.all_to_all(x, 'head', split_axis=0, concat_axis=0, tiled=True)]
    all_to_all x2 -> x3, waiting for transfers between devices: 26.8 us -> 12.3 us  [exchange(): return lax.all_to_all(x, 'head', split_axis=0, concat_axis=0, tiled=True)]
    all_to_all x2 -> x3, starting transfers between devices: 10.5 us -> 17.5 us  [exchange(): return lax.all_to_all(x, 'head', split_axis=0, concat_axis=0, tiled=True)]
    unnamed x16 -> x26, local copies, waits for them, and re-layouts: 0.84 us -> 4.4 us
    ppermute x11 -> x12, starting transfers between devices: 35 us -> 34.9 us  [send(): return lax.ppermute(x, 'seq', pairs)]
  transfers between devices with their start and end apart: 14 -> 16, of which waited for: 4 -> 4; matrix products, arithmetic and copies ran while one was open for 3% -> 2% of each run, Pallas kernels for 11% -> 10%
where the time goes in v11:
time: 202 us; the launch traced here: 201 us
  waiting for transfers between devices  81.6 us (40%)
  starting transfers between devices  59.8 us (30%)
  Pallas kernels  30.5 us (15%)
  blocking collectives  19.2 us (10%)
  local copies, waits for them, and re-layouts  7.03 us (3%)
  other arithmetic  2.04 us (1%)
    ppermute x12, waiting for transfers between devices, send(): return lax.ppermute(x, 'seq', pairs)  69.3 us
    ppermute x12, starting transfers between devices, send(): return lax.ppermute(x, 'seq', pairs)  34.9 us
    pallas_call x3, Pallas kernels, attend(): pl.pallas_call(functools.partial(attend_kernel, tile, per_slab, plan, out...  20.6 us
    all_to_all x1, blocking collectives, exchange(): return lax.all_to_all(x, 'head', split_axis=0, concat_axis=0, tiled=True)  19.2 us
    all_to_all x3, starting transfers between devices, exchange(): return lax.all_to_all(x, 'head', split_axis=0, concat_axis=0, tiled=True)  17.5 us
    all_to_all x3, waiting for transfers between devices, exchange(): return lax.all_to_all(x, 'head', split_axis=0, concat_axis=0, tiled=True)  12.3 us
    pallas_call x3, Pallas kernels, pack(): pl.pallas_call(functools.partial(pack_kernel, picks, width // (groups * H...  7.73 us
    ppermute x1, starting transfers between devices, body(): second_2 = lax.ppermute(far_2, ('seq', 'head'), hop)  7.38 us
  transfers between devices with their start and end apart: 16, of which 4 were waited for; matrix products, arithmetic and copies ran while one was open for 2% of the time, Pallas kernels for 10%

profile of v11, /device:TPU:32, one launch (start us, length us, event | category | flops | bytes accessed | tf_op | source)
XLA Modules:
  0.0 200.6 jit_solution(7183939987161270130)
XLA Ops:
  0.0 2.3 %pack.4 = bf16[8,3,144,128]{3,2,1,0:T(8,128)(2,1)} custom-call(s32[1]{0:T(128)} %bitcast.swap_ref, bf16[144,3072]{1,0:T(8,128)(2,1)} %refs_0_.5, bf16[144,3072]{1,0:T(8,128)(2,1)} %refs_1_.5), custom_call_target="tpu_custom_call" | custom-call | bytes 1769472 | tf_op jit(solution)/shard_map/pack/pallas_call | solution.py:46
  2.3 6.9 %all-to-all-start.1 = ((bf16[8,3,144,128]{3,2,1,0:T(8,128)(2,1)}), bf16[8,3,144,128]{3,2,1,0:T(8,128)(2,1)S(1)}, u32[]{:S(2)}, u32[]{:S(2)}) async-start(bf16[8,3,144,128]{3,2,1,0:T(8,128)(2,1)} %pack.4), calls=%async_computation.1 | async-start | bytes 1769472 | tf_op jit(solution)/shard_map/all_to_all | solution.py:235
  9.2 3.1 %pack.3 = bf16[8,6,144,128]{3,2,1,0:T(8,128)(2,1)} custom-call(s32[1]{0:T(128)} %bitcast.swap_ref, bf16[144,3072]{1,0:T(8,128)(2,1)} %refs_0_.5, bf16[144,3072]{1,0:T(8,128)(2,1)} %refs_1_.5, bf16[144,3072]{1,0:T(8,128)(2,1)} %refs_2_.1), custom_call_target="tpu_custom_call" | custom-call | bytes 3538944 | tf_op jit(solution)/shard_map/pack/pallas_call | solution.py:46
  12.4 12.3 %all-to-all-done.1.refs_3_ = bf16[8,3,144,128]{3,2,1,0:T(8,128)(2,1)S(1)} async-done(((bf16[8,3,144,128]{3,2,1,0:T(8,128)(2,1)}), bf16[8,3,144,128]{3,2,1,0:T(8,128)(2,1)S(1)}, u32[]{:S(2)}, u32[]{:S(2)}) %all-to-all-start.1) | async-done | bytes 884768 | tf_op jit(solution)/shard_map/all_to_all | solution.py:235
  24.7 3.6 %all-to-all-start = ((bf16[8,6,144,128]{3,2,1,0:T(8,128)(2,1)}), bf16[8,6,144,128]{3,2,1,0:T(8,128)(2,1)S(1)}, u32[]{:S(2)}, u32[]{:S(2)}) async-start(bf16[8,6,144,128]{3,2,1,0:T(8,128)(2,1)} %pack.3), calls=%async_computation | async-start | bytes 3538944 | tf_op jit(solution)/shard_map/all_to_all | solution.py:235
  28.3 2.3 %pack.5 = bf16[8,3,144,128]{3,2,1,0:T(8,128)(2,1)} custom-call(s32[1]{0:T(128)} %bitcast.swap_ref, bf16[144,3072]{1,0:T(8,128)(2,1)} %refs_0_.5, bf16[144,3072]{1,0:T(8,128)(2,1)} %refs_1_.5), custom_call_target="tpu_custom_call" | custom-call | bytes 1769472 | tf_op jit(solution)/shard_map/pack/pallas_call | solution.py:46
  30.6 6.4 %collective-permute-start.2 = (bf16[8,3,144,128]{3,2,1,0:T(8,128)(2,1)}, bf16[8,3,144,128]{3,2,1,0:T(8,128)(2,1)S(1)}, u32[]{:S(2)}, u32[]{:S(2)}) collective-permute-start(bf16[8,3,144,128]{3,2,1,0:T(8,128)(2,1)} %pack.5), channel_id=1, source_target_pairs={{0,64},{8,72},{16,80},{24,88},{32,96},{40,104},{48,112},{56,120},{... | collective-permute-start | bytes 2654216 | tf_op jit(solution)/shard_map/ppermute | solution.py:232
  37.0 37.9 %collective-permute-done.2 = bf16[8,3,144,128]{3,2,1,0:T(8,128)(2,1)S(1)} collective-permute-done((bf16[8,3,144,128]{3,2,1,0:T(8,128)(2,1)}, bf16[8,3,144,128]{3,2,1,0:T(8,128)(2,1)S(1)}, u32[]{:S(2)}, u32[]{:S(2)}) %collective-permute-start.2) | collective-permute-done | bytes 884768 | tf_op jit(solution)/shard_map/ppermute | solution.py:232
  75.8 6.9 %all-to-all-start.2 = ((bf16[8,3,144,128]{3,2,1,0:T(8,128)(2,1)}), bf16[8,3,144,128]{3,2,1,0:T(8,128)(2,1)S(1)}, u32[]{:S(2)}, u32[]{:S(2)}) async-start(bf16[8,3,144,128]{3,2,1,0:T(8,128)(2,1)} %copy-done.5), calls=%async_computation.2 | async-start | bytes 1769472 | tf_op jit(solution)/shard_map/all_to_all | solution.py:235
  82.8 5.6 %collective-permute-start.7 = (bf16[8,1,144,128]{3,2,1,0:T(8,128)(2,1)S(1)}, bf16[8,1,144,128]{3,2,1,0:T(8,128)(2,1)}, u32[]{:S(2)}, u32[]{:S(2)}) collective-permute-start(bf16[8,1,144,128]{3,2,1,0:T(8,128)(2,1)S(1)} %slice.28), channel_id=1, source_target_pairs={{0,64},{8,72},{16,80},{24,88},{32,96},{40,104},{48,112},{56,120},{... | collective-permute-start | bytes 884744 | tf_op jit(solution)/shard_map/ppermute | solution.py:232
  89.7 18.8 %collective-permute-done.7.refs_5_ = bf16[8,1,144,128]{3,2,1,0:T(8,128)(2,1)} collective-permute-done((bf16[8,1,144,128]{3,2,1,0:T(8,128)(2,1)S(1)}, bf16[8,1,144,128]{3,2,1,0:T(8,128)(2,1)}, u32[]{:S(2)}, u32[]{:S(2)}) %collective-permute-start.7) | collective-permute-done | bytes 294944 | tf_op jit(solution)/shard_map/ppermute | solution.py:232
  108.4 3.3 %collective-permute-start.9 = (bf16[8,1,144,128]{3,2,1,0:T(8,128)(2,1)}, bf16[8,1,144,128]{3,2,1,0:T(8,128)(2,1)}, u32[]{:S(2)}, u32[]{:S(2)}) collective-permute-start(bf16[8,1,144,128]{3,2,1,0:T(8,128)(2,1)} %collective-permute-done.7.refs_5_), channel_id=1, source_target_pairs={{0,128},{8,136},{16,144},{24,152},{32,160},{40,168},{48,176},{56,1... | collective-permute-start | bytes 884744 | tf_op jit(solution)/shard_map/ppermute | solution.py:232
  112.6 2.0 %collective-permute-start.10 = (bf16[8,2,144,128]{3,2,1,0:T(8,128)(2,1)}, bf16[8,2,144,128]{3,2,1,0:T(8,128)(2,1)}, u32[]{:S(2)}, u32[]{:S(2)}) collective-permute-start(bf16[8,2,144,128]{3,2,1,0:T(8,128)(2,1)} %slice.30), channel_id=1, source_target_pairs={{0,8},{8,16},{16,24},{24,32},{32,40},{40,48},{48,56},{64,72},{72,8... | collective-permute-start | bytes 1769480 | tf_op jit(solution)/shard_map/ppermute | solution.py:232
  114.7 3.6 %collective-permute-start.11 = (bf16[8,2,144,128]{3,2,1,0:T(8,128)(2,1)}, bf16[8,2,144,128]{3,2,1,0:T(8,128)(2,1)}, u32[]{:S(2)}, u32[]{:S(2)}) collective-permute-start(bf16[8,2,144,128]{3,2,1,0:T(8,128)(2,1)} %slice.30), channel_id=1, source_target_pairs={{8,0},{16,8},{24,16},{32,24},{40,32},{48,40},{56,48},{72,64},{80,7... | collective-permute-start | bytes 1769480 | tf_op jit(solution)/shard_map/ppermute | solution.py:232
  119.2 2.1 %collective-permute-start.12 = (bf16[8,2,144,128]{3,2,1,0:T(8,128)(2,1)}, bf16[8,2,144,128]{3,2,1,0:T(8,128)(2,1)}, u32[]{:S(2)}, u32[]{:S(2)}) collective-permute-start(bf16[8,2,144,128]{3,2,1,0:T(8,128)(2,1)} %slice.31), channel_id=1, source_target_pairs={{0,128},{8,136},{16,144},{24,152},{32,160},{40,168},{48,176},{56,1... | collective-permute-start | bytes 1769480 | tf_op jit(solution)/shard_map/ppermute | solution.py:232
  126.2 12.6 %collective-permute-done.8.refs_6_ = bf16[8,1,144,128]{3,2,1,0:T(8,128)(2,1)} collective-permute-done((bf16[8,1,144,128]{3,2,1,0:T(8,128)(2,1)S(1)}, bf16[8,1,144,128]{3,2,1,0:T(8,128)(2,1)}, u32[]{:S(2)}, u32[]{:S(2)}) %collective-permute-start.8) | collective-permute-done | bytes 294944 | tf_op jit(solution)/shard_map/ppermute | solution.py:232
  140.8 2.4 %collective-permute-start = (bf16[8,2,144,128]{3,2,1,0:T(8,128)(2,1)}, bf16[8,2,144,128]{3,2,1,0:T(8,128)(2,1)S(1)}, u32[]{:S(2)}, u32[]{:S(2)}) collective-permute-start(bf16[8,2,144,128]{3,2,1,0:T(8,128)(2,1)} %slice.26), channel_id=1, source_target_pairs={{0,8},{8,16},{16,24},{24,32},{32,40},{40,48},{48,56},{64,72},{72,8... | collective-permute-start | bytes 1769480 | tf_op jit(solution)/shard_map/ppermute | solution.py:232
  143.2 3.2 %collective-permute-start.1 = (bf16[8,2,144,128]{3,2,1,0:T(8,128)(2,1)}, bf16[8,2,144,128]{3,2,1,0:T(8,128)(2,1)S(1)}, u32[]{:S(2)}, u32[]{:S(2)}) collective-permute-start(bf16[8,2,144,128]{3,2,1,0:T(8,128)(2,1)} %slice.26), channel_id=1, source_target_pairs={{8,0},{16,8},{24,16},{32,24},{40,32},{48,40},{56,48},{72,64},{80,7... | collective-permute-start | bytes 1769480 | tf_op jit(solution)/shard_map/ppermute | solution.py:232
  146.4 7.4 %collective-permute-start.4 = (bf16[8,2,144,128]{3,2,1,0:T(8,128)(2,1)S(1)}, bf16[8,2,144,128]{3,2,1,0:T(8,128)(2,1)S(1)}, u32[]{:S(2)}, u32[]{:S(2)}) collective-permute-start(bf16[8,2,144,128]{3,2,1,0:T(8,128)(2,1)S(1)} %collective-permute-done.3.refs_4_), channel_id=1, source_target_pairs={{0,129},{1,128},{2,131},{3,130},{4,133},{5,132},{6,135},{7,134},{8... | collective-permute-start | bytes 1769480 | tf_op jit(solution)/shard_map/ppermute | solution.py:266
  154.9 6.9 %attend.3.refs_8_ = bf16[8,3,144,128]{3,2,1,0:T(8,128)(2,1)} custom-call(s32[3,5]{1,0:T(4,128)} %fusion.1.idx_ref, s32[3,5]{1,0:T(4,128)} %fusion.4.live_ref, bf16[8,6,144,128]{3,2,1,0:T(8,128)(2,1)} %copy-done, bf16[8,2,144,128]{3,2,1,0:T(8,128)(2,1)} %collective-permute-done.10.refs_1_, bf16[8,2,144,128]{3,2,1,0:T(8,128)(2,1)} %collective-permute-done.11.refs_2_, ...), custom_call_target="tpu_custom_call" | custom-call | flops 1132462080 | bytes 3538944 | tf_op jit(solution)/shard_map/attend/pallas_call | solution.py:190
  163.5 6.9 %attend.4.refs_6_ = bf16[8,3,144,128]{3,2,1,0:T(8,128)(2,1)} custom-call(s32[3,5]{1,0:T(4,128)} %fusion.1.idx_ref, s32[3,5]{1,0:T(4,128)} %fusion.4.live_ref, bf16[8,6,144,128]{3,2,1,0:T(8,128)(2,1)} %copy-done, bf16[8,2,144,128]{3,2,1,0:T(8,128)(2,1)} %copy-done.7, bf16[8,2,144,128]{3,2,1,0:T(8,128)(2,1)} %copy-done.8, ...), custom_call_target="tpu_custom_call", output_to_operand_aliasing={{}: (10, {})} | custom-call | flops 1132462080 | bytes 3538944 | tf_op jit(solution)/shard_map/attend/pallas_call | solution.py:190
  172.2 6.9 %attend.5 = bf16[8,3,144,128]{3,2,1,0:T(8,128)(2,1)} custom-call(s32[3,5]{1,0:T(4,128)} %fusion.1.idx_ref, s32[3,5]{1,0:T(4,128)} %fusion.4.live_ref, bf16[8,6,144,128]{3,2,1,0:T(8,128)(2,1)} %copy-done, bf16[8,2,144,128]{3,2,1,0:T(8,128)(2,1)} %copy-done.9, bf16[8,2,144,128]{3,2,1,0:T(8,128)(2,1)} %copy-done.10, ...), custom_call_target="tpu_custom_call", output_to_operand_aliasing={{}: (8, {})} | custom-call | flops 1132462080 | bytes 3538944 | tf_op jit(solution)/shard_map/attend/pallas_call | solution.py:190
  179.1 19.2 %all_to_all.20.part = bf16[8,3,144,128]{3,2,1,0:T(8,128)(2,1)} all-to-all(bf16[8,3,144,128]{3,2,1,0:T(8,128)(2,1)} %attend.5), channel_id=1, replica_groups=mesh['seq'=32,'head'=8] {'head'}, dimensions={0} | all-to-all | bytes 1769472 | tf_op jit(solution)/shard_map/all_to_all | solution.py:235
  198.3 2.2 %unpack.1 = bf16[144,3072]{1,0:T(8,128)(2,1)} custom-call(s32[1]{0:T(128)} %bitcast.swap_ref, bf16[8,3,144,128]{3,2,1,0:T(8,128)(2,1)} %all_to_all.20.part), custom_call_target="tpu_custom_call" | custom-call | bytes 1769472 | tf_op jit(solution)/shard_map/unpack/pallas_call | solution.py:85
  (51 shorter events, 15.4 us)
Async XLA Ops:
  2.3 22.4 %all-to-all-start.1 = ((bf16[8,3,144,128]{3,2,1,0:T(8,128)(2,1)}), bf16[8,3,144,128]{3,2,1,0:T(8,128)(2,1)S(1)}, u32[]{:S(2)}, u32[]{:S(2)}) async-start(bf16[8,3,144,128]{3,2,1,0:T(8,128)(2,1)} %pack.4), calls=%async_computation.1 | async-start | bytes 1769472 | tf_op jit(solution)/shard_map/all_to_all | solution.py:235
  24.7 63.7 %copy-start.1 = (bf16[8,3,144,128]{3,2,1,0:T(8,128)(2,1)}, bf16[8,3,144,128]{3,2,1,0:T(8,128)(2,1)S(1)}, u32[]{:S(2)}) copy-start(bf16[8,3,144,128]{3,2,1,0:T(8,128)(2,1)S(1)} %all-to-all-done.1.refs_3_) | copy-start | bytes 2654212
  24.7 51.1 %all-to-all-start = ((bf16[8,6,144,128]{3,2,1,0:T(8,128)(2,1)}), bf16[8,6,144,128]{3,2,1,0:T(8,128)(2,1)S(1)}, u32[]{:S(2)}, u32[]{:S(2)}) async-start(bf16[8,6,144,128]{3,2,1,0:T(8,128)(2,1)} %pack.3), calls=%async_computation | async-start | bytes 3538944 | tf_op jit(solution)/shard_map/all_to_all | solution.py:235
  30.6 44.3 %collective-permute-start.2 = (bf16[8,3,144,128]{3,2,1,0:T(8,128)(2,1)}, bf16[8,3,144,128]{3,2,1,0:T(8,128)(2,1)S(1)}, u32[]{:S(2)}, u32[]{:S(2)}) collective-permute-start(bf16[8,3,144,128]{3,2,1,0:T(8,128)(2,1)} %pack.5), channel_id=1, source_target_pairs={{0,64},{8,72},{16,80},{24,88},{32,96},{40,104},{48,112},{56,120},{... | collective-permute-start | bytes 2654216 | tf_op jit(solution)/shard_map/ppermute | solution.py:232
  75.8 47.6 %copy-start = (bf16[8,6,144,128]{3,2,1,0:T(8,128)(2,1)}, bf16[8,6,144,128]{3,2,1,0:T(8,128)(2,1)S(1)}, u32[]{:S(2)}) copy-start(bf16[8,6,144,128]{3,2,1,0:T(8,128)(2,1)S(1)} %all-to-all-done.refs_0_) | copy-start | bytes 5308420
  75.8 42.5 %all-to-all-start.2 = ((bf16[8,3,144,128]{3,2,1,0:T(8,128)(2,1)}), bf16[8,3,144,128]{3,2,1,0:T(8,128)(2,1)S(1)}, u32[]{:S(2)}, u32[]{:S(2)}) async-start(bf16[8,3,144,128]{3,2,1,0:T(8,128)(2,1)} %copy-done.5), calls=%async_computation.2 | async-start | bytes 1769472 | tf_op jit(solution)/shard_map/all_to_all | solution.py:235
  82.8 31.9 %copy-start.3 = (bf16[8,1,144,128]{3,2,1,0:T(8,128)(2,1)}, bf16[8,1,144,128]{3,2,1,0:T(8,128)(2,1)S(1)}, u32[]{:S(2)}) copy-start(bf16[8,1,144,128]{3,2,1,0:T(8,128)(2,1)S(1)} %slice.28) | copy-start | bytes 884740
  82.8 25.6 %collective-permute-start.7 = (bf16[8,1,144,128]{3,2,1,0:T(8,128)(2,1)S(1)}, bf16[8,1,144,128]{3,2,1,0:T(8,128)(2,1)}, u32[]{:S(2)}, u32[]{:S(2)}) collective-permute-start(bf16[8,1,144,128]{3,2,1,0:T(8,128)(2,1)S(1)} %slice.28), channel_id=1, source_target_pairs={{0,64},{8,72},{16,80},{24,88},{32,96},{40,104},{48,112},{56,120},{... | collective-permute-start | bytes 884744 | tf_op jit(solution)/shard_map/ppermute | solution.py:232
  89.2 35.1 %collective-permute-start.3 = (bf16[8,2,144,128]{3,2,1,0:T(8,128)(2,1)}, bf16[8,2,144,128]{3,2,1,0:T(8,128)(2,1)S(1)}, u32[]{:S(2)}, u32[]{:S(2)}) collective-permute-start(bf16[8,2,144,128]{3,2,1,0:T(8,128)(2,1)} %slice.26), channel_id=1, source_target_pairs={{0,64},{8,72},{16,80},{24,88},{32,96},{40,104},{48,112},{56,120},{... | collective-permute-start | bytes 1769480 | tf_op jit(solution)/shard_map/ppermute | solution.py:232
  108.4 12.9 %collective-permute-start.9 = (bf16[8,1,144,128]{3,2,1,0:T(8,128)(2,1)}, bf16[8,1,144,128]{3,2,1,0:T(8,128)(2,1)}, u32[]{:S(2)}, u32[]{:S(2)}) collective-permute-start(bf16[8,1,144,128]{3,2,1,0:T(8,128)(2,1)} %collective-permute-done.7.refs_5_), channel_id=1, source_target_pairs={{0,128},{8,136},{16,144},{24,152},{32,160},{40,168},{48,176},{56,1... | collective-permute-start | bytes 884744 | tf_op jit(solution)/shard_map/ppermute | solution.py:232
  112.6 41.2 %copy-start.12 = (s32[3,5]{1,0:T(4,128)S(1)}, s32[3,5]{1,0:T(4,128)}, u32[]{:S(2)}) copy-start(s32[3,5]{1,0:T(4,128)} %param.7) | copy-start | bytes 184
  112.6 28.2 %collective-permute-start.10 = (bf16[8,2,144,128]{3,2,1,0:T(8,128)(2,1)}, bf16[8,2,144,128]{3,2,1,0:T(8,128)(2,1)}, u32[]{:S(2)}, u32[]{:S(2)}) collective-permute-start(bf16[8,2,144,128]{3,2,1,0:T(8,128)(2,1)} %slice.30), channel_id=1, source_target_pairs={{0,8},{8,16},{16,24},{24,32},{32,40},{40,48},{48,56},{64,72},{72,8... | collective-permute-start | bytes 1769480 | tf_op jit(solution)/shard_map/ppermute | solution.py:232
  114.7 28.5 %collective-permute-start.11 = (bf16[8,2,144,128]{3,2,1,0:T(8,128)(2,1)}, bf16[8,2,144,128]{3,2,1,0:T(8,128)(2,1)}, u32[]{:S(2)}, u32[]{:S(2)}) collective-permute-start(bf16[8,2,144,128]{3,2,1,0:T(8,128)(2,1)} %slice.30), channel_id=1, source_target_pairs={{8,0},{16,8},{24,16},{32,24},{40,32},{48,40},{56,48},{72,64},{80,7... | collective-permute-start | bytes 1769480 | tf_op jit(solution)/shard_map/ppermute | solution.py:232
  118.3 5.1 %copy-start.4 = (bf16[8,1,144,128]{3,2,1,0:T(8,128)(2,1)S(1)}, bf16[8,1,144,128]{3,2,1,0:T(8,128)(2,1)}, u32[]{:S(2)}) copy-start(bf16[8,1,144,128]{3,2,1,0:T(8,128)(2,1)} %copy-done.3) | copy-start | bytes 884740
  118.3 6.0 %copy-start.2 = (bf16[8,3,144,128]{3,2,1,0:T(8,128)(2,1)}, bf16[8,3,144,128]{3,2,1,0:T(8,128)(2,1)S(1)}, u32[]{:S(2)}) copy-start(bf16[8,3,144,128]{3,2,1,0:T(8,128)(2,1)S(1)} %all-to-all-done.2.refs_3_.refs_4_) | copy-start | bytes 2654212
  119.2 27.2 %collective-permute-start.12 = (bf16[8,2,144,128]{3,2,1,0:T(8,128)(2,1)}, bf16[8,2,144,128]{3,2,1,0:T(8,128)(2,1)}, u32[]{:S(2)}, u32[]{:S(2)}) collective-permute-start(bf16[8,2,144,128]{3,2,1,0:T(8,128)(2,1)} %slice.31), channel_id=1, source_target_pairs={{0,128},{8,136},{16,144},{24,152},{32,160},{40,168},{48,176},{56,1... | collective-permute-start | bytes 1769480 | tf_op jit(solution)/shard_map/ppermute | solution.py:232
  121.4 17.5 %collective-permute-start.8 = (bf16[8,1,144,128]{3,2,1,0:T(8,128)(2,1)S(1)}, bf16[8,1,144,128]{3,2,1,0:T(8,128)(2,1)}, u32[]{:S(2)}, u32[]{:S(2)}) collective-permute-start(bf16[8,1,144,128]{3,2,1,0:T(8,128)(2,1)S(1)} %slice.29), channel_id=1, source_target_pairs={{0,128},{8,136},{16,144},{24,152},{32,160},{40,168},{48,176},{56,1... | collective-permute-start | bytes 884744 | tf_op jit(solution)/shard_map/ppermute | solution.py:232
  124.3 37.5 %copy-start.6 = (bf16[8,2,144,128]{3,2,1,0:T(8,128)(2,1)}, bf16[8,2,144,128]{3,2,1,0:T(8,128)(2,1)S(1)}, u32[]{:S(2)}) copy-start(bf16[8,2,144,128]{3,2,1,0:T(8,128)(2,1)S(1)} %collective-permute-done.3.refs_4_) | copy-start | bytes 1769476
  124.3 37.5 %collective-permute-start.5 = (bf16[8,2,144,128]{3,2,1,0:T(8,128)(2,1)}, bf16[8,2,144,128]{3,2,1,0:T(8,128)(2,1)S(1)}, u32[]{:S(2)}, u32[]{:S(2)}) collective-permute-start(bf16[8,2,144,128]{3,2,1,0:T(8,128)(2,1)} %pad_maximum_fusion), channel_id=1, source_target_pairs={{0,8},{8,16},{16,24},{24,32},{32,40},{40,48},{48,56},{64,72},{72,8... | collective-permute-start | bytes 1769480 | tf_op jit(solution)/shard_map/ppermute | solution.py:232
  138.8 23.0 %collective-permute-start.6 = (bf16[8,2,144,128]{3,2,1,0:T(8,128)(2,1)}, bf16[8,2,144,128]{3,2,1,0:T(8,128)(2,1)S(1)}, u32[]{:S(2)}, u32[]{:S(2)}) collective-permute-start(bf16[8,2,144,128]{3,2,1,0:T(8,128)(2,1)} %pad_maximum_fusion), channel_id=1, source_target_pairs={{8,0},{16,8},{24,16},{32,24},{40,32},{48,40},{56,48},{72,64},{80,7... | collective-permute-start | bytes 1769480 | tf_op jit(solution)/shard_map/ppermute | solution.py:232
  140.8 29.6 %collective-permute-start = (bf16[8,2,144,128]{3,2,1,0:T(8,128)(2,1)}, bf16[8,2,144,128]{3,2,1,0:T(8,128)(2,1)S(1)}, u32[]{:S(2)}, u32[]{:S(2)}) collective-permute-start(bf16[8,2,144,128]{3,2,1,0:T(8,128)(2,1)} %slice.26), channel_id=1, source_target_pairs={{0,8},{8,16},{16,24},{24,32},{32,40},{40,48},{48,56},{64,72},{72,8... | collective-permute-start | bytes 1769480 | tf_op jit(solution)/shard_map/ppermute | solution.py:232
  143.2 27.2 %collective-permute-start.1 = (bf16[8,2,144,128]{3,2,1,0:T(8,128)(2,1)}, bf16[8,2,144,128]{3,2,1,0:T(8,128)(2,1)S(1)}, u32[]{:S(2)}, u32[]{:S(2)}) collective-permute-start(bf16[8,2,144,128]{3,2,1,0:T(8,128)(2,1)} %slice.26), channel_id=1, source_target_pairs={{8,0},{16,8},{24,16},{32,24},{40,32},{48,40},{56,48},{72,64},{80,7... | collective-permute-start | bytes 1769480 | tf_op jit(solution)/shard_map/ppermute | solution.py:232
  146.4 24.0 %collective-permute-start.4 = (bf16[8,2,144,128]{3,2,1,0:T(8,128)(2,1)S(1)}, bf16[8,2,144,128]{3,2,1,0:T(8,128)(2,1)S(1)}, u32[]{:S(2)}, u32[]{:S(2)}) collective-permute-start(bf16[8,2,144,128]{3,2,1,0:T(8,128)(2,1)S(1)} %collective-permute-done.3.refs_4_), channel_id=1, source_target_pairs={{0,129},{1,128},{2,131},{3,130},{4,133},{5,132},{6,135},{7,134},{8... | collective-permute-start | bytes 1769480 | tf_op jit(solution)/shard_map/ppermute | solution.py:266
  170.4 1.0 copy-start.10
  (5 other events, 4.3 us)

commit v12 on v9

--- a/solution.py
+++ b/solution.py
@@ -111,12 +111,15 @@
     slab = blocks * rows
     copies = []
     for h, taken in enumerate(plan):
-        for at, parts in enumerate(taken):
-            for n, (source, part) in enumerate(parts):
+        for n in range(2):
+            for at, parts in enumerate(taken):
+                if n == len(parts):
+                    continue
+                source, part = parts[n]
                 into = q_held.at[h] if at == 0 else held.at[h, n, pl.ds((at - 1) * blocks, blocks)]
                 copy = pltpu.make_async_copy(sources[source].at[:, part], into, sems.at[h, at, n])
                 copy.start()
-                copies.append((h, copy))
+                copies.append(((h, n), copy))
     flat = held.reshape(heads, 2, held.shape[2] * rows, HD)
     q_flat = q_held.reshape(heads, slab, HD)
     o_flat = o_held.reshape(heads, slab, HD)
@@ -148,19 +151,21 @@
         pv = jnp.dot(expo.astype(jnp.bfloat16), v, preferred_element_type=jnp.float32)
         return (part, pv) if total is None else (total + part, mixed + pv)
 
-    def arrive(head):
-        for h, copy in copies:
-            if h == head:
+    def arrive(head, n):
+        for which, copy in copies:
+            if which == (head, n):
                 copy.wait()
 
-    arrive(0)
+    arrive(0, 0)
     most = None
     for j in range(slots):
         most = score(0, j, most)
     outs = []
     for n, (h, t, p) in enumerate(items):
         if n + 1 < len(items) and items[n + 1][0] != h:
-            arrive(h + 1)
+            arrive(h + 1, 0)
+        if t == 0 and p == 0:
+            arrive(h, 1)
         top = jnp.max(most, axis=1, keepdims=True) * SCALE2
         most = total = mixed = None
         for j in range(slots):

time: 192 us -> 192 us (level)
  no operation moved by 1% of the time
where the time goes in v12:
time: 192 us; the launch traced here: 191 us
  waiting for transfers between devices  82.5 us (43%)
  starting transfers between devices  52.5 us (27%)
  Pallas kernels  26.5 us (14%)
  blocking collectives  24 us (12%)
  local copies, waits for them, and re-layouts  4.46 us (2%)
    ppermute x9, waiting for transfers between devices, send(): return lax.ppermute(x, 'seq', pairs)  69 us
    ppermute x9, starting transfers between devices, send(): return lax.ppermute(x, 'seq', pairs)  34.6 us
    all_to_all x1, blocking collectives, exchange(): return lax.all_to_all(x, 'head', split_axis=0, concat_axis=0, tiled=True)  24 us
    pallas_call x2, Pallas kernels, attend(): pl.pallas_call(functools.partial(attend_kernel, tile, per_slab, plan, out...  16.7 us
    all_to_all x3, starting transfers between devices, exchange(): return lax.all_to_all(x, 'head', split_axis=0, concat_axis=0, tiled=True)  16.6 us
    all_to_all x3, waiting for transfers between devices, exchange(): return lax.all_to_all(x, 'head', split_axis=0, concat_axis=0, tiled=True)  12.3 us
    pallas_call x3, Pallas kernels, pack(): pl.pallas_call(functools.partial(pack_kernel, picks, width // (groups * H...  7.72 us
  transfers between devices with their start and end apart: 13, of which 5 were waited for; matrix products, arithmetic and copies ran while one was open for 2% of the time, Pallas kernels for 6%

profile of v12, /device:TPU:2, one launch (start us, length us, event | category | flops | bytes accessed | tf_op | source)
XLA Modules:
  0.0 191.4 jit_solution(8939500385540647392)
XLA Ops:
  0.0 2.3 %pack.4 = bf16[8,3,144,128]{3,2,1,0:T(8,128)(2,1)} custom-call(s32[1]{0:T(128)} %bitcast.swap_ref, bf16[144,3072]{1,0:T(8,128)(2,1)} %refs_0_.5, bf16[144,3072]{1,0:T(8,128)(2,1)} %refs_1_.5), custom_call_target="tpu_custom_call" | custom-call | bytes 1769472 | tf_op jit(solution)/shard_map/pack/pallas_call | solution.py:46
  2.3 6.0 %all-to-all-start.1 = ((bf16[8,3,144,128]{3,2,1,0:T(8,128)(2,1)}), bf16[8,3,144,128]{3,2,1,0:T(8,128)(2,1)S(1)}, u32[]{:S(2)}, u32[]{:S(2)}) async-start(bf16[8,3,144,128]{3,2,1,0:T(8,128)(2,1)} %pack.4), calls=%async_computation.1 | async-start | bytes 1769472 | tf_op jit(solution)/shard_map/all_to_all | solution.py:240
  8.3 3.1 %pack.3 = bf16[8,6,144,128]{3,2,1,0:T(8,128)(2,1)} custom-call(s32[1]{0:T(128)} %bitcast.swap_ref, bf16[144,3072]{1,0:T(8,128)(2,1)} %refs_0_.5, bf16[144,3072]{1,0:T(8,128)(2,1)} %refs_1_.5, bf16[144,3072]{1,0:T(8,128)(2,1)} %refs_2_.1), custom_call_target="tpu_custom_call" | custom-call | bytes 3538944 | tf_op jit(solution)/shard_map/pack/pallas_call | solution.py:46
  11.5 12.3 %all-to-all-done.1.refs_1_ = bf16[8,3,144,128]{3,2,1,0:T(8,128)(2,1)S(1)} async-done(((bf16[8,3,144,128]{3,2,1,0:T(8,128)(2,1)}), bf16[8,3,144,128]{3,2,1,0:T(8,128)(2,1)S(1)}, u32[]{:S(2)}, u32[]{:S(2)}) %all-to-all-start.1) | async-done | bytes 884768 | tf_op jit(solution)/shard_map/all_to_all | solution.py:240
  23.8 3.6 %all-to-all-start = ((bf16[8,6,144,128]{3,2,1,0:T(8,128)(2,1)}), bf16[8,6,144,128]{3,2,1,0:T(8,128)(2,1)S(1)}, u32[]{:S(2)}, u32[]{:S(2)}) async-start(bf16[8,6,144,128]{3,2,1,0:T(8,128)(2,1)} %pack.3), calls=%async_computation | async-start | bytes 3538944 | tf_op jit(solution)/shard_map/all_to_all | solution.py:240
  27.4 2.3 %pack.5 = bf16[8,3,144,128]{3,2,1,0:T(8,128)(2,1)} custom-call(s32[1]{0:T(128)} %bitcast.swap_ref, bf16[144,3072]{1,0:T(8,128)(2,1)} %refs_0_.5, bf16[144,3072]{1,0:T(8,128)(2,1)} %refs_1_.5), custom_call_target="tpu_custom_call" | custom-call | bytes 1769472 | tf_op jit(solution)/shard_map/pack/pallas_call | solution.py:46
  29.7 7.3 %collective-permute-start.2 = (bf16[8,3,144,128]{3,2,1,0:T(8,128)(2,1)}, bf16[8,3,144,128]{3,2,1,0:T(8,128)(2,1)S(1)}, u32[]{:S(2)}, u32[]{:S(2)}) collective-permute-start(bf16[8,3,144,128]{3,2,1,0:T(8,128)(2,1)} %pack.5), channel_id=1, source_target_pairs={{0,64},{8,72},{16,80},{24,88},{32,96},{40,104},{48,112},{56,120},{... | collective-permute-start | bytes 2654216 | tf_op jit(solution)/shard_map/ppermute | solution.py:237
  37.0 36.6 %collective-permute-done.2 = bf16[8,3,144,128]{3,2,1,0:T(8,128)(2,1)S(1)} collective-permute-done((bf16[8,3,144,128]{3,2,1,0:T(8,128)(2,1)}, bf16[8,3,144,128]{3,2,1,0:T(8,128)(2,1)S(1)}, u32[]{:S(2)}, u32[]{:S(2)}) %collective-permute-start.2) | collective-permute-done | bytes 884768 | tf_op jit(solution)/shard_map/ppermute | solution.py:237
  74.5 6.9 %all-to-all-start.2 = ((bf16[8,3,144,128]{3,2,1,0:T(8,128)(2,1)}), bf16[8,3,144,128]{3,2,1,0:T(8,128)(2,1)S(1)}, u32[]{:S(2)}, u32[]{:S(2)}) async-start(bf16[8,3,144,128]{3,2,1,0:T(8,128)(2,1)} %copy-done.5), calls=%async_computation.2 | async-start | bytes 1769472 | tf_op jit(solution)/shard_map/all_to_all | solution.py:240
  82.3 6.5 %collective-permute-start.8 = (bf16[8,2,144,128]{3,2,1,0:T(8,128)(2,1)}, bf16[8,2,144,128]{3,2,1,0:T(8,128)(2,1)}, u32[]{:S(2)}, u32[]{:S(2)}) collective-permute-start(bf16[8,2,144,128]{3,2,1,0:T(8,128)(2,1)} %slice.14), channel_id=1, source_target_pairs={{0,64},{8,72},{16,80},{24,88},{32,96},{40,104},{48,112},{56,120},{... | collective-permute-start | bytes 1769480 | tf_op jit(solution)/shard_map/ppermute | solution.py:237
  89.8 1.3 collective-permute-start.6
  91.0 3.1 %collective-permute-start.5 = (bf16[8,3,144,128]{3,2,1,0:T(8,128)(2,1)}, bf16[8,3,144,128]{3,2,1,0:T(8,128)(2,1)S(1)}, u32[]{:S(2)}, u32[]{:S(2)}) collective-permute-start(bf16[8,3,144,128]{3,2,1,0:T(8,128)(2,1)} %slice.13), channel_id=1, source_target_pairs={{0,8},{8,16},{16,24},{24,32},{32,40},{40,48},{48,56},{64,72},{72,8... | collective-permute-start | bytes 2654216 | tf_op jit(solution)/shard_map/ppermute | solution.py:237
  94.9 1.3 collective-permute-start.7
  96.2 26.3 %collective-permute-done.3.refs_4_ = bf16[8,1,144,128]{3,2,1,0:T(8,128)(2,1)} collective-permute-done((bf16[8,1,144,128]{3,2,1,0:T(8,128)(2,1)}, bf16[8,1,144,128]{3,2,1,0:T(8,128)(2,1)}, u32[]{:S(2)}, u32[]{:S(2)}) %collective-permute-start.3) | collective-permute-done | bytes 294944 | tf_op jit(solution)/shard_map/ppermute | solution.py:237
  122.5 1.3 collective-permute-start.1
  123.8 12.5 %collective-permute-start = (bf16[8,3,144,128]{3,2,1,0:T(8,128)(2,1)S(1)}, bf16[8,3,144,128]{3,2,1,0:T(8,128)(2,1)}, u32[]{:S(2)}, u32[]{:S(2)}) collective-permute-start(bf16[8,3,144,128]{3,2,1,0:T(8,128)(2,1)S(1)} %all-to-all-done.1.refs_1_), channel_id=1, source_target_pairs={{0,8},{8,16},{16,24},{24,32},{32,40},{40,48},{48,56},{64,72},{72,8... | collective-permute-start | bytes 2654216 | tf_op jit(solution)/shard_map/ppermute | solution.py:237
  136.3 1.3 collective-permute-start.9
  138.2 1.5 collective-permute-start.4
  141.2 6.4 %attend.2.refs_12_ = bf16[8,3,144,128]{3,2,1,0:T(8,128)(2,1)} custom-call(s32[3,5]{1,0:T(4,128)} %fusion.1.idx_ref, s32[3,5]{1,0:T(4,128)} %fusion.4.live_ref, bf16[8,6,144,128]{3,2,1,0:T(8,128)(2,1)} %copy-done, bf16[8,3,144,128]{3,2,1,0:T(8,128)(2,1)} %copy-done.3, bf16[8,3,144,128]{3,2,1,0:T(8,128)(2,1)} %collective-permute-done.6.refs_2_.refs_7_, ...), custom_call_target="tpu_custom_call" | custom-call | flops 1132462080 | bytes 3538944 | tf_op jit(solution)/shard_map/attend/pallas_call | solution.py:195
  147.6 6.1 %collective-permute-done.4.refs_5_ = bf16[8,1,144,128]{3,2,1,0:T(8,128)(2,1)} collective-permute-done((bf16[8,1,144,128]{3,2,1,0:T(8,128)(2,1)}, bf16[8,1,144,128]{3,2,1,0:T(8,128)(2,1)}, u32[]{:S(2)}, u32[]{:S(2)}) %collective-permute-start.4) | collective-permute-done | bytes 294944 | tf_op jit(solution)/shard_map/ppermute | solution.py:237
  153.7 1.2 collective-permute-done.9.refs_10_
  154.9 10.2 %attend.3 = bf16[8,3,144,128]{3,2,1,0:T(8,128)(2,1)} custom-call(s32[3,5]{1,0:T(4,128)} %fusion.1.idx_ref, s32[3,5]{1,0:T(4,128)} %fusion.4.live_ref, bf16[8,6,144,128]{3,2,1,0:T(8,128)(2,1)} %copy-done, bf16[8,3,144,128]{3,2,1,0:T(8,128)(2,1)} %copy-done.1, bf16[8,3,144,128]{3,2,1,0:T(8,128)(2,1)} %collective-permute-done.refs_2_, ...), custom_call_target="tpu_custom_call", output_to_operand_aliasing={{}: (14, {})} | custom-call | flops 2264924160 | bytes 7077888 | tf_op jit(solution)/shard_map/attend/pallas_call | solution.py:195
  165.1 24.0 %all_to_all.20.part = bf16[8,3,144,128]{3,2,1,0:T(8,128)(2,1)} all-to-all(bf16[8,3,144,128]{3,2,1,0:T(8,128)(2,1)} %attend.3), channel_id=1, replica_groups=mesh['seq'=32,'head'=8] {'head'}, dimensions={0} | all-to-all | bytes 1769472 | tf_op jit(solution)/shard_map/all_to_all | solution.py:240
  189.1 2.2 %unpack.1 = bf16[144,3072]{1,0:T(8,128)(2,1)} custom-call(s32[1]{0:T(128)} %bitcast.swap_ref, bf16[8,3,144,128]{3,2,1,0:T(8,128)(2,1)} %all_to_all.20.part), custom_call_target="tpu_custom_call" | custom-call | bytes 1769472 | tf_op jit(solution)/shard_map/unpack/pallas_call | solution.py:85
  (28 shorter events, 5.6 us)
Async XLA Ops:
  2.3 21.5 %all-to-all-start.1 = ((bf16[8,3,144,128]{3,2,1,0:T(8,128)(2,1)}), bf16[8,3,144,128]{3,2,1,0:T(8,128)(2,1)S(1)}, u32[]{:S(2)}, u32[]{:S(2)}) async-start(bf16[8,3,144,128]{3,2,1,0:T(8,128)(2,1)} %pack.4), calls=%async_computation.1 | async-start | bytes 1769472 | tf_op jit(solution)/shard_map/all_to_all | solution.py:240
  23.8 100.0 %copy-start.1 = (bf16[8,3,144,128]{3,2,1,0:T(8,128)(2,1)}, bf16[8,3,144,128]{3,2,1,0:T(8,128)(2,1)S(1)}, u32[]{:S(2)}) copy-start(bf16[8,3,144,128]{3,2,1,0:T(8,128)(2,1)S(1)} %all-to-all-done.1.refs_1_) | copy-start | bytes 2654212
  23.8 50.7 %all-to-all-start = ((bf16[8,6,144,128]{3,2,1,0:T(8,128)(2,1)}), bf16[8,6,144,128]{3,2,1,0:T(8,128)(2,1)S(1)}, u32[]{:S(2)}, u32[]{:S(2)}) async-start(bf16[8,6,144,128]{3,2,1,0:T(8,128)(2,1)} %pack.3), calls=%async_computation | async-start | bytes 3538944 | tf_op jit(solution)/shard_map/all_to_all | solution.py:240
  29.7 43.9 %collective-permute-start.2 = (bf16[8,3,144,128]{3,2,1,0:T(8,128)(2,1)}, bf16[8,3,144,128]{3,2,1,0:T(8,128)(2,1)S(1)}, u32[]{:S(2)}, u32[]{:S(2)}) collective-permute-start(bf16[8,3,144,128]{3,2,1,0:T(8,128)(2,1)} %pack.5), channel_id=1, source_target_pairs={{0,64},{8,72},{16,80},{24,88},{32,96},{40,104},{48,112},{56,120},{... | collective-permute-start | bytes 2654216 | tf_op jit(solution)/shard_map/ppermute | solution.py:237
  73.6 0.9 copy-start.5
  74.5 15.3 %copy-start = (bf16[8,6,144,128]{3,2,1,0:T(8,128)(2,1)}, bf16[8,6,144,128]{3,2,1,0:T(8,128)(2,1)S(1)}, u32[]{:S(2)}) copy-start(bf16[8,6,144,128]{3,2,1,0:T(8,128)(2,1)S(1)} %all-to-all-done.refs_0_) | copy-start | bytes 5308420
  74.5 20.4 %all-to-all-start.2 = ((bf16[8,3,144,128]{3,2,1,0:T(8,128)(2,1)}), bf16[8,3,144,128]{3,2,1,0:T(8,128)(2,1)S(1)}, u32[]{:S(2)}, u32[]{:S(2)}) async-start(bf16[8,3,144,128]{3,2,1,0:T(8,128)(2,1)} %copy-done.5), calls=%async_computation.2 | async-start | bytes 1769472 | tf_op jit(solution)/shard_map/all_to_all | solution.py:240
  81.4 56.1 %copy-start.6 = (s32[3,5]{1,0:T(4,128)S(1)}, s32[3,5]{1,0:T(4,128)}, u32[]{:S(2)}) copy-start(s32[3,5]{1,0:T(4,128)} %param.7) | copy-start | bytes 184
  82.3 41.5 %collective-permute-start.8 = (bf16[8,2,144,128]{3,2,1,0:T(8,128)(2,1)}, bf16[8,2,144,128]{3,2,1,0:T(8,128)(2,1)}, u32[]{:S(2)}, u32[]{:S(2)}) collective-permute-start(bf16[8,2,144,128]{3,2,1,0:T(8,128)(2,1)} %slice.14), channel_id=1, source_target_pairs={{0,64},{8,72},{16,80},{24,88},{32,96},{40,104},{48,112},{56,120},{... | collective-permute-start | bytes 1769480 | tf_op jit(solution)/shard_map/ppermute | solution.py:237
  89.8 46.5 %collective-permute-start.6 = (bf16[8,3,144,128]{3,2,1,0:T(8,128)(2,1)}, bf16[8,3,144,128]{3,2,1,0:T(8,128)(2,1)}, u32[]{:S(2)}, u32[]{:S(2)}) collective-permute-start(bf16[8,3,144,128]{3,2,1,0:T(8,128)(2,1)} %slice.13), channel_id=1, source_target_pairs={{8,0},{16,8},{24,16},{32,24},{40,32},{48,40},{56,48},{72,64},{80,7... | collective-permute-start | bytes 2654216 | tf_op jit(solution)/shard_map/ppermute | solution.py:237
  91.0 47.1 %collective-permute-start.5 = (bf16[8,3,144,128]{3,2,1,0:T(8,128)(2,1)}, bf16[8,3,144,128]{3,2,1,0:T(8,128)(2,1)S(1)}, u32[]{:S(2)}, u32[]{:S(2)}) collective-permute-start(bf16[8,3,144,128]{3,2,1,0:T(8,128)(2,1)} %slice.13), channel_id=1, source_target_pairs={{0,8},{8,16},{16,24},{24,32},{32,40},{40,48},{48,56},{64,72},{72,8... | collective-permute-start | bytes 2654216 | tf_op jit(solution)/shard_map/ppermute | solution.py:237
  94.9 27.6 %collective-permute-start.3 = (bf16[8,1,144,128]{3,2,1,0:T(8,128)(2,1)}, bf16[8,1,144,128]{3,2,1,0:T(8,128)(2,1)}, u32[]{:S(2)}, u32[]{:S(2)}) collective-permute-start(bf16[8,1,144,128]{3,2,1,0:T(8,128)(2,1)} %slice.12), channel_id=1, source_target_pairs={{0,64},{8,72},{16,80},{24,88},{32,96},{40,104},{48,112},{56,120},{... | collective-permute-start | bytes 884744 | tf_op jit(solution)/shard_map/ppermute | solution.py:237
  94.9 45.3 %copy-start.2 = (bf16[8,3,144,128]{3,2,1,0:T(8,128)(2,1)}, bf16[8,3,144,128]{3,2,1,0:T(8,128)(2,1)S(1)}, u32[]{:S(2)}) copy-start(bf16[8,3,144,128]{3,2,1,0:T(8,128)(2,1)S(1)} %all-to-all-done.2.refs_3_.refs_8_) | copy-start | bytes 2654212
  94.9 45.3 %collective-permute-start.7 = (bf16[8,3,144,128]{3,2,1,0:T(8,128)(2,1)S(1)}, bf16[8,3,144,128]{3,2,1,0:T(8,128)(2,1)S(1)}, u32[]{:S(2)}, u32[]{:S(2)}) collective-permute-start(bf16[8,3,144,128]{3,2,1,0:T(8,128)(2,1)S(1)} %all-to-all-done.2.refs_3_.refs_8_), channel_id=1, source_target_pairs={{0,128},{8,136},{16,144},{24,152},{32,160},{40,168},{48,176},{56,1... | collective-permute-start | bytes 2654216 | tf_op jit(solution)/shard_map/ppermute | solution.py:237
  122.5 31.3 %collective-permute-start.1 = (bf16[8,3,144,128]{3,2,1,0:T(8,128)(2,1)S(1)}, bf16[8,3,144,128]{3,2,1,0:T(8,128)(2,1)}, u32[]{:S(2)}, u32[]{:S(2)}) collective-permute-start(bf16[8,3,144,128]{3,2,1,0:T(8,128)(2,1)S(1)} %all-to-all-done.1.refs_1_), channel_id=1, source_target_pairs={{8,0},{16,8},{24,16},{32,24},{40,32},{48,40},{56,48},{72,64},{80,7... | collective-permute-start | bytes 2654216 | tf_op jit(solution)/shard_map/ppermute | solution.py:237
  123.8 30.0 %collective-permute-start = (bf16[8,3,144,128]{3,2,1,0:T(8,128)(2,1)S(1)}, bf16[8,3,144,128]{3,2,1,0:T(8,128)(2,1)}, u32[]{:S(2)}, u32[]{:S(2)}) collective-permute-start(bf16[8,3,144,128]{3,2,1,0:T(8,128)(2,1)S(1)} %all-to-all-done.1.refs_1_), channel_id=1, source_target_pairs={{0,8},{8,16},{16,24},{24,32},{32,40},{40,48},{48,56},{64,72},{72,8... | collective-permute-start | bytes 2654216 | tf_op jit(solution)/shard_map/ppermute | solution.py:237
  136.3 18.7 %collective-permute-start.9 = (bf16[8,2,144,128]{3,2,1,0:T(8,128)(2,1)}, bf16[8,2,144,128]{3,2,1,0:T(8,128)(2,1)}, u32[]{:S(2)}, u32[]{:S(2)}) collective-permute-start(bf16[8,2,144,128]{3,2,1,0:T(8,128)(2,1)} %collective-permute-done.8.refs_11_), channel_id=1, source_target_pairs={{0,129},{1,128},{2,131},{3,130},{4,133},{5,132},{6,135},{7,134},{8... | collective-permute-start | bytes 1769480 | tf_op jit(solution)/shard_map/ppermute | solution.py:271
  138.2 2.0 %copy-start.3 = (bf16[8,3,144,128]{3,2,1,0:T(8,128)(2,1)}, bf16[8,3,144,128]{3,2,1,0:T(8,128)(2,1)S(1)}, u32[]{:S(2)}) copy-start(bf16[8,3,144,128]{3,2,1,0:T(8,128)(2,1)S(1)} %collective-permute-done.5.refs_1_.refs_6_) | copy-start | bytes 2654212
  138.2 15.6 %collective-permute-start.4 = (bf16[8,1,144,128]{3,2,1,0:T(8,128)(2,1)}, bf16[8,1,144,128]{3,2,1,0:T(8,128)(2,1)}, u32[]{:S(2)}, u32[]{:S(2)}) collective-permute-start(bf16[8,1,144,128]{3,2,1,0:T(8,128)(2,1)} %collective-permute-done.3.refs_4_), channel_id=1, source_target_pairs={{0,128},{8,136},{16,144},{24,152},{32,160},{40,168},{48,176},{56,1... | collective-permute-start | bytes 884744 | tf_op jit(solution)/shard_map/ppermute | solution.py:237
  140.2 0.9 copy-start.4
